TPU v7x, 256 devices: a whole 4x4x8 slice. The times are simulated.
256 devices in a mesh: ang: 32 (over y_hi, z, core), row: 8 (over x, y_lo).
Axes of the slice: x: 4, y: 4 (y_hi: 2, y_lo: 2; y = y_hi * 2 + y_lo), z: 8, core: 2. Of those that a mesh axis runs over, the one named last changes fastest.
Arguments:
- echoes: bfloat16 [1024, 2, 16384], P('ang', None, 'row'), may hold values from -6 to 6
- pulse_ids: int32 [64, 512], replicated, may hold values from 0 to 1023, as said below
- bin_start: int32 [64, 512], replicated, may hold values from 0 to 16256
- live_count: int32 [64, 32], replicated, may hold values from 1 to 16
- wavenum: int32 [1024], replicated, may hold values from 1 to 32767
- interp: bfloat16 [64, 128, 128], P('row'), may hold values from -0.5 to 0.5
Outputs:
- image: bfloat16 [32768, 2, 8192], P('ang', None, 'row')
Inputs may be any that keep to these rules, and one draw needn't show every extreme that they name: `pulse_ids`: entries 16 * a to 16 * a + 15 of each tile name distinct pulses of aperture block a, numbered a * 32 to a * 32 + 31.
All inputs are finite; a program needn't handle non-finite values.
Results may differ from a plain program's by a relative error of at most 0.0055.
Values may be sent and summed in bfloat16 or wider, within the bound.
No kernel may reach another device: no remote copies, remote signals or barrier semaphores. Data moves between devices by JAX's collectives and lax.ppermute only.
A program may use at most 320 MiB of HBM per device.

v0:
```python
import math

import jax
import jax.numpy as jnp
from jax import lax
from jax.sharding import Mesh
from jax.sharding import PartitionSpec as P

COLS = 32768
ROW = ("row_0", "row_1")


def gather_axes(shard, axes, dim):
    whole = shard
    for number in range(len(axes) - 1, -1, -1):
        whole = lax.all_gather(whole, axes[number], axis=dim, tiled=True)
    return whole


def body(echoes, pulse_ids, bin_start, live_count, wavenum, interp):
    blocks = lax.axis_size("ang")
    ang_index = lax.axis_index("ang")
    row_index = lax.axis_index(ROW)
    tiles_mine = interp.shape[0]
    tile_rows = interp.shape[1]
    window = interp.shape[2]
    block_pulses = echoes.shape[0]
    foot_len = pulse_ids.shape[1]
    per_block = foot_len // blocks
    col_dev = COLS // blocks
    first_tile = row_index * tiles_mine
    first_entry = ang_index * per_block
    zero_index = jnp.zeros((), jnp.int32)
    my_ids = (
        lax.dynamic_slice(pulse_ids, (first_tile, first_entry), (tiles_mine, per_block))
        - ang_index * block_pulses
    )
    my_starts = lax.dynamic_slice(bin_start, (first_tile, first_entry), (tiles_mine, per_block))
    my_live = lax.dynamic_slice(live_count, (first_tile, ang_index), (tiles_mine, 1))
    kept_mask = jnp.arange(per_block, dtype=jnp.int32)[None, :] < my_live
    full_bins = gather_axes(echoes, ROW, 2)

    def cut_panel(pulse, anchor):
        return lax.dynamic_slice(full_bins, (pulse, zero_index, anchor), (1, 2, window))[0]

    panels = jax.vmap(jax.vmap(cut_panel, out_axes=1))(my_ids, my_starts)
    panels = jnp.where(kept_mask[:, None, :, None], panels, jnp.zeros_like(panels))
    carried = jnp.einsum(
        "tib,tckb->tcki", interp, panels, preferred_element_type=jnp.float32
    ).astype(jnp.bfloat16)
    tile_ids = lax.dynamic_slice_in_dim(pulse_ids, first_tile, tiles_mine, 0)
    columns = ang_index * col_dev + jnp.arange(col_dev, dtype=jnp.int32)
    step_angle = 2.0 * math.pi / COLS
    norm_scale = foot_len ** (-0.5)

    def tile_terms(focus_tile, ids_tile):
        rates = wavenum[ids_tile]
        phase_angle = (rates[:, None] * columns[None, :] % COLS).astype(jnp.float32) * step_angle
        left = jnp.concatenate(
            [jnp.cos(phase_angle).astype(jnp.bfloat16), jnp.sin(phase_angle).astype(jnp.bfloat16)],
            0,
        )
        focus_real = focus_tile[0]
        focus_imag = focus_tile[1]
        upper = jnp.concatenate([focus_real, focus_imag], 1)
        lower = jnp.concatenate([-focus_imag, focus_real], 1)
        right = jnp.concatenate([upper, lower], 0)
        return lax.dot_general(
            left, right, (((0,), (0,)), ((), ())), preferred_element_type=jnp.float32
        )

    gathered = lax.all_gather(carried, "ang", axis=2, tiled=True)
    summed = tuple((tile_terms(gathered[tile], tile_ids[tile]) for tile in range(tiles_mine)))
    pieces = [
        (total * norm_scale).astype(jnp.bfloat16).reshape(col_dev, 2, tile_rows) for total in summed
    ]
    return jnp.concatenate(pieces, 2)


def solution(mesh):
    finer = Mesh(mesh.devices.reshape(mesh.shape["ang"], 4, 2), ("ang", "row_0", "row_1"))
    return jax.shard_map(
        body,
        mesh=finer,
        in_specs=(P("ang", None, ROW), P(), P(), P(), P(), P(ROW, None, None)),
        out_specs=P("ang", None, ROW),
        check_vma=False,
    )
```

profile of v0, /device:TPU:1, one launch (start us, length us, event | category | flops | bytes accessed | tf_op | source)
XLA Modules:
  0.0 326.5 jit_solution(14141377698474495977)
XLA Ops:
  7.6 7.6 %all_gather.9 = bf16[32,2,4096]{2,0,1:T(8,128)(2,1)} all-gather(bf16[32,2,2048]{2,0,1:T(8,128)(2,1)S(1)} %copy.27), channel_id=1, replica_groups=mesh['ang'=32,'row_0'=4,'row_1'=2] {'row_1'}, dimensions={2}, use_global_device_ids=true | all-gather | bytes 786432 | tf_op jit(solution)/shard_map/all_gather | solution.py:16
  17.0 36.8 %all-gather.3.cloned.1.call-done = bf16[32,2,16384]{2,0,1:T(8,128)(2,1)} async-done(((bf16[32,2,4096]{2,0,1:T(8,128)(2,1)}), bf16[32,2,16384]{2,0,1:T(8,128)(2,1)}) %all-gather.3.cloned.1.call-update) | async-done | bytes 2097168 | tf_op jit(solution)/shard_map/all_gather | solution.py:16
  53.8 103.4 %copy.28 = bf16[32,2,16384]{1,0,2:T(8,128)(2,1)} copy(bf16[32,2,16384]{2,0,1:T(8,128)(2,1)} %all-gather.3.cloned.1.call-done) | data formatting | bytes 4194304 | tf_op jit(solution)/shard_map/all_gather | solution.py:16
  157.2 17.4 %gather_fusion.1 = bf16[128,2,128]{1,0,2:T(8,128)(2,1)} fusion(bf16[32,2,16384]{1,0,2:T(8,128)(2,1)} %copy.28, s32[128]{0:T(128)S(1)} %reshape.330), kind=kCustom, calls=%fused_computation.1 | custom fusion | bytes 132608 | tf_op jit(solution)/shard_map/vmap(vmap())/gather | solution.py:44
  174.6 6.2 %copy.29 = bf16[8,16,2,128]{3,1,2,0:T(8,128)(2,1)S(1)} copy(bf16[8,16,2,128]{2,1,0,3:T(8,128)(2,1)} %bitcast.107) | data formatting | bytes 131072 | tf_op jit(solution)/shard_map/vmap(vmap())/squeeze | solution.py:44
  182.8 2.3 gather_fusion.8
  185.1 2.3 gather_fusion.7
  187.4 2.3 gather_fusion.6
  189.7 2.3 gather_fusion.5
  192.0 2.3 gather_fusion.4
  194.3 2.3 gather_fusion.3
  196.6 2.3 gather_fusion.2
  198.9 2.3 gather_fusion
  201.2 70.2 %cosine_convert_fusion = (bf16[512,1024]{1,0:T(8,128)(2,1)}, bf16[512,1024]{1,0:T(8,128)(2,1)}, bf16[512,1024]{1,0:T(8,128)(2,1)}, bf16[512,1024]{1,0:T(8,128)(2...) fusion(s32[1024]{0:T(1024)S(1)} %iota_add_fusion, ...), kind=kLoop, calls=%fused_computation.106 | loop fusion | flops 67108864 | bytes 16797696 | tf_op jit(solution)/shard_map/convert_element_type | solution.py:60
  271.5 2.4 fusion.186
  275.2 2.8 fusion.80
  278.0 1.3 copy.30
  279.3 3.2 fusion.83
  282.5 1.3 copy.31
  283.9 2.9 fusion.86
  286.8 1.3 copy.32
  288.1 3.2 fusion.89
  291.3 1.3 copy.33
  292.6 2.9 fusion.92
  295.5 1.3 copy.34
  296.8 3.2 fusion.95
  300.0 1.3 copy.35
  301.3 3.2 fusion.98
  304.6 2.0 copy.36
  306.5 3.2 fusion.101
  309.7 2.0 copy.37
  316.5 2.0 copy-done.5
  (37 shorter events, 12.0 us)
Async XLA Ops:
  6.5 174.3 %copy-start = (bf16[8,128,128]{2,1,0:T(8,128)(2,1)S(1)}, bf16[8,128,128]{2,1,0:T(8,128)(2,1)}, u32[]{:S(2)}) copy-start(bf16[8,128,128]{2,1,0:T(8,128)(2,1)} %param.11) | copy-start | bytes 786436
  6.5 47.3 %all-gather.3.cloned.1.call-start = ((), (), s32[]{:S(2)}) async-start(), calls=%async_computation | async-start | bytes 2621440 | tf_op jit(solution)/shard_map/all_gather | solution.py:16
  15.3 256.2 %all-gather.5.cloned.1.call-start = ((), (), s32[]{:S(2)}) async-start(), calls=%async_computation.1 | async-start | bytes 2162688 | tf_op jit(solution)/shard_map/all_gather | solution.py:72
  174.6 8.2 %copy-start.1 = (s32[1024]{0:T(1024)S(1)}, s32[1024]{0:T(1024)}, u32[]{:S(2)}) copy-start(s32[1024]{0:T(1024)} %param.10) | copy-start | bytes 12292
  271.5 2.4 copy-start.2
  312.8 2.9 copy-start.3
  313.6 5.0 %copy-start.4 = (bf16[1024,2,128]{2,1,0:T(2,128)(2,1)S(1)}, bf16[1024,2,128]{2,1,0:T(2,128)(2,1)}, u32[]{:S(2)}) copy-start(bf16[1024,2,128]{2,1,0:T(2,128)(2,1)} %copy.37) | copy-start | bytes 1572868
  316.5 2.0 copy-start.5
Sparse Core Ops, SparseCore 0:
  15.4 38.3 all-gather.2
  181.9 77.7 all-gather.4
where the time goes:
time: 328 us; the launch traced here: 327 us
  local copies, waits for them, and re-layouts  168 us (51%)
  other arithmetic  74.6 us (23%)
  waiting for transfers between devices  36.8 us (11%)
  matrix products  25.5 us (8%)
  between operations  13.7 us (4%)
  blocking collectives  7.61 us (2%)
    all_gather x1, local copies, waits for them, and re-layouts, gather_axes(): whole = lax.all_gather(whole, axes[number], axis=dim, tiled=True)  103 us
    convert_element_type x1, other arithmetic, tile_terms(): jnp.cos(phase_angle).astype(jnp.bfloat16)  70.2 us
    all_gather x1, waiting for transfers between devices, gather_axes(): whole = lax.all_gather(whole, axes[number], axis=dim, tiled=True)  36.8 us
    dot_general x8, matrix products, tile_terms(): lax.dot_general(left, right, (((0,), (0,)), ((), ())), preferred_element_...  24.6 us
    gather x8, local copies, waits for them, and re-layouts, tile_terms(): rates = wavenum[ids_tile]  18.3 us
    gather x1, local copies, waits for them, and re-layouts, cut_panel(): lax.dynamic_slice(full_bins, (pulse, zero_index, anchor), (1, 2, window))[0]  17.4 us
    reshape x8, local copies, waits for them, and re-layouts, body(): (total * norm_scale).astype(jnp.bfloat16).reshape(col_dev, 2, tile_rows)  11.8 us
    unnamed x20, local copies, waits for them, and re-layouts  7.79 us
  transfers between devices with their start and end apart: 2, of which 1 were waited for; matrix products, arithmetic and copies ran while one was open for 28% of the time, Pallas kernels for 0%

commit v1 on v0

v1 whole, which is shorter than its diff:
```python
import functools
import math

import jax
import jax.numpy as jnp
from jax import lax
from jax.experimental import pallas as pl
from jax.experimental.pallas import tpu as pltpu
from jax.sharding import Mesh
from jax.sharding import PartitionSpec as P

COLS = 32768
LANES = 128
ANG = ("yh", "z", "core")
ROW = ("x", "yl")
FINE = ("yh", "z", "core", "x", "yl")
GROUP = 8


def pack_kernel(low_ref, high_ref, bins_ref, offs_ref, out_ref, low_sc, high_sc, *, bins):
    windows = low_ref.shape[0]

    def take(step, _):
        for u in range(16):
            w = step * 16 + u
            lo = pl.multiple_of(low_ref[w], 2)
            hi = pl.multiple_of(high_ref[w], 2)
            at = pl.multiple_of(w * 2, 2)
            low_sc[pl.ds(at, 2), :] = bins_ref[pl.ds(lo, 2), :]
            high_sc[pl.ds(at, 2), :] = bins_ref[pl.ds(hi, 2), :]
        return 0

    lax.fori_loop(0, windows // 16, take, 0)
    lane = lax.broadcasted_iota(jnp.int32, (16, LANES), 1)

    def shift(step, _):
        for u in range(4):
            rows = pl.ds(pl.multiple_of((step * 4 + u) * 16, 16), 16)
            offs = offs_ref[rows, :]
            low = low_sc[rows, :]
            high = high_sc[rows, :]
            for bit in range(7):
                by = 1 << bit
                on = (offs & by) != 0
                low = jnp.where(on, pltpu.roll(low, LANES - by, 1), low)
                high = jnp.where(on, pltpu.roll(high, LANES - by, 1), high)
            here = offs + lane
            cut = jnp.where((offs & (LANES - 1)) + lane < LANES, low, high)
            cut = jnp.where((here >= 0) & (here < bins), cut, 0.0)
            out_ref[rows, :] = cut.astype(jnp.bfloat16)
        return 0

    lax.fori_loop(0, windows * 2 // 64, shift, 0)


def pack(echoes, ids, starts, live):
    pulses, parts, bins = echoes.shape
    panels = bins // LANES
    row_index = lax.axis_index(ROW)
    tiles, per_block = ids.shape
    windows = tiles * per_block
    rows = (
        echoes.astype(jnp.float32)
        .reshape(pulses, parts, panels, LANES)
        .transpose(0, 2, 1, 3)
        .reshape(pulses * panels * parts, LANES)
    )
    offs = starts - row_index * bins
    used = jnp.arange(per_block, dtype=jnp.int32)[None, :] < live[:, None]
    offs = jnp.where(used, offs, -2 * COLS).reshape(windows)
    panel = offs >> 7
    base = ids.reshape(windows) * (panels * parts)
    low = base + jnp.clip(panel, 0, panels - 1) * parts
    high = base + jnp.clip(panel + 1, 0, panels - 1) * parts
    spread = jnp.broadcast_to(offs[:, None, None], (windows, parts, LANES)).reshape(
        windows * parts, LANES
    )
    smem = pl.BlockSpec(memory_space=pltpu.SMEM)
    vmem = pl.BlockSpec(memory_space=pltpu.VMEM)
    return pl.pallas_call(
        functools.partial(pack_kernel, bins=bins),
        out_shape=jax.ShapeDtypeStruct((windows * parts, LANES), jnp.bfloat16),
        in_specs=[smem, smem, vmem, vmem],
        out_specs=vmem,
        scratch_shapes=[pltpu.VMEM((windows * parts, LANES), jnp.float32)] * 2,
        compiler_params=pltpu.CompilerParams(vmem_limit_bytes=24 << 20),
        name="pack",
    )(low, high, rows, spread)


def focus_kernel(got_ref, interp_ref, out_ref):
    tiles = interp_ref.shape[0]
    rows = out_ref.shape[0] // tiles
    panels = got_ref[0].astype(jnp.float32)
    for source in range(1, got_ref.shape[0]):
        panels += got_ref[source].astype(jnp.float32)
    panels = panels.astype(jnp.bfloat16)
    for tile in range(tiles):
        out_ref[tile * rows : (tile + 1) * rows, :] = lax.dot_general(
            panels[tile * rows : (tile + 1) * rows, :],
            interp_ref[tile],
            (((1,), (1,)), ((), ())),
            preferred_element_type=jnp.float32,
        ).astype(jnp.bfloat16)


def focus(got, interp):
    return pl.pallas_call(
        focus_kernel,
        out_shape=jax.ShapeDtypeStruct(got.shape[1:], jnp.bfloat16),
        in_specs=[pl.BlockSpec(memory_space=pltpu.VMEM)] * 2,
        out_specs=pl.BlockSpec(memory_space=pltpu.VMEM),
        name="focus",
    )(got, interp)


def image_kernel(*refs, tiles, scale):
    code_ref, cos_ref, sin_ref = refs[:3]
    blocks = refs[3:-2]
    out_ref, spread = refs[-2:]
    pulses = cos_ref.shape[1]
    half = spread.shape[0] // 2

    @pl.when(pl.program_id(0) == 0)
    def _():
        both = blocks[0].shape[0] // (blocks[0].shape[1] * 2)
        entry_rows = 32
        per = GROUP // 2
        slots = GROUP * 32
        row = lax.broadcasted_iota(jnp.int32, (2 * slots, GROUP * entry_rows), 0)
        for group in range(len(blocks) // per):
            for tile in range(tiles):
                parts = []
                for ref in blocks[group * per : (group + 1) * per]:
                    for side in range(2):
                        first = side * tiles * entry_rows + tile * entry_rows
                        parts.append(ref[first : first + entry_rows, :])
                stacked = jnp.concatenate(parts, 0)
                hot = row == code_ref[tile, group, :, :]
                hot = jnp.where(hot, 1.0, 0.0).astype(jnp.bfloat16)
                placed = jnp.dot(hot, stacked, preferred_element_type=jnp.float32).astype(jnp.bfloat16)
                columns = slice(tile * LANES, (tile + 1) * LANES)
                spread[group * slots : (group + 1) * slots, columns] = placed[:slots]
                spread[half + group * slots : half + (group + 1) * slots, columns] = placed[slots:]

    total = jnp.dot(cos_ref[...], spread[:half, :], preferred_element_type=jnp.float32)
    total += jnp.dot(sin_ref[...], spread[half:, :], preferred_element_type=jnp.float32)
    out_ref[...] = (total * scale).astype(jnp.bfloat16).reshape(out_ref.shape)


def image(code, cos, sin, blocks, tiles, scale):
    rows, pulses = cos.shape
    step = 256
    whole = pl.BlockSpec(memory_space=pltpu.VMEM)
    return pl.pallas_call(
        functools.partial(image_kernel, tiles=tiles, scale=scale),
        out_shape=jax.ShapeDtypeStruct((rows // 2, 2, tiles * LANES), jnp.bfloat16),
        grid=(rows // step,),
        in_specs=[whole]
        + [pl.BlockSpec((step, pulses), lambda i: (i, 0))] * 2
        + [whole] * len(blocks),
        out_specs=pl.BlockSpec((step // 2, 2, tiles * LANES), lambda i: (i, 0, 0)),
        scratch_shapes=[pltpu.VMEM((2 * pulses, tiles * LANES), jnp.bfloat16)],
        compiler_params=pltpu.CompilerParams(vmem_limit_bytes=40 << 20),
        name="image",
    )(code, cos, sin, *blocks)


def pick(table, index):
    hot = index[:, None] == jnp.arange(table.shape[0], dtype=jnp.int32)[None, :]
    wide = hot.reshape(hot.shape + (1,) * (table.ndim - 1))
    return jnp.sum(jnp.where(wide, table[None], 0), axis=1)


def twiddles(rates, first_column, columns):
    step_angle = 2.0 * math.pi / COLS
    fine = 32
    coarse_k = first_column + fine * jnp.arange(columns // fine, dtype=jnp.int32)
    coarse = ((rates[None, :] * coarse_k[:, None]) % COLS).astype(jnp.float32) * step_angle
    row = jnp.arange(2 * fine, dtype=jnp.int32)
    turn = rates[None, :] * (row // 2)[:, None] + (COLS - (COLS // 4) * (row % 2))[:, None]
    within = (turn % COLS).astype(jnp.float32) * step_angle
    coarse_c, coarse_s, fine_c, fine_s = lax.optimization_barrier(
        (jnp.cos(coarse), jnp.sin(coarse), jnp.cos(within), jnp.sin(within))
    )
    coarse_c, coarse_s = coarse_c[:, None, :], coarse_s[:, None, :]
    fine_c, fine_s = fine_c[None], fine_s[None]
    shape = (2 * columns, rates.shape[0])
    cos = (coarse_c * fine_c - coarse_s * fine_s).astype(jnp.bfloat16).reshape(shape)
    sin = (-coarse_s * fine_c - coarse_c * fine_s).astype(jnp.bfloat16).reshape(shape)
    return cos, sin


def body(echoes, pulse_ids, bin_start, live_count, wavenum, interp):
    blocks = lax.axis_size(ANG)
    ang_index = lax.axis_index(ANG)
    row_index = lax.axis_index(ROW)
    n_rows = lax.axis_size(ROW)
    ring = lax.axis_size("z")
    tiles_mine = interp.shape[0]
    block_pulses = echoes.shape[0]
    foot_len = pulse_ids.shape[1]
    per_block = foot_len // blocks
    col_dev = COLS // blocks
    first_entry = ang_index * per_block
    local_ids = pulse_ids % block_pulses

    my_ids = lax.dynamic_slice_in_dim(local_ids, first_entry, per_block, 1)
    my_starts = lax.dynamic_slice_in_dim(bin_start, first_entry, per_block, 1)
    my_live = lax.dynamic_slice_in_dim(live_count, ang_index, 1, 1)[:, 0]
    packed = pack(echoes, my_ids, my_starts, my_live)
    rows = packed.shape[0] // n_rows
    got = lax.all_to_all(packed.reshape(n_rows, rows, LANES), ROW, 0, 0, tiled=True)
    mine = focus(got, interp)

    swap = [(0, 1), (1, 0)]
    ahead = [(i, (i + 1) % ring) for i in range(ring)]
    behind = [(i, (i - 1) % ring) for i in range(ring)]
    other = lax.ppermute(mine, "yh", swap)
    block = jnp.concatenate([mine, other], 0)
    held = [block]
    shifts = [0]
    forward = backward = block
    for step in range(1, ring // 2 + 1):
        forward = lax.ppermute(forward, "z", ahead)
        held.append(forward)
        shifts.append(-step)
        if step < ring - step:
            backward = lax.ppermute(backward, "z", behind)
            held.append(backward)
            shifts.append(step)
    sibling = [lax.ppermute(b, "core", swap) for b in held]
    arrays, zs, cores = [], [], []
    for near, far, shift in zip(held, sibling, shifts):
        arrays += [near, far]
        zs += [shift, shift]
        cores += [0, 1]
    yh, z, core = (lax.axis_index(name) for name in ANG)
    at_z = (z + jnp.repeat(jnp.array(zs, jnp.int32), 2)) % ring
    at_core = core ^ jnp.repeat(jnp.array(cores, jnp.int32), 2)
    at_yh = yh ^ jnp.tile(jnp.array([0, 1], jnp.int32), len(arrays))
    order = (at_yh * ring + at_z) * 2 + at_core

    tile_ids = lax.dynamic_slice_in_dim(local_ids, row_index * tiles_mine, tiles_mine, 0)
    by_block = tile_ids.reshape(tiles_mine, blocks, per_block).transpose(1, 0, 2)
    placed = pick(by_block, order).transpose(1, 0, 2)
    placed = placed + block_pulses * (jnp.arange(blocks, dtype=jnp.int32) % GROUP)[None, :, None]
    code = placed[..., None] + GROUP * block_pulses * jnp.arange(2, dtype=jnp.int32)
    code = code.reshape(tiles_mine, blocks // GROUP, 1, GROUP * per_block * 2)
    rates = pick(wavenum.reshape(blocks, block_pulses), order).reshape(-1)
    cos, sin = twiddles(rates, ang_index * col_dev, col_dev)
    return image(code, cos, sin, arrays, tiles_mine, foot_len ** (-0.5))


def solution(mesh):
    finer = Mesh(mesh.devices.reshape(2, -1, 2, 4, 2), FINE)
    return jax.shard_map(
        body,
        mesh=finer,
        in_specs=(P(ANG, None, ROW), P(), P(), P(), P(), P(ROW, None, None)),
        out_specs=P(ANG, None, ROW),
        check_vma=False,
    )
```

time: 328 us -> 101 us (0.31)
  local copies, waits for them, and re-layouts: 168 us -> 7.62 us
  other arithmetic: 74.6 us -> 15.8 us
  Pallas kernels: 0 us -> 34.7 us
  starting transfers between devices: 0.04 us -> 27.9 us
  matrix products: 25.5 us -> 0 us
  waiting for transfers between devices: 36.8 us -> 14.6 us
  between operations: 13.7 us -> 0.29 us
  blocking collectives: 7.61 us -> 0 us
    all_gather x1 -> x0, local copies, waits for them, and re-layouts: 103 us -> none  [gather_axes(): whole = lax.all_gather(whole, axes[number], axis=dim, tiled=True)]
    convert_element_type x1, other arithmetic: 70.2 us -> 5.28 us  [twiddles(): (-coarse_s * fine_c - coarse_c * fine_s).astype(jnp.bfloat16).reshape(shape)]
    all_gather x2 -> x0, waiting for transfers between devices: 36.8 us -> none  [the longest x1 36.8 us: gather_axes(): whole = lax.all_gather(whole, axes[number], axis=dim, tiled=True)]
    gather x9 -> x0, local copies, waits for them, and re-layouts: 35.7 us -> none  [the longest x8 18.3 us: tile_terms(): rates = wavenum[ids_tile]]
    pallas_call x0 -> x3, Pallas kernels: none -> 34.7 us  [the longest x1 19.2 us: pack(): pl.pallas_call(functools.partial(pack_kernel, bins=bins), out_shape=jax.S...]
    dot_general x9 -> x0, matrix products: 25.5 us -> none  [the longest x8 24.6 us: tile_terms(): lax.dot_general(left, right, (((0,), (0,)), ((), ())), preferred_element_...]
    ppermute x0 -> x16, starting transfers between devices: none -> 22 us  [the longest x3 9.75 us: body(): backward = lax.ppermute(backward, 'z', behind)]
    reshape x8 -> x2, local copies, waits for them, and re-layouts: 11.8 us -> 0.17 us  [the longest x1 0.09 us: body(): tile_ids.reshape(tiles_mine, blocks, per_block).transpose(1, 0, 2)]
  transfers between devices with their start and end apart: 2 -> 17, of which waited for: 1 -> 6; matrix products, arithmetic and copies ran while one was open for 28% -> 13% of each run, Pallas kernels for 0% -> 0%
where the time goes in v1:
time: 101 us
  Pallas kernels  34.7 us (34%)
  starting transfers between devices  27.9 us (28%)
  other arithmetic  15.8 us (16%)
  waiting for transfers between devices  14.6 us (14%)
  local copies, waits for them, and re-layouts  7.62 us (8%)
    pallas_call x1, Pallas kernels, pack(): pl.pallas_call(functools.partial(pack_kernel, bins=bins), out_shape=jax.S...  19.2 us
    pallas_call x1, Pallas kernels, image(): pl.pallas_call(functools.partial(image_kernel, tiles=tiles, scale=scale),...  13.4 us
    ppermute x3, starting transfers between devices, body(): backward = lax.ppermute(backward, 'z', behind)  9.75 us
    ppermute x8, starting transfers between devices, body(): sibling = [lax.ppermute(b, 'core', swap) for b in held]  7.93 us
    all_to_all x1, waiting for transfers between devices, body(): lax.all_to_all(packed.reshape(n_rows, rows, LANES), ROW, 0, 0, tiled=True)  6.62 us
    all_to_all x1, starting transfers between devices, body(): lax.all_to_all(packed.reshape(n_rows, rows, LANES), ROW, 0, 0, tiled=True)  5.86 us
    convert_element_type x1, other arithmetic, twiddles(): (-coarse_s * fine_c - coarse_c * fine_s).astype(jnp.bfloat16).reshape(shape)  5.28 us
    unnamed x14, local copies, waits for them, and re-layouts  5.18 us
  transfers between devices with their start and end apart: 17, of which 6 were waited for; matrix products, arithmetic and copies ran while one was open for 13% of the time, Pallas kernels for 0%

profile of v1, /device:TPU:1, one launch (start us, length us, event | category | flops | bytes accessed | tf_op | source)
XLA Modules:
  0.0 100.8 jit_solution(9306164727845123741)
XLA Ops:
  0.0 1.0 add_select_fusion.2
  1.1 0.9 subtract_select_fusion
  2.6 1.2 %bitcast_convert_fusion = f32[32,2,16,128]{3,1,2,0:T(2,128)S(1)} fusion(bf16[32,2,2048]{2,1,0:T(2,128)(2,1)} %param.9), kind=kLoop, calls=%fused_computation.10 | loop fusion | flops 131072 | bytes 786432 | tf_op jit(solution)/shard_map/reshape | solution.py:66
  4.1 19.2 %pack.1 = bf16[2048,128]{1,0:T(8,128)(2,1)} custom-call(s32[1024]{0:T(1024)S(1)} %get-tuple-element.16.low_ref, s32[1024]{0:T(1024)S(1)} %get-tuple-element.15.high_ref, f32[1024,128]{1,0:T(8,128)S(1)} %bitcast.17, s32[2048,128]{1,0:T(8,128)S(1)} %broadcast_in_dim.89.offs_ref), custom_call_target="tpu_custom_call" | custom-call | tf_op jit(solution)/shard_map/pack/pallas_call | solution.py:80
  23.4 5.9 %all-to-all-start = ((bf16[8,256,128]{2,1,0:T(8,128)(2,1)}), bf16[8,256,128]{2,1,0:T(8,128)(2,1)S(1)}, u32[]{:S(2)}, u32[]{:S(2)}) async-start(bf16[8,256,128]{2,1,0:T(8,128)(2,1)} %bitcast.9), calls=%async_computation | async-start | bytes 1048576 | tf_op jit(solution)/shard_map/all_to_all | solution.py:213
  30.2 1.1 %fusion.3 = (f32[64,1024]{1,0:T(8,128)S(1)}, f32[64,1024]{1,0:T(8,128)S(1)}) fusion(s32[64]{0:T(128)S(1)} %get-tuple-element.22, s32[64]{0:T(128)S(1)} %get-tuple-element.21, s32[1024]{0:T(1024)S(1)} %mul.204), kind=kLoop, calls=%fused_computation.19 | loop fusion | flops 983040 | bytes 528896 | tf_op jit(solution)/shard_map/sin | solution.py:184
  31.3 6.6 %all-to-all-done.got_ref = bf16[8,256,128]{2,1,0:T(8,128)(2,1)S(1)} async-done(((bf16[8,256,128]{2,1,0:T(8,128)(2,1)}), bf16[8,256,128]{2,1,0:T(8,128)(2,1)S(1)}, u32[]{:S(2)}, u32[]{:S(2)}) %all-to-all-start) | async-done | bytes 524320 | tf_op jit(solution)/shard_map/all_to_all | solution.py:213
  37.9 0.8 copy-done.3
  38.7 2.0 %focus.1 = bf16[256,128]{1,0:T(8,128)(2,1)} custom-call(bf16[8,256,128]{2,1,0:T(8,128)(2,1)} %copy-done.3, bf16[8,128,128]{2,1,0:T(8,128)(2,1)} %interp_ref.1), custom_call_target="tpu_custom_call" | custom-call | tf_op jit(solution)/shard_map/focus/pallas_call | solution.py:108
  40.7 2.6 %collective-permute-start = (bf16[256,128]{1,0:T(8,128)(2,1)}, bf16[256,128]{1,0:T(8,128)(2,1)S(1)}, u32[]{:S(2)}, u32[]{:S(2)}) collective-permute-start(bf16[256,128]{1,0:T(8,128)(2,1)} %focus.1), channel_id=1, source_target_pairs={{0,128},{128,0},{1,129},{129,1},{2,130},{130,2},{3,131},{131,3},{4... | collective-permute-start | bytes 196616 | tf_op jit(solution)/shard_map/ppermute | solution.py:219
  43.4 2.2 %collective-permute-done = bf16[256,128]{1,0:T(8,128)(2,1)S(1)} collective-permute-done((bf16[256,128]{1,0:T(8,128)(2,1)}, bf16[256,128]{1,0:T(8,128)(2,1)S(1)}, u32[]{:S(2)}, u32[]{:S(2)}) %collective-permute-start) | collective-permute-done | bytes 65568 | tf_op jit(solution)/shard_map/ppermute | solution.py:219
  45.6 0.8 pad_maximum_fusion.refs_3_
  46.4 1.7 %collective-permute-start.2 = (bf16[512,128]{1,0:T(8,128)(2,1)S(1)}, bf16[512,128]{1,0:T(8,128)(2,1)S(1)}, u32[]{:S(2)}, u32[]{:S(2)}) collective-permute-start(bf16[512,128]{1,0:T(8,128)(2,1)S(1)} %pad_maximum_fusion.refs_3_), channel_id=1, source_target_pairs={{0,16},{16,32},{32,48},{48,64},{64,80},{80,96},{96,112},{112,0},{1... | collective-permute-start | bytes 393224 | tf_op jit(solution)/shard_map/ppermute | solution.py:225
  48.1 0.6 fusion.9
  48.7 4.0 %collective-permute-start.4 = (bf16[512,128]{1,0:T(8,128)(2,1)S(1)}, bf16[512,128]{1,0:T(8,128)(2,1)S(1)}, u32[]{:S(2)}, u32[]{:S(2)}) collective-permute-start(bf16[512,128]{1,0:T(8,128)(2,1)S(1)} %pad_maximum_fusion.refs_3_), channel_id=1, source_target_pairs={{0,112},{16,0},{32,16},{48,32},{64,48},{80,64},{96,80},{112,96},{1... | collective-permute-start | bytes 393224 | tf_op jit(solution)/shard_map/ppermute | solution.py:229
  52.8 1.7 %collective-permute-done.2.refs_5_ = bf16[512,128]{1,0:T(8,128)(2,1)S(1)} collective-permute-done((bf16[512,128]{1,0:T(8,128)(2,1)S(1)}, bf16[512,128]{1,0:T(8,128)(2,1)S(1)}, u32[]{:S(2)}, u32[]{:S(2)}) %collective-permute-start.2) | collective-permute-done | bytes 131104 | tf_op jit(solution)/shard_map/ppermute | solution.py:225
  54.4 5.3 %subtract_convert_fusion = (bf16[32,64,1024]{2,1,0:T(8,128)(2,1)}, bf16[32,64,1024]{2,1,0:T(8,128)(2,1)}) fusion(f32[32,1024]{1,0:T(8,128)S(1)} %neg.4, f32[64,1024]{1,0:T(8,128)S(1)} %get-tuple-element.12, f32[64,1024]{1,0:T(8,128)S(1)} %get-tuple-element.10, f32[32,1024]{1,0:T(8,128)S(1)} %get-tuple-element.9, f32[32,1024]{1,0:T(8,128)S(1)} %get-tuple-element.11), kind=kLoop, calls=%fused_computation | loop fusion | flops 16777216 | bytes 9306112 | tf_op jit(solution)/shard_map/convert_element_type | solution.py:190
  59.9 2.7 %collective-permute-start.8 = (bf16[512,128]{1,0:T(8,128)(2,1)S(1)}, bf16[512,128]{1,0:T(8,128)(2,1)S(1)}, u32[]{:S(2)}, u32[]{:S(2)}) collective-permute-start(bf16[512,128]{1,0:T(8,128)(2,1)S(1)} %collective-permute-done.4.refs_7_), channel_id=1, source_target_pairs={{0,112},{16,0},{32,16},{48,32},{64,48},{80,64},{96,80},{112,96},{1... | collective-permute-start | bytes 393224 | tf_op jit(solution)/shard_map/ppermute | solution.py:229
  62.7 4.4 %select_reduce_fusion = s32[32,8,16]{2,1,0:T(8,128)S(1)} fusion(s32[32,8,16]{0,2,1:T(8,128)S(1)} %copy.14, pred[32,32]{1,0:T(8,128)(4,1)S(1)} %iota_compare_fusion.1), kind=kLoop, calls=%fused_computation.2 | loop fusion | flops 258048 | bytes 33792 | tf_op jit(solution)/shard_map/reduce_sum | solution.py:172
  67.1 4.4 %collective-permute-start.1 = (bf16[512,128]{1,0:T(8,128)(2,1)S(1)}, bf16[512,128]{1,0:T(8,128)(2,1)S(1)}, u32[]{:S(2)}, u32[]{:S(2)}) collective-permute-start(bf16[512,128]{1,0:T(8,128)(2,1)S(1)} %pad_maximum_fusion.refs_3_), channel_id=1, source_target_pairs={{0,8},{8,0},{1,9},{9,1},{2,10},{10,2},{3,11},{11,3},{4,12},{12,4},... | collective-permute-start | bytes 393224 | tf_op jit(solution)/shard_map/ppermute | solution.py:232
  71.6 0.4 collective-permute-start.3
  72.0 3.0 %collective-permute-start.12 = (bf16[512,128]{1,0:T(8,128)(2,1)S(1)}, bf16[512,128]{1,0:T(8,128)(2,1)S(1)}, u32[]{:S(2)}, u32[]{:S(2)}) collective-permute-start(bf16[512,128]{1,0:T(8,128)(2,1)S(1)} %collective-permute-done.8.refs_11_), channel_id=1, source_target_pairs={{0,112},{16,0},{32,16},{48,32},{64,48},{80,64},{96,80},{112,96},{1... | collective-permute-start | bytes 393224 | tf_op jit(solution)/shard_map/ppermute | solution.py:229
  75.8 0.4 collective-permute-start.9
  76.4 0.4 collective-permute-start.11
  76.8 1.0 collective-permute-done.12.refs_15_
  77.8 0.9 collective-permute-start.13
  78.7 2.2 %collective-permute-done.14.refs_17_ = bf16[512,128]{1,0:T(8,128)(2,1)S(1)} collective-permute-done((bf16[512,128]{1,0:T(8,128)(2,1)S(1)}, bf16[512,128]{1,0:T(8,128)(2,1)S(1)}, u32[]{:S(2)}, u32[]{:S(2)}) %collective-permute-start.14) | collective-permute-done | bytes 131104 | tf_op jit(solution)/shard_map/ppermute | solution.py:225
  80.9 1.2 %collective-permute-start.15 = (bf16[512,128]{1,0:T(8,128)(2,1)S(1)}, bf16[512,128]{1,0:T(8,128)(2,1)S(1)}, u32[]{:S(2)}, u32[]{:S(2)}) collective-permute-start(bf16[512,128]{1,0:T(8,128)(2,1)S(1)} %collective-permute-done.14.refs_17_), channel_id=1, source_target_pairs={{0,8},{8,0},{1,9},{9,1},{2,10},{10,2},{3,11},{11,3},{4,12},{12,4},... | collective-permute-start | bytes 393224 | tf_op jit(solution)/shard_map/ppermute | solution.py:232
  82.1 0.9 collective-permute-done.15.refs_18_
  83.1 2.2 %copy-done.1 = bf16[32,64,1024]{2,1,0:T(8,128)(2,1)S(1)} copy-done((bf16[32,64,1024]{2,1,0:T(8,128)(2,1)S(1)}, bf16[32,64,1024]{2,1,0:T(8,128)(2,1)}, u32[]{:S(2)}) %copy-start.1) | copy-done | bytes 4194328
  85.2 2.2 %copy-done.2 = bf16[32,64,1024]{2,1,0:T(8,128)(2,1)S(1)} copy-done((bf16[32,64,1024]{2,1,0:T(8,128)(2,1)S(1)}, bf16[32,64,1024]{2,1,0:T(8,128)(2,1)}, u32[]{:S(2)}) %copy-start.2) | copy-done | bytes 4194328
  87.4 13.4 %image.1 = bf16[1024,2,1024]{2,1,0:T(2,128)(2,1)} custom-call(s32[8,4,1,256]{3,2,1,0:T(1,128)S(1)} %broadcast_add_fusion.refs_0_, bf16[2048,1024]{1,0:T(8,128)(2,1)S(1)} %bitcast.16, bf16[2048,1024]{1,0:T(8,128)(2,1)S(1)} %bitcast.15, bf16[512,128]{1,0:T(8,128)(2,1)S(1)} %pad_maximum_fusion.refs_3_, bf16[512,128]{1,0:T(8,128)(2,1)S(1)} %collective-permute-done.1.refs_4_, ...), custom_call_target="tpu_custom_call" | custom-call | tf_op jit(solution)/shard_map/image/pallas_call | solution.py:155
  (62 shorter events, 3.2 us)
Async XLA Ops:
  0.0 1.0 %copy-start = (s32[64,32]{0,1:T(8,128)S(1)}, s32[64,32]{0,1:T(8,128)}, u32[]{:S(2)}) copy-start(s32[64,32]{0,1:T(8,128)} %param.12) | copy-start | bytes 24580
  0.0 29.2 %copy-start.6 = (s32[16]{0:T(128)S(1)}, s32[16]{0:T(128)}, u32[]{:S(2)}) copy-start(s32[16]{0:T(128)} %constant.142.clone) | copy-start | bytes 196
  0.0 29.3 %copy-start.5 = (s32[16]{0:T(128)S(1)}, s32[16]{0:T(128)}, u32[]{:S(2)}) copy-start(s32[16]{0:T(128)} %constant.141.clone) | copy-start | bytes 196
  0.0 29.8 %copy-start.4 = (s32[1024]{0:T(1024)S(1)}, s32[1024]{0:T(1024)}, u32[]{:S(2)}) copy-start(s32[1024]{0:T(1024)} %param.13) | copy-start | bytes 12292
  23.4 14.6 %all-to-all-start = ((bf16[8,256,128]{2,1,0:T(8,128)(2,1)}), bf16[8,256,128]{2,1,0:T(8,128)(2,1)S(1)}, u32[]{:S(2)}, u32[]{:S(2)}) async-start(bf16[8,256,128]{2,1,0:T(8,128)(2,1)} %bitcast.9), calls=%async_computation | async-start | bytes 1048576 | tf_op jit(solution)/shard_map/all_to_all | solution.py:213
  37.9 0.8 copy-start.3
  40.7 4.8 %collective-permute-start = (bf16[256,128]{1,0:T(8,128)(2,1)}, bf16[256,128]{1,0:T(8,128)(2,1)S(1)}, u32[]{:S(2)}, u32[]{:S(2)}) collective-permute-start(bf16[256,128]{1,0:T(8,128)(2,1)} %focus.1), channel_id=1, source_target_pairs={{0,128},{128,0},{1,129},{129,1},{2,130},{130,2},{3,131},{131,3},{4... | collective-permute-start | bytes 196616 | tf_op jit(solution)/shard_map/ppermute | solution.py:219
  46.4 8.0 %collective-permute-start.2 = (bf16[512,128]{1,0:T(8,128)(2,1)S(1)}, bf16[512,128]{1,0:T(8,128)(2,1)S(1)}, u32[]{:S(2)}, u32[]{:S(2)}) collective-permute-start(bf16[512,128]{1,0:T(8,128)(2,1)S(1)} %pad_maximum_fusion.refs_3_), channel_id=1, source_target_pairs={{0,16},{16,32},{32,48},{48,64},{64,80},{80,96},{96,112},{112,0},{1... | collective-permute-start | bytes 393224 | tf_op jit(solution)/shard_map/ppermute | solution.py:225
  48.7 11.2 %collective-permute-start.4 = (bf16[512,128]{1,0:T(8,128)(2,1)S(1)}, bf16[512,128]{1,0:T(8,128)(2,1)S(1)}, u32[]{:S(2)}, u32[]{:S(2)}) collective-permute-start(bf16[512,128]{1,0:T(8,128)(2,1)S(1)} %pad_maximum_fusion.refs_3_), channel_id=1, source_target_pairs={{0,112},{16,0},{32,16},{48,32},{64,48},{80,64},{96,80},{112,96},{1... | collective-permute-start | bytes 393224 | tf_op jit(solution)/shard_map/ppermute | solution.py:229
  54.4 8.2 %collective-permute-start.6 = (bf16[512,128]{1,0:T(8,128)(2,1)S(1)}, bf16[512,128]{1,0:T(8,128)(2,1)S(1)}, u32[]{:S(2)}, u32[]{:S(2)}) collective-permute-start(bf16[512,128]{1,0:T(8,128)(2,1)S(1)} %collective-permute-done.2.refs_5_), channel_id=1, source_target_pairs={{0,16},{16,32},{32,48},{48,64},{64,80},{80,96},{96,112},{112,0},{1... | collective-permute-start | bytes 393224 | tf_op jit(solution)/shard_map/ppermute | solution.py:225
  59.9 12.1 %collective-permute-start.8 = (bf16[512,128]{1,0:T(8,128)(2,1)S(1)}, bf16[512,128]{1,0:T(8,128)(2,1)S(1)}, u32[]{:S(2)}, u32[]{:S(2)}) collective-permute-start(bf16[512,128]{1,0:T(8,128)(2,1)S(1)} %collective-permute-done.4.refs_7_), channel_id=1, source_target_pairs={{0,112},{16,0},{32,16},{48,32},{64,48},{80,64},{96,80},{112,96},{1... | collective-permute-start | bytes 393224 | tf_op jit(solution)/shard_map/ppermute | solution.py:229
  62.7 12.3 %collective-permute-start.10 = (bf16[512,128]{1,0:T(8,128)(2,1)S(1)}, bf16[512,128]{1,0:T(8,128)(2,1)S(1)}, u32[]{:S(2)}, u32[]{:S(2)}) collective-permute-start(bf16[512,128]{1,0:T(8,128)(2,1)S(1)} %collective-permute-done.6.refs_9_), channel_id=1, source_target_pairs={{0,16},{16,32},{32,48},{48,64},{64,80},{80,96},{96,112},{112,0},{1... | collective-permute-start | bytes 393224 | tf_op jit(solution)/shard_map/ppermute | solution.py:225
  67.1 8.8 %collective-permute-start.1 = (bf16[512,128]{1,0:T(8,128)(2,1)S(1)}, bf16[512,128]{1,0:T(8,128)(2,1)S(1)}, u32[]{:S(2)}, u32[]{:S(2)}) collective-permute-start(bf16[512,128]{1,0:T(8,128)(2,1)S(1)} %pad_maximum_fusion.refs_3_), channel_id=1, source_target_pairs={{0,8},{8,0},{1,9},{9,1},{2,10},{10,2},{3,11},{11,3},{4,12},{12,4},... | collective-permute-start | bytes 393224 | tf_op jit(solution)/shard_map/ppermute | solution.py:232
  71.5 4.8 %collective-permute-start.5 = (bf16[512,128]{1,0:T(8,128)(2,1)S(1)}, bf16[512,128]{1,0:T(8,128)(2,1)S(1)}, u32[]{:S(2)}, u32[]{:S(2)}) collective-permute-start(bf16[512,128]{1,0:T(8,128)(2,1)S(1)} %collective-permute-done.4.refs_7_), channel_id=1, source_target_pairs={{0,8},{8,0},{1,9},{9,1},{2,10},{10,2},{3,11},{11,3},{4,12},{12,4},... | collective-permute-start | bytes 393224 | tf_op jit(solution)/shard_map/ppermute | solution.py:232
  71.6 4.9 %collective-permute-start.3 = (bf16[512,128]{1,0:T(8,128)(2,1)S(1)}, bf16[512,128]{1,0:T(8,128)(2,1)S(1)}, u32[]{:S(2)}, u32[]{:S(2)}) collective-permute-start(bf16[512,128]{1,0:T(8,128)(2,1)S(1)} %collective-permute-done.2.refs_5_), channel_id=1, source_target_pairs={{0,8},{8,0},{1,9},{9,1},{2,10},{10,2},{3,11},{11,3},{4,12},{12,4},... | collective-permute-start | bytes 393224 | tf_op jit(solution)/shard_map/ppermute | solution.py:232
  72.0 5.8 %collective-permute-start.12 = (bf16[512,128]{1,0:T(8,128)(2,1)S(1)}, bf16[512,128]{1,0:T(8,128)(2,1)S(1)}, u32[]{:S(2)}, u32[]{:S(2)}) collective-permute-start(bf16[512,128]{1,0:T(8,128)(2,1)S(1)} %collective-permute-done.8.refs_11_), channel_id=1, source_target_pairs={{0,112},{16,0},{32,16},{48,32},{64,48},{80,64},{96,80},{112,96},{1... | collective-permute-start | bytes 393224 | tf_op jit(solution)/shard_map/ppermute | solution.py:229
  74.9 5.9 %collective-permute-start.14 = (bf16[512,128]{1,0:T(8,128)(2,1)S(1)}, bf16[512,128]{1,0:T(8,128)(2,1)S(1)}, u32[]{:S(2)}, u32[]{:S(2)}) collective-permute-start(bf16[512,128]{1,0:T(8,128)(2,1)S(1)} %collective-permute-done.10.refs_13_), channel_id=1, source_target_pairs={{0,16},{16,32},{32,48},{48,64},{64,80},{80,96},{96,112},{112,0},{1... | collective-permute-start | bytes 393224 | tf_op jit(solution)/shard_map/ppermute | solution.py:225
  75.8 6.3 %collective-permute-start.9 = (bf16[512,128]{1,0:T(8,128)(2,1)S(1)}, bf16[512,128]{1,0:T(8,128)(2,1)S(1)}, u32[]{:S(2)}, u32[]{:S(2)}) collective-permute-start(bf16[512,128]{1,0:T(8,128)(2,1)S(1)} %collective-permute-done.8.refs_11_), channel_id=1, source_target_pairs={{0,8},{8,0},{1,9},{9,1},{2,10},{10,2},{3,11},{11,3},{4,12},{12,4},... | collective-permute-start | bytes 393224 | tf_op jit(solution)/shard_map/ppermute | solution.py:232
  76.3 5.8 %collective-permute-start.7 = (bf16[512,128]{1,0:T(8,128)(2,1)S(1)}, bf16[512,128]{1,0:T(8,128)(2,1)S(1)}, u32[]{:S(2)}, u32[]{:S(2)}) collective-permute-start(bf16[512,128]{1,0:T(8,128)(2,1)S(1)} %collective-permute-done.6.refs_9_), channel_id=1, source_target_pairs={{0,8},{8,0},{1,9},{9,1},{2,10},{10,2},{3,11},{11,3},{4,12},{12,4},... | collective-permute-start | bytes 393224 | tf_op jit(solution)/shard_map/ppermute | solution.py:232
  76.4 5.7 %collective-permute-start.11 = (bf16[512,128]{1,0:T(8,128)(2,1)S(1)}, bf16[512,128]{1,0:T(8,128)(2,1)S(1)}, u32[]{:S(2)}, u32[]{:S(2)}) collective-permute-start(bf16[512,128]{1,0:T(8,128)(2,1)S(1)} %collective-permute-done.10.refs_13_), channel_id=1, source_target_pairs={{0,8},{8,0},{1,9},{9,1},{2,10},{10,2},{3,11},{11,3},{4,12},{12,4},... | collective-permute-start | bytes 393224 | tf_op jit(solution)/shard_map/ppermute | solution.py:232
  77.8 4.3 %collective-permute-start.13 = (bf16[512,128]{1,0:T(8,128)(2,1)S(1)}, bf16[512,128]{1,0:T(8,128)(2,1)S(1)}, u32[]{:S(2)}, u32[]{:S(2)}) collective-permute-start(bf16[512,128]{1,0:T(8,128)(2,1)S(1)} %collective-permute-done.12.refs_15_), channel_id=1, source_target_pairs={{0,8},{8,0},{1,9},{9,1},{2,10},{10,2},{3,11},{11,3},{4,12},{12,4},... | collective-permute-start | bytes 393224 | tf_op jit(solution)/shard_map/ppermute | solution.py:232
  80.9 2.2 %collective-permute-start.15 = (bf16[512,128]{1,0:T(8,128)(2,1)S(1)}, bf16[512,128]{1,0:T(8,128)(2,1)S(1)}, u32[]{:S(2)}, u32[]{:S(2)}) collective-permute-start(bf16[512,128]{1,0:T(8,128)(2,1)S(1)} %collective-permute-done.14.refs_17_), channel_id=1, source_target_pairs={{0,8},{8,0},{1,9},{9,1},{2,10},{10,2},{3,11},{11,3},{4,12},{12,4},... | collective-permute-start | bytes 393224 | tf_op jit(solution)/shard_map/ppermute | solution.py:232
  83.1 2.2 %copy-start.1 = (bf16[32,64,1024]{2,1,0:T(8,128)(2,1)S(1)}, bf16[32,64,1024]{2,1,0:T(8,128)(2,1)}, u32[]{:S(2)}) copy-start(bf16[32,64,1024]{2,1,0:T(8,128)(2,1)} %get-tuple-element.13) | copy-start | bytes 12582916
  85.2 2.2 %copy-start.2 = (bf16[32,64,1024]{2,1,0:T(8,128)(2,1)S(1)}, bf16[32,64,1024]{2,1,0:T(8,128)(2,1)}, u32[]{:S(2)}) copy-start(bf16[32,64,1024]{2,1,0:T(8,128)(2,1)} %get-tuple-element.14) | copy-start | bytes 12582916

commit v2 on v0

v2 whole, which is shorter than its diff:
```python
import functools
import math

import jax
import jax.numpy as jnp
from jax import lax
from jax.experimental import pallas as pl
from jax.experimental.pallas import tpu as pltpu
from jax.sharding import Mesh
from jax.sharding import PartitionSpec as P

COLS = 32768
LANES = 128
FINE_K = 32
ANG = ("yh", "z", "core")
ROW = ("x", "yl")
FINE = ("yh", "z", "core", "x", "yl")
SMEM = pl.BlockSpec(memory_space=pltpu.SMEM)
VMEM = pl.BlockSpec(memory_space=pltpu.VMEM)


def pack_kernel(word_ref, bins_ref, out_ref, cut_sc):
    tiles, per_block = word_ref.shape
    lane = lax.broadcasted_iota(jnp.int32, (2, LANES), 1)
    at_once = 4

    def take(step, _):
        for u in range(at_once):
            for entry in range(per_block):
                word = word_ref[step * at_once + u, entry]
                row = pl.multiple_of(word >> 7, 2)
                low = bins_ref[pl.ds(row, 2), :]
                high = bins_ref[pl.ds(pl.multiple_of(row + 2, 2), 2), :]
                cut = jnp.where(lane >= (word & (LANES - 1)), low, high)
                at = ((step * at_once + u) * per_block + entry) * 2
                cut_sc[pl.ds(pl.multiple_of(at, 2), 2), :] = pltpu.roll(cut, (-word) & (LANES - 1), 1)
        return 0

    lax.fori_loop(0, tiles // at_once, take, 0)
    out_ref[...] = cut_sc[...].astype(jnp.bfloat16)


def pack(echoes, ids, starts, live):
    pulses, parts, bins = echoes.shape
    panels = bins // LANES
    tiles, per_block = ids.shape
    rows = echoes.astype(jnp.float32).reshape(pulses, parts, panels, LANES).transpose(0, 2, 1, 3)
    rows = jnp.pad(rows, ((0, 0), (1, 1), (0, 0), (0, 0)))
    rows = rows.reshape(pulses * (panels + 2) * parts, LANES)
    offs = starts - lax.axis_index(ROW) * bins
    used = jnp.arange(per_block, dtype=jnp.int32)[None, :] < live
    inside = used & (offs > -LANES) & (offs < bins)
    first = jnp.where(inside, ids * (panels + 2) + (offs >> 7) + 1, panels + 1)
    word = first * (parts * LANES) + (offs & (LANES - 1))
    return pl.pallas_call(
        pack_kernel,
        out_shape=jax.ShapeDtypeStruct((tiles * per_block * parts, LANES), jnp.bfloat16),
        in_specs=[SMEM, VMEM],
        out_specs=VMEM,
        scratch_shapes=[pltpu.VMEM((tiles * per_block * parts, LANES), jnp.float32)],
        compiler_params=pltpu.CompilerParams(vmem_limit_bytes=8 << 20),
        name="pack",
    )(word, rows)


def focus_kernel(got_ref, interp_ref, out_ref):
    tiles = interp_ref.shape[0]
    rows = out_ref.shape[0] // tiles
    panels = got_ref[0].astype(jnp.float32)
    for source in range(1, got_ref.shape[0]):
        panels += got_ref[source].astype(jnp.float32)
    panels = panels.astype(jnp.bfloat16)
    for tile in range(tiles):
        out_ref[tile * rows : (tile + 1) * rows, :] = lax.dot_general(
            panels[tile * rows : (tile + 1) * rows, :],
            interp_ref[tile],
            (((1,), (1,)), ((), ())),
            preferred_element_type=jnp.float32,
        ).astype(jnp.bfloat16)


def focus(got, interp):
    return pl.pallas_call(
        focus_kernel,
        out_shape=jax.ShapeDtypeStruct(got.shape[1:], jnp.bfloat16),
        in_specs=[VMEM] * 2,
        out_specs=VMEM,
        compiler_params=pltpu.CompilerParams(vmem_limit_bytes=4 << 20),
        name="focus",
    )(got, interp)


def place(pair_ref, code_ref, blocks, first, spread):
    tiles = code_ref.shape[0]
    half = spread.shape[0] // 2
    slots = 2 * 32
    wide = code_ref.shape[3]
    side = wide // 2
    row = lax.broadcasted_iota(jnp.int32, (2 * slots, wide), 0)
    for number, ref in enumerate(blocks):
        pair = pair_ref[first + number]
        for tile in range(tiles):
            entries = [ref[(s * tiles + tile) * side : (s * tiles + tile + 1) * side, :] for s in (0, 1)]
            hot = jnp.where(row == code_ref[tile, pair], 1.0, 0.0).astype(jnp.bfloat16)
            placed = jnp.dot(
                hot, jnp.concatenate(entries, 0), preferred_element_type=jnp.float32
            ).astype(jnp.bfloat16)
            columns = slice(tile * LANES, (tile + 1) * LANES)
            spread[number * slots : (number + 1) * slots, columns] = placed[:slots]
            spread[half + number * slots : half + (number + 1) * slots, columns] = placed[slots:]


def turns(coarse_ref, fine_ref, coarse, count, first, pulses):
    columns = pl.ds(first, pulses)
    fine_c, fine_s = fine_ref[0, :, columns], fine_ref[1, :, columns]
    cos, sin = [], []
    for number in range(count):
        here = coarse + number
        coarse_c, coarse_s = coarse_ref[0, here, :, columns], coarse_ref[1, here, :, columns]
        cos.append((coarse_c * fine_c - coarse_s * fine_s).astype(jnp.bfloat16))
        sin.append((-coarse_s * fine_c - coarse_c * fine_s).astype(jnp.bfloat16))
    return jnp.concatenate([jnp.concatenate(cos, 0), jnp.concatenate(sin, 0)], 1)


def part_kernel(pair_ref, code_ref, coarse_ref, fine_ref, *refs, first, n_blocks, more):
    blocks, rest = refs[:n_blocks], refs[n_blocks:]
    held = rest[0] if more else None
    total_ref, spread = rest[-2:]
    place(pair_ref, code_ref, blocks, first, spread)
    count = 4
    rows = count * fine_ref.shape[1]

    def step(number, _):
        here = pl.ds(pl.multiple_of(number * rows, rows), rows)
        left = turns(coarse_ref, fine_ref, number * count, count, first * 64, spread.shape[0] // 2)
        new = jnp.dot(left, spread[...], preferred_element_type=jnp.float32)
        total_ref[here, :] = held[here, :] + new if more else new
        return 0

    lax.fori_loop(0, coarse_ref.shape[1] // count, step, 0)


def last_kernel(pair_ref, code_ref, coarse_ref, fine_ref, *refs, first, n_blocks, scale):
    blocks, (held_ref, out_ref, spread) = refs[:n_blocks], refs[n_blocks:]
    number = pl.program_id(0)

    @pl.when(number == 0)
    def _():
        place(pair_ref, code_ref, blocks, first, spread)

    count = out_ref.shape[0] // FINE_K
    rows = out_ref.shape[0] * 2
    left = turns(coarse_ref, fine_ref, number * count, count, first * 64, spread.shape[0] // 2)
    new = jnp.dot(left, spread[...], preferred_element_type=jnp.float32)
    total = held_ref[pl.ds(pl.multiple_of(number * rows, rows), rows), :] + new
    out_ref[...] = (total * scale).astype(jnp.bfloat16).reshape(out_ref.shape)


def part(pairs, code, coarse, fine, blocks, held, first, scale=None):
    tiles = code.shape[0]
    rows = coarse.shape[1] * fine.shape[1]
    n = tiles * LANES
    depth = len(blocks) * 128
    operands = (pairs, code, coarse, fine, *blocks) + (() if held is None else (held,))
    specs = [SMEM] + [VMEM] * (len(operands) - 1)
    scratch = [pltpu.VMEM((depth, n), jnp.bfloat16)]
    params = pltpu.CompilerParams(vmem_limit_bytes=16 << 20)
    cost = pl.CostEstimate(
        flops=2 * rows * depth * n, transcendentals=0, bytes_accessed=rows * n * 4
    )
    if scale is None:
        return pl.pallas_call(
            functools.partial(
                part_kernel, first=first, n_blocks=len(blocks), more=held is not None
            ),
            out_shape=jax.ShapeDtypeStruct((rows, n), jnp.float32),
            in_specs=specs,
            out_specs=VMEM,
            scratch_shapes=scratch,
            input_output_aliases={} if held is None else {len(operands) - 1: 0},
            compiler_params=params,
            cost_estimate=cost,
            name="part",
        )(*operands)
    step = 128
    return pl.pallas_call(
        functools.partial(last_kernel, first=first, n_blocks=len(blocks), scale=scale),
        out_shape=jax.ShapeDtypeStruct((rows // 2, 2, n), jnp.bfloat16),
        grid=(rows // 2 // step,),
        in_specs=specs,
        out_specs=pl.BlockSpec((step, 2, n), lambda i: (i, 0, 0)),
        scratch_shapes=scratch,
        compiler_params=params,
        cost_estimate=cost,
        name="last",
    )(*operands)


def pick(table, index):
    hot = index[:, None] == jnp.arange(table.shape[0], dtype=jnp.int32)[None, :]
    return jnp.sum(jnp.where(hot[:, :, None], table[None], 0), axis=1)


def twiddles(rates, first_column, columns):
    step_angle = 2.0 * math.pi / COLS
    coarse_k = first_column + FINE_K * jnp.arange(columns // FINE_K, dtype=jnp.int32)
    coarse = ((rates[None, :] * coarse_k[:, None]) % COLS).astype(jnp.float32) * step_angle
    row = jnp.arange(2 * FINE_K, dtype=jnp.int32)
    turn = rates[None, :] * (row // 2)[:, None] + (COLS - (COLS // 4) * (row % 2))[:, None]
    within = (turn % COLS).astype(jnp.float32) * step_angle
    return (
        jnp.stack([jnp.cos(coarse), jnp.sin(coarse)])[:, :, None, :],
        jnp.stack([jnp.cos(within), jnp.sin(within)]),
    )


def body(echoes, pulse_ids, bin_start, live_count, wavenum, interp):
    blocks = lax.axis_size(ANG)
    ang_index = lax.axis_index(ANG)
    n_rows = lax.axis_size(ROW)
    ring = lax.axis_size("z")
    tiles_mine = interp.shape[0]
    block_pulses = echoes.shape[0]
    foot_len = pulse_ids.shape[1]
    per_block = foot_len // blocks
    col_dev = COLS // blocks
    first_entry = ang_index * per_block

    my_ids = lax.dynamic_slice_in_dim(pulse_ids, first_entry, per_block, 1)
    my_starts = lax.dynamic_slice_in_dim(bin_start, first_entry, per_block, 1)
    my_live = lax.dynamic_slice_in_dim(live_count, ang_index, 1, 1)
    packed = pack(echoes, my_ids - ang_index * block_pulses, my_starts, my_live)
    rows = packed.shape[0] // n_rows
    got = lax.all_to_all(packed.reshape(n_rows, rows, LANES), ROW, 0, 0, tiled=True)
    mine = focus(got, interp)

    yh, z, core = (lax.axis_index(name) for name in ANG)
    half = ring // 2
    zs = [0]
    for step in range(1, half + 1):
        zs += [-step] if step == half else [-step, step]
    shift = jnp.repeat(jnp.array(zs, jnp.int32), 2)
    at_core = core ^ (jnp.arange(2 * ring, dtype=jnp.int32) % 2)
    pairs = ((z + shift) % ring) * 2 + at_core
    order = (pairs[:, None] + 2 * ring * (yh ^ jnp.arange(2, dtype=jnp.int32))[None, :]).reshape(-1)
    tile_ids = lax.dynamic_slice_in_dim(
        pulse_ids, lax.axis_index(ROW) * tiles_mine, tiles_mine, 0
    ).reshape(tiles_mine, 2, 2 * ring, per_block)
    tile_ids = jnp.where(yh == 0, tile_ids, tile_ids[:, ::-1]) % block_pulses
    tile_ids = tile_ids + block_pulses * jnp.arange(2, dtype=jnp.int32)[None, :, None, None]
    code = tile_ids.transpose(0, 2, 1, 3)[..., None] + 2 * block_pulses * jnp.arange(2, dtype=jnp.int32)
    code = code.reshape(tiles_mine, 2 * ring, 1, 4 * per_block)
    rates = pick(wavenum.reshape(blocks, block_pulses), order).reshape(-1)
    coarse, fine = twiddles(rates, ang_index * col_dev, col_dev)

    swap = [(0, 1), (1, 0)]
    ahead = [(i, (i + 1) % ring) for i in range(ring)]
    behind = [(i, (i - 1) % ring) for i in range(ring)]
    other = lax.ppermute(mine, "yh", swap)
    forward = backward = jnp.concatenate([mine, other], 0)
    held = [forward]
    for step in range(1, half + 1):
        forward = lax.ppermute(forward, "z", ahead)
        held.append(forward)
        if step < half:
            backward = lax.ppermute(backward, "z", behind)
            held.append(backward)
    arrays = []
    for near in held:
        arrays += [near, lax.ppermute(near, "core", swap)]
    total = None
    cuts = [0, 6, 10, 14, 16]
    for first, last in zip(cuts, cuts[1:]):
        scale = foot_len ** (-0.5) if last == len(arrays) else None
        total = part(pairs, code, coarse, fine, arrays[first:last], total, first, scale)
    return total


def solution(mesh):
    finer = Mesh(mesh.devices.reshape(2, -1, 2, 4, 2), FINE)
    return jax.shard_map(
        body,
        mesh=finer,
        in_specs=(P(ANG, None, ROW), P(), P(), P(), P(), P(ROW, None, None)),
        out_specs=P(ANG, None, ROW),
        check_vma=False,
    )
```

time: 328 us -> 75.1 us (0.23)
  local copies, waits for them, and re-layouts: 168 us -> 4.58 us
  other arithmetic: 74.6 us -> 3.9 us
  starting transfers between devices: 0.04 us -> 29.9 us
  waiting for transfers between devices: 36.8 us -> 9.4 us
  Pallas kernels: 0 us -> 26.7 us
  matrix products: 25.5 us -> 0 us
  between operations: 13.7 us -> 0.19 us
  blocking collectives: 7.61 us -> 0 us
    all_gather x1 -> x0, local copies, waits for them, and re-layouts: 103 us -> none  [gather_axes(): whole = lax.all_gather(whole, axes[number], axis=dim, tiled=True)]
    convert_element_type x1 -> x0, other arithmetic: 70.2 us -> none  [tile_terms(): jnp.cos(phase_angle).astype(jnp.bfloat16)]
    all_gather x2 -> x0, waiting for transfers between devices: 36.8 us -> none  [the longest x1 36.8 us: gather_axes(): whole = lax.all_gather(whole, axes[number], axis=dim, tiled=True)]
    gather x9 -> x0, local copies, waits for them, and re-layouts: 35.7 us -> none  [the longest x8 18.3 us: tile_terms(): rates = wavenum[ids_tile]]
    pallas_call x0 -> x6, Pallas kernels: none -> 26.7 us  [the longest x3 15.9 us: part(): pl.pallas_call(functools.partial(part_kernel, first=first, n_blocks=len(b...]
    dot_general x9 -> x0, matrix products: 25.5 us -> none  [the longest x8 24.6 us: tile_terms(): lax.dot_general(left, right, (((0,), (0,)), ((), ())), preferred_element_...]
    ppermute x0 -> x16, starting transfers between devices: none -> 24 us  [the longest x3 10.4 us: body(): backward = lax.ppermute(backward, 'z', behind)]
    reshape x8 -> x1, local copies, waits for them, and re-layouts: 11.8 us -> 0.09 us  [body(): tile_ids = lax.dynamic_slice_in_dim(pulse_ids, lax.axis_index(ROW) * tile...]
  transfers between devices with their start and end apart: 2 -> 17, of which waited for: 1 -> 5; matrix products, arithmetic and copies ran while one was open for 28% -> 7% of each run, Pallas kernels for 0% -> 21%
where the time goes in v2:
time: 75.1 us; the launch traced here: 74.7 us
  starting transfers between devices  29.9 us (40%)
  Pallas kernels  26.7 us (36%)
  waiting for transfers between devices  9.4 us (13%)
  local copies, waits for them, and re-layouts  4.58 us (6%)
  other arithmetic  3.9 us (5%)
    pallas_call x3, Pallas kernels, part(): pl.pallas_call(functools.partial(part_kernel, first=first, n_blocks=len(b...  15.9 us
    ppermute x3, starting transfers between devices, body(): backward = lax.ppermute(backward, 'z', behind)  10.4 us
    ppermute x8, starting transfers between devices, body(): arrays += [near, lax.ppermute(near, 'core', swap)]  9.26 us
    all_to_all x1, starting transfers between devices, body(): lax.all_to_all(packed.reshape(n_rows, rows, LANES), ROW, 0, 0, tiled=True)  5.86 us
    pallas_call x1, Pallas kernels, part(): pl.pallas_call(functools.partial(last_kernel, first=first, n_blocks=len(b...  5.78 us
    pallas_call x1, Pallas kernels, pack(): pl.pallas_call(pack_kernel, out_shape=jax.ShapeDtypeStruct((tiles * per_b...  4.84 us
    all_to_all x1, waiting for transfers between devices, body(): lax.all_to_all(packed.reshape(n_rows, rows, LANES), ROW, 0, 0, tiled=True)  3.62 us
    ppermute x1, starting transfers between devices, body(): other = lax.ppermute(mine, 'yh', swap)  2.68 us
  transfers between devices with their start and end apart: 17, of which 5 were waited for; matrix products, arithmetic and copies ran while one was open for 7% of the time, Pallas kernels for 21%

profile of v2, /device:TPU:1, one launch (start us, length us, event | category | flops | bytes accessed | tf_op | source)
XLA Modules:
  0.0 74.7 jit_solution(4052416482481575594)
XLA Ops:
  0.0 1.2 %pad.5 = bf16[32,18,2,128]{3,2,1,0:T(2,128)(2,1)S(1)} pad(bf16[32,16,2,128]{3,2,1,0:T(2,128)(2,1)} %bitcast.13, bf16[]{:T(256)} %constant.148.clone.1), padding=0_0x1_1x0_0x0_0 | pad | bytes 557058 | tf_op jit(solution)/shard_map/jit(_pad)/pad | solution.py:48
  1.3 0.9 %and_add_fusion.word_ref = s32[64,16]{1,0:T(8,128)S(1)} fusion(s32[64,512]{1,0:T(8,128)} %param.8, s32[]{:T(128)S(6)} %select_n.116, s32[64,512]{1,0:T(8,128)} %param.9, s32[]{:T(128)S(6)} %mul.197, s32[]{:T(128)S(6)} %mul.196, s32[64]{0:T(128)S(1)} %fusion.17), kind=kLoop, calls=%fused_computation.29 | loop fusion | flops 15360 | bytes 12556 | tf_op jit(solution)/shard_map/add | solution.py:54
  2.2 4.8 %pack.1 = bf16[2048,128]{1,0:T(8,128)(2,1)} custom-call(s32[64,16]{1,0:T(8,128)S(1)} %and_add_fusion.word_ref, f32[1152,128]{1,0:T(8,128)S(1)} %convert.5.bins_ref), custom_call_target="tpu_custom_call" | custom-call | tf_op jit(solution)/shard_map/pack/pallas_call | solution.py:55
  7.0 5.9 %all-to-all-start = ((bf16[8,256,128]{2,1,0:T(8,128)(2,1)}), bf16[8,256,128]{2,1,0:T(8,128)(2,1)S(1)}, u32[]{:S(2)}, u32[]{:S(2)}) async-start(bf16[8,256,128]{2,1,0:T(8,128)(2,1)} %bitcast.6), calls=%async_computation | async-start | bytes 1048576 | tf_op jit(solution)/shard_map/all_to_all | solution.py:234
  12.9 0.7 broadcast_add_fusion.2
  14.0 0.8 %broadcast_in_dim.45 = s32[32,32]{1,0:T(8,128)S(1)} reshape(s32[1024]{0:T(1024)} %param.11) | data formatting | bytes 8192 | tf_op jit(solution)/shard_map/jit(_where)/broadcast_in_dim | solution.py:201
  14.7 0.2 select_reduce_fusion
  15.0 0.7 constant_dynamic-slice_fusion.1
  16.2 0.6 fusion.12
  16.8 1.1 %fusion.4 = (f32[1,64,1024]{2,1,0:T(8,128)S(1)}, f32[1,64,1024]{2,1,0:T(8,128)S(1)}) fusion(s32[64]{0:T(128)S(1)} %get-tuple-element.10, s32[64]{0:T(128)S(1)} %get-tuple-element.9, s32[1024]{0:T(1024)S(1)} %mul.177), kind=kLoop, calls=%fused_computation.19 | loop fusion | flops 983040 | bytes 528896 | tf_op jit(solution)/shard_map/cos | solution.py:213
  17.9 3.6 %all-to-all-done.got_ref = bf16[8,256,128]{2,1,0:T(8,128)(2,1)S(1)} async-done(((bf16[8,256,128]{2,1,0:T(8,128)(2,1)}), bf16[8,256,128]{2,1,0:T(8,128)(2,1)S(1)}, u32[]{:S(2)}, u32[]{:S(2)}) %all-to-all-start) | async-done | bytes 524320 | tf_op jit(solution)/shard_map/all_to_all | solution.py:234
  21.6 0.9 %copy-done.1 = bf16[8,128,128]{2,1,0:T(8,128)(2,1)S(1)} copy-done((bf16[8,128,128]{2,1,0:T(8,128)(2,1)S(1)}, bf16[8,128,128]{2,1,0:T(8,128)(2,1)}, u32[]{:S(2)}) %copy-start.1) | copy-done | bytes 262168
  22.5 0.2 focus.1
  22.7 2.7 %collective-permute-start = (bf16[256,128]{1,0:T(8,128)(2,1)S(1)}, bf16[256,128]{1,0:T(8,128)(2,1)S(1)}, u32[]{:S(2)}, u32[]{:S(2)}) collective-permute-start(bf16[256,128]{1,0:T(8,128)(2,1)S(1)} %focus.1), channel_id=1, source_target_pairs={{0,128},{128,0},{1,129},{129,1},{2,130},{130,2},{3,131},{131,3},{4... | collective-permute-start | bytes 196616 | tf_op jit(solution)/shard_map/ppermute | solution.py:259
  25.5 1.9 %collective-permute-done = bf16[256,128]{1,0:T(8,128)(2,1)S(1)} collective-permute-done((bf16[256,128]{1,0:T(8,128)(2,1)S(1)}, bf16[256,128]{1,0:T(8,128)(2,1)S(1)}, u32[]{:S(2)}, u32[]{:S(2)}) %collective-permute-start) | collective-permute-done | bytes 65568 | tf_op jit(solution)/shard_map/ppermute | solution.py:259
  27.4 1.7 %collective-permute-start.1 = (bf16[512,128]{1,0:T(8,128)(2,1)S(1)}, bf16[512,128]{1,0:T(8,128)(2,1)S(1)}, u32[]{:S(2)}, u32[]{:S(2)}) collective-permute-start(bf16[512,128]{1,0:T(8,128)(2,1)S(1)} %pad_maximum_fusion.2.refs_0_), channel_id=1, source_target_pairs={{0,16},{16,32},{32,48},{48,64},{64,80},{80,96},{96,112},{112,0},{1... | collective-permute-start | bytes 393224 | tf_op jit(solution)/shard_map/ppermute | solution.py:263
  29.1 4.0 %collective-permute-start.7 = (bf16[512,128]{1,0:T(8,128)(2,1)S(1)}, bf16[512,128]{1,0:T(8,128)(2,1)S(1)}, u32[]{:S(2)}, u32[]{:S(2)}) collective-permute-start(bf16[512,128]{1,0:T(8,128)(2,1)S(1)} %pad_maximum_fusion.2.refs_0_), channel_id=1, source_target_pairs={{0,112},{16,0},{32,16},{48,32},{64,48},{80,64},{96,80},{112,96},{1... | collective-permute-start | bytes 393224 | tf_op jit(solution)/shard_map/ppermute | solution.py:266
  33.2 3.2 %collective-permute-start.13 = (bf16[512,128]{1,0:T(8,128)(2,1)S(1)}, bf16[512,128]{1,0:T(8,128)(2,1)S(1)}, u32[]{:S(2)}, u32[]{:S(2)}) collective-permute-start(bf16[512,128]{1,0:T(8,128)(2,1)S(1)} %pad_maximum_fusion.2.refs_0_), channel_id=1, source_target_pairs={{0,8},{8,0},{1,9},{9,1},{2,10},{10,2},{3,11},{11,3},{4,12},{12,4},... | collective-permute-start | bytes 393224 | tf_op jit(solution)/shard_map/ppermute | solution.py:270
  36.5 2.7 %collective-permute-start.14 = (bf16[512,128]{1,0:T(8,128)(2,1)S(1)}, bf16[512,128]{1,0:T(8,128)(2,1)S(1)}, u32[]{:S(2)}, u32[]{:S(2)}) collective-permute-start(bf16[512,128]{1,0:T(8,128)(2,1)S(1)} %collective-permute-done.1.refs_2_), channel_id=1, source_target_pairs={{0,8},{8,0},{1,9},{9,1},{2,10},{10,2},{3,11},{11,3},{4,12},{12,4},... | collective-permute-start | bytes 393224 | tf_op jit(solution)/shard_map/ppermute | solution.py:270
  39.3 2.9 %collective-permute-start.8 = (bf16[512,128]{1,0:T(8,128)(2,1)S(1)}, bf16[512,128]{1,0:T(8,128)(2,1)S(1)}, u32[]{:S(2)}, u32[]{:S(2)}) collective-permute-start(bf16[512,128]{1,0:T(8,128)(2,1)S(1)} %collective-permute-done.7.refs_4_), channel_id=1, source_target_pairs={{0,112},{16,0},{32,16},{48,32},{64,48},{80,64},{96,80},{112,96},{1... | collective-permute-start | bytes 393224 | tf_op jit(solution)/shard_map/ppermute | solution.py:266
  42.5 2.5 %collective-permute-done.8.refs_2_ = bf16[512,128]{1,0:T(8,128)(2,1)S(1)} collective-permute-done((bf16[512,128]{1,0:T(8,128)(2,1)S(1)}, bf16[512,128]{1,0:T(8,128)(2,1)S(1)}, u32[]{:S(2)}, u32[]{:S(2)}) %collective-permute-start.8) | collective-permute-done | bytes 131104 | tf_op jit(solution)/shard_map/ppermute | solution.py:266
  45.0 1.0 %collective-permute-start.12 = (bf16[512,128]{1,0:T(8,128)(2,1)S(1)}, bf16[512,128]{1,0:T(8,128)(2,1)S(1)}, u32[]{:S(2)}, u32[]{:S(2)}) collective-permute-start(bf16[512,128]{1,0:T(8,128)(2,1)S(1)} %collective-permute-done.8.refs_2_), channel_id=1, source_target_pairs={{0,8},{8,0},{1,9},{9,1},{2,10},{10,2},{3,11},{11,3},{4,12},{12,4},... | collective-permute-start | bytes 393224 | tf_op jit(solution)/shard_map/ppermute | solution.py:270
  45.9 3.4 %collective-permute-start.9 = (bf16[512,128]{1,0:T(8,128)(2,1)S(1)}, bf16[512,128]{1,0:T(8,128)(2,1)S(1)}, u32[]{:S(2)}, u32[]{:S(2)}) collective-permute-start(bf16[512,128]{1,0:T(8,128)(2,1)S(1)} %collective-permute-done.8.refs_2_), channel_id=1, source_target_pairs={{0,112},{16,0},{32,16},{48,32},{64,48},{80,64},{96,80},{112,96},{1... | collective-permute-start | bytes 393224 | tf_op jit(solution)/shard_map/ppermute | solution.py:266
  49.4 0.3 collective-permute-start.11
  49.7 5.8 %part.3.refs_4_ = f32[2048,1024]{1,0:T(8,128)S(1)} custom-call(s32[16]{0:T(128)S(1)} %fusion.19.pair_ref, s32[8,16,1,64]{3,2,1,0:T(1,128)S(1)} %broadcast_add_fusion.code_ref, f32[2,32,1,1024]{3,2,1,0:T(1,128)S(1)} %broadcast_in_dim.48.coarse_ref, f32[2,64,1024]{2,1,0:T(8,128)S(1)} %pad_maximum_fusion.fine_ref, ...), custom_call_target="tpu_custom_call" | custom-call | flops 3221225472 | bytes 8388608 | tf_op jit(solution)/shard_map/part/pallas_call | solution.py:172
  55.5 0.2 collective-permute-done.3.refs_0_
  55.7 1.1 %collective-permute-start.6 = (bf16[512,128]{1,0:T(8,128)(2,1)S(1)}, bf16[512,128]{1,0:T(8,128)(2,1)S(1)}, u32[]{:S(2)}, u32[]{:S(2)}) collective-permute-start(bf16[512,128]{1,0:T(8,128)(2,1)S(1)} %collective-permute-done.3.refs_0_), channel_id=1, source_target_pairs={{0,8},{8,0},{1,9},{9,1},{2,10},{10,2},{3,11},{11,3},{4,12},{12,4},... | collective-permute-start | bytes 393224 | tf_op jit(solution)/shard_map/ppermute | solution.py:270
  56.9 5.1 %part.4.refs_4_ = f32[2048,1024]{1,0:T(8,128)S(1)} custom-call(s32[16]{0:T(128)S(1)} %fusion.19.pair_ref, s32[8,16,1,64]{3,2,1,0:T(1,128)S(1)} %broadcast_add_fusion.code_ref, f32[2,32,1,1024]{3,2,1,0:T(1,128)S(1)} %broadcast_in_dim.48.coarse_ref, f32[2,64,1024]{2,1,0:T(8,128)S(1)} %pad_maximum_fusion.fine_ref, ...), custom_call_target="tpu_custom_call", output_to_operand_aliasing={{}: (8, {})} | custom-call | flops 2147483648 | bytes 8388608 | tf_op jit(solution)/shard_map/part/pallas_call | solution.py:172
  62.0 1.2 %collective-permute-done.4.refs_0_ = bf16[512,128]{1,0:T(8,128)(2,1)S(1)} collective-permute-done((bf16[512,128]{1,0:T(8,128)(2,1)S(1)}, bf16[512,128]{1,0:T(8,128)(2,1)S(1)}, u32[]{:S(2)}, u32[]{:S(2)}) %collective-permute-start.4) | collective-permute-done | bytes 131104 | tf_op jit(solution)/shard_map/ppermute | solution.py:263
  63.1 0.8 %collective-permute-start.5 = (bf16[512,128]{1,0:T(8,128)(2,1)S(1)}, bf16[512,128]{1,0:T(8,128)(2,1)S(1)}, u32[]{:S(2)}, u32[]{:S(2)}) collective-permute-start(bf16[512,128]{1,0:T(8,128)(2,1)S(1)} %collective-permute-done.4.refs_0_), channel_id=1, source_target_pairs={{0,8},{8,0},{1,9},{9,1},{2,10},{10,2},{3,11},{11,3},{4,12},{12,4},... | collective-permute-start | bytes 393224 | tf_op jit(solution)/shard_map/ppermute | solution.py:270
  63.9 5.0 %part.5.refs_2_ = f32[2048,1024]{1,0:T(8,128)S(1)} custom-call(s32[16]{0:T(128)S(1)} %fusion.19.pair_ref, s32[8,16,1,64]{3,2,1,0:T(1,128)S(1)} %broadcast_add_fusion.code_ref, f32[2,32,1,1024]{3,2,1,0:T(1,128)S(1)} %broadcast_in_dim.48.coarse_ref, f32[2,64,1024]{2,1,0:T(8,128)S(1)} %pad_maximum_fusion.fine_ref, ...), custom_call_target="tpu_custom_call", output_to_operand_aliasing={{}: (8, {})} | custom-call | flops 2147483648 | bytes 8388608 | tf_op jit(solution)/shard_map/part/pallas_call | solution.py:172
  68.9 5.8 %last.1 = bf16[1024,2,1024]{2,1,0:T(2,128)(2,1)} custom-call(s32[16]{0:T(128)S(1)} %fusion.19.pair_ref, s32[8,16,1,64]{3,2,1,0:T(1,128)S(1)} %broadcast_add_fusion.code_ref, f32[2,32,1,1024]{3,2,1,0:T(1,128)S(1)} %broadcast_in_dim.48.coarse_ref, f32[2,64,1024]{2,1,0:T(8,128)S(1)} %pad_maximum_fusion.fine_ref, ...), custom_call_target="tpu_custom_call" | custom-call | flops 1073741824 | bytes 8388608 | tf_op jit(solution)/shard_map/last/pallas_call | solution.py:186
  (46 shorter events, 1.6 us)
Async XLA Ops:
  0.0 1.2 %copy-start = (s32[64,32]{0,1:T(8,128)S(1)}, s32[64,32]{0,1:T(8,128)}, u32[]{:S(2)}) copy-start(s32[64,32]{0,1:T(8,128)} %param.10) | copy-start | bytes 24580
  7.0 14.6 %all-to-all-start = ((bf16[8,256,128]{2,1,0:T(8,128)(2,1)}), bf16[8,256,128]{2,1,0:T(8,128)(2,1)S(1)}, u32[]{:S(2)}, u32[]{:S(2)}) async-start(bf16[8,256,128]{2,1,0:T(8,128)(2,1)} %bitcast.6), calls=%async_computation | async-start | bytes 1048576 | tf_op jit(solution)/shard_map/all_to_all | solution.py:234
  21.6 1.0 %copy-start.1 = (bf16[8,128,128]{2,1,0:T(8,128)(2,1)S(1)}, bf16[8,128,128]{2,1,0:T(8,128)(2,1)}, u32[]{:S(2)}) copy-start(bf16[8,128,128]{2,1,0:T(8,128)(2,1)} %interp_ref.1) | copy-start | bytes 786436
  22.7 4.7 %collective-permute-start = (bf16[256,128]{1,0:T(8,128)(2,1)S(1)}, bf16[256,128]{1,0:T(8,128)(2,1)S(1)}, u32[]{:S(2)}, u32[]{:S(2)}) collective-permute-start(bf16[256,128]{1,0:T(8,128)(2,1)S(1)} %focus.1), channel_id=1, source_target_pairs={{0,128},{128,0},{1,129},{129,1},{2,130},{130,2},{3,131},{131,3},{4... | collective-permute-start | bytes 196616 | tf_op jit(solution)/shard_map/ppermute | solution.py:259
  27.4 9.0 %collective-permute-start.1 = (bf16[512,128]{1,0:T(8,128)(2,1)S(1)}, bf16[512,128]{1,0:T(8,128)(2,1)S(1)}, u32[]{:S(2)}, u32[]{:S(2)}) collective-permute-start(bf16[512,128]{1,0:T(8,128)(2,1)S(1)} %pad_maximum_fusion.2.refs_0_), channel_id=1, source_target_pairs={{0,16},{16,32},{32,48},{48,64},{64,80},{80,96},{96,112},{112,0},{1... | collective-permute-start | bytes 393224 | tf_op jit(solution)/shard_map/ppermute | solution.py:263
  29.1 10.1 %collective-permute-start.7 = (bf16[512,128]{1,0:T(8,128)(2,1)S(1)}, bf16[512,128]{1,0:T(8,128)(2,1)S(1)}, u32[]{:S(2)}, u32[]{:S(2)}) collective-permute-start(bf16[512,128]{1,0:T(8,128)(2,1)S(1)} %pad_maximum_fusion.2.refs_0_), channel_id=1, source_target_pairs={{0,112},{16,0},{32,16},{48,32},{64,48},{80,64},{96,80},{112,96},{1... | collective-permute-start | bytes 393224 | tf_op jit(solution)/shard_map/ppermute | solution.py:266
  33.2 12.7 %collective-permute-start.13 = (bf16[512,128]{1,0:T(8,128)(2,1)S(1)}, bf16[512,128]{1,0:T(8,128)(2,1)S(1)}, u32[]{:S(2)}, u32[]{:S(2)}) collective-permute-start(bf16[512,128]{1,0:T(8,128)(2,1)S(1)} %pad_maximum_fusion.2.refs_0_), channel_id=1, source_target_pairs={{0,8},{8,0},{1,9},{9,1},{2,10},{10,2},{3,11},{11,3},{4,12},{12,4},... | collective-permute-start | bytes 393224 | tf_op jit(solution)/shard_map/ppermute | solution.py:270
  36.5 13.2 %collective-permute-start.14 = (bf16[512,128]{1,0:T(8,128)(2,1)S(1)}, bf16[512,128]{1,0:T(8,128)(2,1)S(1)}, u32[]{:S(2)}, u32[]{:S(2)}) collective-permute-start(bf16[512,128]{1,0:T(8,128)(2,1)S(1)} %collective-permute-done.1.refs_2_), channel_id=1, source_target_pairs={{0,8},{8,0},{1,9},{9,1},{2,10},{10,2},{3,11},{11,3},{4,12},{12,4},... | collective-permute-start | bytes 393224 | tf_op jit(solution)/shard_map/ppermute | solution.py:270
  39.2 10.2 %collective-permute-start.2 = (bf16[512,128]{1,0:T(8,128)(2,1)S(1)}, bf16[512,128]{1,0:T(8,128)(2,1)S(1)}, u32[]{:S(2)}, u32[]{:S(2)}) collective-permute-start(bf16[512,128]{1,0:T(8,128)(2,1)S(1)} %collective-permute-done.1.refs_2_), channel_id=1, source_target_pairs={{0,16},{16,32},{32,48},{48,64},{64,80},{80,96},{96,112},{112,0},{1... | collective-permute-start | bytes 393224 | tf_op jit(solution)/shard_map/ppermute | solution.py:263
  39.2 10.5 %collective-permute-start.15 = (bf16[512,128]{1,0:T(8,128)(2,1)S(1)}, bf16[512,128]{1,0:T(8,128)(2,1)S(1)}, u32[]{:S(2)}, u32[]{:S(2)}) collective-permute-start(bf16[512,128]{1,0:T(8,128)(2,1)S(1)} %collective-permute-done.7.refs_4_), channel_id=1, source_target_pairs={{0,8},{8,0},{1,9},{9,1},{2,10},{10,2},{3,11},{11,3},{4,12},{12,4},... | collective-permute-start | bytes 393224 | tf_op jit(solution)/shard_map/ppermute | solution.py:270
  39.3 5.7 %collective-permute-start.8 = (bf16[512,128]{1,0:T(8,128)(2,1)S(1)}, bf16[512,128]{1,0:T(8,128)(2,1)S(1)}, u32[]{:S(2)}, u32[]{:S(2)}) collective-permute-start(bf16[512,128]{1,0:T(8,128)(2,1)S(1)} %collective-permute-done.7.refs_4_), channel_id=1, source_target_pairs={{0,112},{16,0},{32,16},{48,32},{64,48},{80,64},{96,80},{112,96},{1... | collective-permute-start | bytes 393224 | tf_op jit(solution)/shard_map/ppermute | solution.py:266
  45.0 11.9 %collective-permute-start.12 = (bf16[512,128]{1,0:T(8,128)(2,1)S(1)}, bf16[512,128]{1,0:T(8,128)(2,1)S(1)}, u32[]{:S(2)}, u32[]{:S(2)}) collective-permute-start(bf16[512,128]{1,0:T(8,128)(2,1)S(1)} %collective-permute-done.8.refs_2_), channel_id=1, source_target_pairs={{0,8},{8,0},{1,9},{9,1},{2,10},{10,2},{3,11},{11,3},{4,12},{12,4},... | collective-permute-start | bytes 393224 | tf_op jit(solution)/shard_map/ppermute | solution.py:270
  45.9 10.8 %collective-permute-start.9 = (bf16[512,128]{1,0:T(8,128)(2,1)S(1)}, bf16[512,128]{1,0:T(8,128)(2,1)S(1)}, u32[]{:S(2)}, u32[]{:S(2)}) collective-permute-start(bf16[512,128]{1,0:T(8,128)(2,1)S(1)} %collective-permute-done.8.refs_2_), channel_id=1, source_target_pairs={{0,112},{16,0},{32,16},{48,32},{64,48},{80,64},{96,80},{112,96},{1... | collective-permute-start | bytes 393224 | tf_op jit(solution)/shard_map/ppermute | solution.py:266
  49.4 7.5 %collective-permute-start.11 = (bf16[512,128]{1,0:T(8,128)(2,1)S(1)}, bf16[512,128]{1,0:T(8,128)(2,1)S(1)}, u32[]{:S(2)}, u32[]{:S(2)}) collective-permute-start(bf16[512,128]{1,0:T(8,128)(2,1)S(1)} %collective-permute-done.2.refs_0_), channel_id=1, source_target_pairs={{0,8},{8,0},{1,9},{9,1},{2,10},{10,2},{3,11},{11,3},{4,12},{12,4},... | collective-permute-start | bytes 393224 | tf_op jit(solution)/shard_map/ppermute | solution.py:270
  49.7 6.0 %collective-permute-start.3 = (bf16[512,128]{1,0:T(8,128)(2,1)S(1)}, bf16[512,128]{1,0:T(8,128)(2,1)S(1)}, u32[]{:S(2)}, u32[]{:S(2)}) collective-permute-start(bf16[512,128]{1,0:T(8,128)(2,1)S(1)} %collective-permute-done.2.refs_0_), channel_id=1, source_target_pairs={{0,16},{16,32},{32,48},{48,64},{64,80},{80,96},{96,112},{112,0},{1... | collective-permute-start | bytes 393224 | tf_op jit(solution)/shard_map/ppermute | solution.py:263
  55.7 8.2 %collective-permute-start.6 = (bf16[512,128]{1,0:T(8,128)(2,1)S(1)}, bf16[512,128]{1,0:T(8,128)(2,1)S(1)}, u32[]{:S(2)}, u32[]{:S(2)}) collective-permute-start(bf16[512,128]{1,0:T(8,128)(2,1)S(1)} %collective-permute-done.3.refs_0_), channel_id=1, source_target_pairs={{0,8},{8,0},{1,9},{9,1},{2,10},{10,2},{3,11},{11,3},{4,12},{12,4},... | collective-permute-start | bytes 393224 | tf_op jit(solution)/shard_map/ppermute | solution.py:270
  56.8 6.3 %collective-permute-start.4 = (bf16[512,128]{1,0:T(8,128)(2,1)S(1)}, bf16[512,128]{1,0:T(8,128)(2,1)S(1)}, u32[]{:S(2)}, u32[]{:S(2)}) collective-permute-start(bf16[512,128]{1,0:T(8,128)(2,1)S(1)} %collective-permute-done.3.refs_0_), channel_id=1, source_target_pairs={{0,16},{16,32},{32,48},{48,64},{64,80},{80,96},{96,112},{112,0},{1... | collective-permute-start | bytes 393224 | tf_op jit(solution)/shard_map/ppermute | solution.py:263
  56.8 7.1 %collective-permute-start.10 = (bf16[512,128]{1,0:T(8,128)(2,1)S(1)}, bf16[512,128]{1,0:T(8,128)(2,1)S(1)}, u32[]{:S(2)}, u32[]{:S(2)}) collective-permute-start(bf16[512,128]{1,0:T(8,128)(2,1)S(1)} %collective-permute-done.9.refs_2_), channel_id=1, source_target_pairs={{0,8},{8,0},{1,9},{9,1},{2,10},{10,2},{3,11},{11,3},{4,12},{12,4},... | collective-permute-start | bytes 393224 | tf_op jit(solution)/shard_map/ppermute | solution.py:270
  63.1 5.8 %collective-permute-start.5 = (bf16[512,128]{1,0:T(8,128)(2,1)S(1)}, bf16[512,128]{1,0:T(8,128)(2,1)S(1)}, u32[]{:S(2)}, u32[]{:S(2)}) collective-permute-start(bf16[512,128]{1,0:T(8,128)(2,1)S(1)} %collective-permute-done.4.refs_0_), channel_id=1, source_target_pairs={{0,8},{8,0},{1,9},{9,1},{2,10},{10,2},{3,11},{11,3},{4,12},{12,4},... | collective-permute-start | bytes 393224 | tf_op jit(solution)/shard_map/ppermute | solution.py:270

commit v3 on v2

--- a/solution.py
+++ b/solution.py
@@ -63,8 +63,8 @@
     )(word, rows)
 
 
-def focus_kernel(got_ref, interp_ref, out_ref):
-    tiles = interp_ref.shape[0]
+def focus_kernel(got_ref, turned_ref, out_ref):
+    tiles = turned_ref.shape[0]
     rows = out_ref.shape[0] // tiles
     panels = got_ref[0].astype(jnp.float32)
     for source in range(1, got_ref.shape[0]):
@@ -73,13 +73,13 @@
     for tile in range(tiles):
         out_ref[tile * rows : (tile + 1) * rows, :] = lax.dot_general(
             panels[tile * rows : (tile + 1) * rows, :],
-            interp_ref[tile],
-            (((1,), (1,)), ((), ())),
+            turned_ref[tile],
+            (((1,), (0,)), ((), ())),
             preferred_element_type=jnp.float32,
         ).astype(jnp.bfloat16)
 
 
-def focus(got, interp):
+def focus(got, turned):
     return pl.pallas_call(
         focus_kernel,
         out_shape=jax.ShapeDtypeStruct(got.shape[1:], jnp.bfloat16),
@@ -87,7 +87,7 @@
         out_specs=VMEM,
         compiler_params=pltpu.CompilerParams(vmem_limit_bytes=4 << 20),
         name="focus",
-    )(got, interp)
+    )(got, turned)
 
 
 def place(pair_ref, code_ref, blocks, first, spread):
@@ -110,64 +110,75 @@
             spread[half + number * slots : half + (number + 1) * slots, columns] = placed[slots:]
 
 
-def turns(coarse_ref, fine_ref, coarse, count, first, pulses):
-    columns = pl.ds(first, pulses)
-    fine_c, fine_s = fine_ref[0, :, columns], fine_ref[1, :, columns]
-    cos, sin = [], []
-    for number in range(count):
-        here = coarse + number
-        coarse_c, coarse_s = coarse_ref[0, here, :, columns], coarse_ref[1, here, :, columns]
-        cos.append((coarse_c * fine_c - coarse_s * fine_s).astype(jnp.bfloat16))
-        sin.append((-coarse_s * fine_c - coarse_c * fine_s).astype(jnp.bfloat16))
-    return jnp.concatenate([jnp.concatenate(cos, 0), jnp.concatenate(sin, 0)], 1)
-
-
-def part_kernel(pair_ref, code_ref, coarse_ref, fine_ref, *refs, first, n_blocks, more):
+def turn_kernel(coarse_ref, fine_ref, *out_refs):
+    pulses = coarse_ref.shape[3] // len(out_refs)
+    rows = fine_ref.shape[1]
+
+    def step(number, _):
+        here = pl.ds(pl.multiple_of(number * rows, rows), rows)
+        for which, out_ref in enumerate(out_refs):
+            columns = pl.ds(which * pulses, pulses)
+            coarse_c, coarse_s = coarse_ref[0, number, :, columns], coarse_ref[1, number, :, columns]
+            fine_c, fine_s = fine_ref[0, :, columns], fine_ref[1, :, columns]
+            out_ref[here, :pulses] = (coarse_c * fine_c - coarse_s * fine_s).astype(jnp.bfloat16)
+            out_ref[here, pulses:] = (-coarse_s * fine_c - coarse_c * fine_s).astype(jnp.bfloat16)
+        return 0
+
+    lax.fori_loop(0, coarse_ref.shape[1], step, 0, unroll=4)
+
+
+def turns(coarse, fine, parts):
+    rows = coarse.shape[1] * fine.shape[1]
+    shape = jax.ShapeDtypeStruct((rows, 2 * coarse.shape[3] // parts), jnp.bfloat16)
+    return pl.pallas_call(
+        turn_kernel,
+        out_shape=[shape] * parts,
+        in_specs=[VMEM] * 2,
+        out_specs=[VMEM] * parts,
+        compiler_params=pltpu.CompilerParams(vmem_limit_bytes=24 << 20),
+        name="turns",
+    )(coarse, fine)
+
+
+def part_kernel(pair_ref, code_ref, turn_ref, *refs, first, n_blocks, more):
     blocks, rest = refs[:n_blocks], refs[n_blocks:]
-    held = rest[0] if more else None
     total_ref, spread = rest[-2:]
     place(pair_ref, code_ref, blocks, first, spread)
-    count = 4
-    rows = count * fine_ref.shape[1]
-
-    def step(number, _):
-        here = pl.ds(pl.multiple_of(number * rows, rows), rows)
-        left = turns(coarse_ref, fine_ref, number * count, count, first * 64, spread.shape[0] // 2)
-        new = jnp.dot(left, spread[...], preferred_element_type=jnp.float32)
-        total_ref[here, :] = held[here, :] + new if more else new
-        return 0
-
-    lax.fori_loop(0, coarse_ref.shape[1] // count, step, 0)
-
-
-def last_kernel(pair_ref, code_ref, coarse_ref, fine_ref, *refs, first, n_blocks, scale):
-    blocks, (held_ref, out_ref, spread) = refs[:n_blocks], refs[n_blocks:]
-    number = pl.program_id(0)
-
-    @pl.when(number == 0)
-    def _():
-        place(pair_ref, code_ref, blocks, first, spread)
-
-    count = out_ref.shape[0] // FINE_K
-    rows = out_ref.shape[0] * 2
-    left = turns(coarse_ref, fine_ref, number * count, count, first * 64, spread.shape[0] // 2)
-    new = jnp.dot(left, spread[...], preferred_element_type=jnp.float32)
-    total = held_ref[pl.ds(pl.multiple_of(number * rows, rows), rows), :] + new
-    out_ref[...] = (total * scale).astype(jnp.bfloat16).reshape(out_ref.shape)
-
-
-def part(pairs, code, coarse, fine, blocks, held, first, scale=None):
+    rows = 512
+    for start in range(0, turn_ref.shape[0], rows):
+        here = slice(start, start + rows)
+        new = jnp.dot(turn_ref[here, :], spread[...], preferred_element_type=jnp.float32)
+        total_ref[here, :] = rest[0][here, :] + new if more else new
+
+
+def last_kernel(pair_ref, code_ref, turn_ref, *refs, first, n_blocks, scale):
+    blocks, (held_ref, out_ref, spread, ready, sems) = refs[:n_blocks], refs[n_blocks:]
+    place(pair_ref, code_ref, blocks, first, spread)
+    copies = sems.shape[0]
+    columns = ready.shape[0] // copies
+    rows = 2 * columns
+    sent = []
+    for number in range(copies):
+        here = slice(number * rows, (number + 1) * rows)
+        new = jnp.dot(turn_ref[here, :], spread[...], preferred_element_type=jnp.float32)
+        total = ((held_ref[here, :] + new) * scale).astype(jnp.bfloat16)
+        there = pl.ds(number * columns, columns)
+        ready[there] = total.reshape((columns,) + ready.shape[1:])
+        copy = pltpu.make_async_copy(ready.at[there], out_ref.at[there], sems.at[number])
+        copy.start()
+        sent.append(copy)
+    for copy in sent:
+        copy.wait()
+
+
+def part(pairs, code, turn, blocks, held, first, scale=None):
     tiles = code.shape[0]
-    rows = coarse.shape[1] * fine.shape[1]
+    rows, depth = turn.shape
     n = tiles * LANES
-    depth = len(blocks) * 128
-    operands = (pairs, code, coarse, fine, *blocks) + (() if held is None else (held,))
+    operands = (pairs, code, turn, *blocks) + (() if held is None else (held,))
     specs = [SMEM] + [VMEM] * (len(operands) - 1)
     scratch = [pltpu.VMEM((depth, n), jnp.bfloat16)]
-    params = pltpu.CompilerParams(vmem_limit_bytes=16 << 20)
-    cost = pl.CostEstimate(
-        flops=2 * rows * depth * n, transcendentals=0, bytes_accessed=rows * n * 4
-    )
+    params = pltpu.CompilerParams(vmem_limit_bytes=24 << 20)
     if scale is None:
         return pl.pallas_call(
             functools.partial(
@@ -179,19 +190,17 @@
             scratch_shapes=scratch,
             input_output_aliases={} if held is None else {len(operands) - 1: 0},
             compiler_params=params,
-            cost_estimate=cost,
             name="part",
         )(*operands)
-    step = 128
+    shape = jax.ShapeDtypeStruct((rows // 2, 2, n), jnp.bfloat16)
     return pl.pallas_call(
         functools.partial(last_kernel, first=first, n_blocks=len(blocks), scale=scale),
-        out_shape=jax.ShapeDtypeStruct((rows // 2, 2, n), jnp.bfloat16),
-        grid=(rows // 2 // step,),
+        out_shape=shape,
         in_specs=specs,
-        out_specs=pl.BlockSpec((step, 2, n), lambda i: (i, 0, 0)),
-        scratch_shapes=scratch,
+        out_specs=pl.BlockSpec(memory_space=pl.ANY),
+        scratch_shapes=scratch
+        + [pltpu.VMEM(shape.shape, shape.dtype), pltpu.SemaphoreType.DMA((8,))],
         compiler_params=params,
-        cost_estimate=cost,
         name="last",
     )(*operands)
 
@@ -232,16 +241,17 @@
     packed = pack(echoes, my_ids - ang_index * block_pulses, my_starts, my_live)
     rows = packed.shape[0] // n_rows
     got = lax.all_to_all(packed.reshape(n_rows, rows, LANES), ROW, 0, 0, tiled=True)
-    mine = focus(got, interp)
+    mine = focus(got, interp.swapaxes(1, 2))
 
     yh, z, core = (lax.axis_index(name) for name in ANG)
     half = ring // 2
-    zs = [0]
-    for step in range(1, half + 1):
-        zs += [-step] if step == half else [-step, step]
-    shift = jnp.repeat(jnp.array(zs, jnp.int32), 2)
-    at_core = core ^ (jnp.arange(2 * ring, dtype=jnp.int32) % 2)
-    pairs = ((z + shift) % ring) * 2 + at_core
+    shift, side = [0, 0, -1, 1], [0, 1, 0, 0]
+    for step in range(2, half):
+        shift += [1 - step, step - 1, -step, step]
+        side += [1, 1, 0, 0]
+    shift = jnp.array(shift + [1 - half, half - 1, half, half], jnp.int32)
+    side = jnp.array(side + [1, 1, 0, 1], jnp.int32)
+    pairs = ((z + shift) % ring) * 2 + (core ^ side)
     order = (pairs[:, None] + 2 * ring * (yh ^ jnp.arange(2, dtype=jnp.int32))[None, :]).reshape(-1)
     tile_ids = lax.dynamic_slice_in_dim(
         pulse_ids, lax.axis_index(ROW) * tiles_mine, tiles_mine, 0
@@ -253,27 +263,31 @@
     rates = pick(wavenum.reshape(blocks, block_pulses), order).reshape(-1)
     coarse, fine = twiddles(rates, ang_index * col_dev, col_dev)
 
+    tables = turns(coarse, fine, half)
+
     swap = [(0, 1), (1, 0)]
     ahead = [(i, (i + 1) % ring) for i in range(ring)]
     behind = [(i, (i - 1) % ring) for i in range(ring)]
     other = lax.ppermute(mine, "yh", swap)
     forward = backward = jnp.concatenate([mine, other], 0)
-    held = [forward]
-    for step in range(1, half + 1):
-        forward = lax.ppermute(forward, "z", ahead)
-        held.append(forward)
-        if step < half:
-            backward = lax.ppermute(backward, "z", behind)
-            held.append(backward)
-    arrays = []
-    for near in held:
-        arrays += [near, lax.ppermute(near, "core", swap)]
-    total = None
-    cuts = [0, 6, 10, 14, 16]
-    for first, last in zip(cuts, cuts[1:]):
-        scale = foot_len ** (-0.5) if last == len(arrays) else None
-        total = part(pairs, code, coarse, fine, arrays[first:last], total, first, scale)
-    return total
+    near = [forward]
+    far, total = [], None
+    for step in range(1, half):
+        arriving = lax.ppermute(forward, "z", ahead), lax.ppermute(backward, "z", behind)
+        far = [lax.ppermute(block, "core", swap) for block in near]
+        if step > 1:
+            total = part(pairs, code, tables[step - 2], blocks, total, 4 * (step - 2))
+            forward, backward, total = lax.optimization_barrier((*arriving, total))
+        else:
+            forward, backward = lax.optimization_barrier(arriving)
+        blocks = ([*near] if step == 1 else []) + far + [forward, backward]
+        near = [forward, backward]
+    opposite = lax.ppermute(forward, "z", ahead)
+    far = [lax.ppermute(block, "core", swap) for block in near]
+    total = part(pairs, code, tables[half - 2], blocks, total, 4 * (half - 2))
+    opposite, total = lax.optimization_barrier((opposite, total))
+    blocks = far + [opposite, lax.ppermute(opposite, "core", swap)]
+    return part(pairs, code, tables[half - 1], blocks, total, 4 * (half - 1), foot_len ** (-0.5))
 
 
 def solution(mesh):

time: 75.1 us -> 68.7 us (0.915)
  Pallas kernels: 26.7 us -> 21.7 us
  waiting for transfers between devices: 9.4 us -> 8.45 us
  local copies, waits for them, and re-layouts: 4.58 us -> 3.7 us
    pallas_call x3, Pallas kernels: 15.9 us -> 10.2 us  [part(): pl.pallas_call(functools.partial(part_kernel, first=first, n_blocks=len(b...]
    pallas_call x0 -> x1, Pallas kernels: none -> 2.01 us  [turns(): pl.pallas_call(turn_kernel, out_shape=[shape] * parts, in_specs=[VMEM] *...]
    pallas_call x1, Pallas kernels: 5.78 us -> 4.5 us  [part(): pl.pallas_call(functools.partial(last_kernel, first=first, n_blocks=len(b...]
    ppermute x15, waiting for transfers between devices: 3.9 us -> 2.63 us  [the longest x1 1.61 us: body(): opposite = lax.ppermute(forward, 'z', ahead)]
    unnamed x4 -> x5, local copies, waits for them, and re-layouts: 0.95 us -> 0.19 us
  transfers between devices with their start and end apart: 17 -> 17, of which waited for: 5 -> 4; matrix products, arithmetic and copies ran while one was open for 7% -> 8% of each run, Pallas kernels for 21% -> 18%
where the time goes in v3:
time: 68.7 us; the launch traced here: 68.4 us
  starting transfers between devices  30.2 us (44%)
  Pallas kernels  21.7 us (32%)
  waiting for transfers between devices  8.45 us (12%)
  other arithmetic  3.89 us (6%)
  local copies, waits for them, and re-layouts  3.7 us (5%)
    ppermute x3, starting transfers between devices, body(): lax.ppermute(backward, 'z', behind)  11.3 us
    pallas_call x3, Pallas kernels, part(): pl.pallas_call(functools.partial(part_kernel, first=first, n_blocks=len(b...  10.2 us
    ppermute x7, starting transfers between devices, body(): far = [lax.ppermute(block, 'core', swap) for block in near]  8.74 us
    all_to_all x1, starting transfers between devices, body(): lax.all_to_all(packed.reshape(n_rows, rows, LANES), ROW, 0, 0, tiled=True)  5.86 us
    pallas_call x1, Pallas kernels, pack(): pl.pallas_call(pack_kernel, out_shape=jax.ShapeDtypeStruct((tiles * per_b...  4.84 us
    pallas_call x1, Pallas kernels, part(): pl.pallas_call(functools.partial(last_kernel, first=first, n_blocks=len(b...  4.5 us
    all_to_all x1, waiting for transfers between devices, body(): lax.all_to_all(packed.reshape(n_rows, rows, LANES), ROW, 0, 0, tiled=True)  3.85 us
    ppermute x1, starting transfers between devices, body(): other = lax.ppermute(mine, 'yh', swap)  2.71 us
  transfers between devices with their start and end apart: 17, of which 4 were waited for; matrix products, arithmetic and copies ran while one was open for 8% of the time, Pallas kernels for 18%

profile of v3, /device:TPU:1, one launch (start us, length us, event | category | flops | bytes accessed | tf_op | source)
XLA Modules:
  0.0 68.4 jit_solution(14669975851214347245)
XLA Ops:
  0.0 1.2 %pad.5 = bf16[32,18,2,128]{3,2,1,0:T(2,128)(2,1)S(1)} pad(bf16[32,16,2,128]{3,2,1,0:T(2,128)(2,1)} %bitcast.15, bf16[]{:T(256)} %constant.139.clone.1), padding=0_0x1_1x0_0x0_0 | pad | bytes 557058 | tf_op jit(solution)/shard_map/jit(_pad)/pad | solution.py:48
  1.3 0.9 %and_add_fusion.word_ref = s32[64,16]{1,0:T(8,128)S(1)} fusion(s32[64,512]{1,0:T(8,128)} %param.9, s32[]{:T(128)S(6)} %select_n.103, s32[64,512]{1,0:T(8,128)} %param.10, s32[]{:T(128)S(6)} %mul.193, s32[]{:T(128)S(6)} %mul.192, s32[64]{0:T(128)S(1)} %fusion.20), kind=kLoop, calls=%fused_computation.29 | loop fusion | flops 15360 | bytes 12556 | tf_op jit(solution)/shard_map/add | solution.py:54
  2.2 4.8 %pack.1 = bf16[2048,128]{1,0:T(8,128)(2,1)} custom-call(s32[64,16]{1,0:T(8,128)S(1)} %and_add_fusion.word_ref, f32[1152,128]{1,0:T(8,128)S(1)} %convert.5.bins_ref), custom_call_target="tpu_custom_call" | custom-call | tf_op jit(solution)/shard_map/pack/pallas_call | solution.py:55
  7.0 5.9 %all-to-all-start = ((bf16[8,256,128]{2,1,0:T(8,128)(2,1)}), bf16[8,256,128]{2,1,0:T(8,128)(2,1)S(1)}, u32[]{:S(2)}, u32[]{:S(2)}) async-start(bf16[8,256,128]{2,1,0:T(8,128)(2,1)} %bitcast.6), calls=%async_computation | async-start | bytes 1048576 | tf_op jit(solution)/shard_map/all_to_all | solution.py:243
  12.9 0.7 %fusion.19.pair_ref = s32[16]{0:T(128)S(1)} fusion(s32[16]{0:T(128)} %constant.140.clone, s32[16]{0:T(128)} %constant.141.clone, s32[]{:T(128)S(6)} %axis_index.36, s32[]{:T(128)S(6)} %axis_index.33), kind=kLoop, calls=%fused_computation.51 | loop fusion | flops 240 | bytes 200 | tf_op jit(solution)/shard_map/add | solution.py:254
  13.9 0.7 %constant_dynamic-slice_fusion.1 = s32[8,512]{1,0:T(8,128)S(1)} fusion(s32[64,512]{1,0:T(8,128)} %param.9, s32[]{:T(128)S(6)} %select_n.94), kind=kLoop, calls=%fused_computation.46 | loop fusion | bytes 32772 | tf_op jit(solution)/shard_map/dynamic_slice | solution.py:256
  14.6 0.8 %broadcast_in_dim.41 = s32[32,32]{1,0:T(8,128)S(1)} reshape(s32[1024]{0:T(1024)} %param.12) | data formatting | bytes 8192 | tf_op jit(solution)/shard_map/jit(_where)/broadcast_in_dim | solution.py:210
  15.3 0.2 select_reduce_fusion
  15.8 0.2 copy.20
  15.9 0.6 fusion.12
  16.6 1.1 %fusion.4 = (f32[1,64,1024]{2,1,0:T(8,128)S(1)}, f32[1,64,1024]{2,1,0:T(8,128)S(1)}) fusion(s32[64]{0:T(128)S(1)} %get-tuple-element.38, s32[64]{0:T(128)S(1)} %get-tuple-element.37, s32[1024]{0:T(1024)S(1)} %mul.173), kind=kLoop, calls=%fused_computation.19 | loop fusion | flops 983040 | bytes 528896 | tf_op jit(solution)/shard_map/cos | solution.py:222
  17.7 3.8 %all-to-all-done.got_ref = bf16[8,256,128]{2,1,0:T(8,128)(2,1)S(1)} async-done(((bf16[8,256,128]{2,1,0:T(8,128)(2,1)}), bf16[8,256,128]{2,1,0:T(8,128)(2,1)S(1)}, u32[]{:S(2)}, u32[]{:S(2)}) %all-to-all-start) | async-done | bytes 524320 | tf_op jit(solution)/shard_map/all_to_all | solution.py:243
  21.6 0.2 focus.1
  21.8 2.7 %collective-permute-start = (bf16[256,128]{1,0:T(8,128)(2,1)S(1)}, bf16[256,128]{1,0:T(8,128)(2,1)S(1)}, u32[]{:S(2)}, u32[]{:S(2)}) collective-permute-start(bf16[256,128]{1,0:T(8,128)(2,1)S(1)} %focus.1), channel_id=1, source_target_pairs={{0,128},{128,0},{1,129},{129,1},{2,130},{130,2},{3,131},{131,3},{4... | collective-permute-start | bytes 196616 | tf_op jit(solution)/shard_map/ppermute | solution.py:271
  24.5 2.0 %collective-permute-done = bf16[256,128]{1,0:T(8,128)(2,1)S(1)} collective-permute-done((bf16[256,128]{1,0:T(8,128)(2,1)S(1)}, bf16[256,128]{1,0:T(8,128)(2,1)S(1)}, u32[]{:S(2)}, u32[]{:S(2)}) %collective-permute-start) | collective-permute-done | bytes 65568 | tf_op jit(solution)/shard_map/ppermute | solution.py:271
  26.5 5.7 %collective-permute-start.2 = (bf16[512,128]{1,0:T(8,128)(2,1)S(1)}, bf16[512,128]{1,0:T(8,128)(2,1)S(1)}, u32[]{:S(2)}, u32[]{:S(2)}) collective-permute-start(bf16[512,128]{1,0:T(8,128)(2,1)S(1)} %pad_maximum_fusion.2.refs_0_), channel_id=1, source_target_pairs={{0,112},{16,0},{32,16},{48,32},{64,48},{80,64},{96,80},{112,96},{1... | collective-permute-start | bytes 393224 | tf_op jit(solution)/shard_map/ppermute | solution.py:276
  32.4 0.1 copy.18
  32.5 0.2 broadcast_in_dim.44.coarse_ref
  32.8 2.0 %turns.1 = (bf16[2048,512]{1,0:T(8,128)(2,1)S(1)}, bf16[2048,512]{1,0:T(8,128)(2,1)S(1)}, bf16[2048,512]{1,0:T(8,128)(2,1)S(1)}, bf16[2048,512]{1,0:T(8,128)(2,1)S(1)}) custom-call(f32[2,32,1,1024]{3,2,1,0:T(1,128)S(1)} %broadcast_in_dim.44.coarse_ref, f32[2,64,1024]{2,1,0:T(8,128)S(1)} %pad_maximum_fusion.fine_ref), custom_call_target="tpu_custom_call" | custom-call | tf_op jit(solution)/shard_map/turns/pallas_call | solution.py:133
  34.8 3.2 %collective-permute-start.5 = (bf16[512,128]{1,0:T(8,128)(2,1)S(1)}, bf16[512,128]{1,0:T(8,128)(2,1)S(1)}, u32[]{:S(2)}, u32[]{:S(2)}) collective-permute-start(bf16[512,128]{1,0:T(8,128)(2,1)S(1)} %pad_maximum_fusion.2.refs_0_), channel_id=1, source_target_pairs={{0,8},{8,0},{1,9},{9,1},{2,10},{10,2},{3,11},{11,3},{4,12},{12,4},... | collective-permute-start | bytes 393224 | tf_op jit(solution)/shard_map/ppermute | solution.py:277
  38.1 3.0 %collective-permute-start.4 = (bf16[512,128]{1,0:T(8,128)(2,1)S(1)}, bf16[512,128]{1,0:T(8,128)(2,1)S(1)}, u32[]{:S(2)}, u32[]{:S(2)}) collective-permute-start(bf16[512,128]{1,0:T(8,128)(2,1)S(1)} %collective-permute-done.2.refs_3_), channel_id=1, source_target_pairs={{0,112},{16,0},{32,16},{48,32},{64,48},{80,64},{96,80},{112,96},{1... | collective-permute-start | bytes 393224 | tf_op jit(solution)/shard_map/ppermute | solution.py:276
  41.1 3.7 %collective-permute-start.8 = (bf16[512,128]{1,0:T(8,128)(2,1)S(1)}, bf16[512,128]{1,0:T(8,128)(2,1)S(1)}, u32[]{:S(2)}, u32[]{:S(2)}) collective-permute-start(bf16[512,128]{1,0:T(8,128)(2,1)S(1)} %collective-permute-done.1.refs_2_), channel_id=1, source_target_pairs={{0,8},{8,0},{1,9},{9,1},{2,10},{10,2},{3,11},{11,3},{4,12},{12,4},... | collective-permute-start | bytes 393224 | tf_op jit(solution)/shard_map/ppermute | solution.py:277
  45.0 3.3 %part.3.refs_4_ = f32[2048,1024]{1,0:T(8,128)S(1)} custom-call(s32[16]{0:T(128)S(1)} %fusion.19.pair_ref, s32[8,16,1,64]{3,2,1,0:T(1,128)S(1)} %broadcast_add_fusion.code_ref, bf16[2048,512]{1,0:T(8,128)(2,1)S(1)} %get-tuple-element.22.turn_ref, bf16[512,128]{1,0:T(8,128)(2,1)S(1)} %pad_maximum_fusion.2.refs_0_, ...), custom_call_target="tpu_custom_call" | custom-call | tf_op jit(solution)/shard_map/part/pallas_call | solution.py:183
  48.4 2.7 %collective-permute-start.7 = (bf16[512,128]{1,0:T(8,128)(2,1)S(1)}, bf16[512,128]{1,0:T(8,128)(2,1)S(1)}, u32[]{:S(2)}, u32[]{:S(2)}) collective-permute-start(bf16[512,128]{1,0:T(8,128)(2,1)S(1)} %collective-permute-done.4.refs_3_), channel_id=1, source_target_pairs={{0,112},{16,0},{32,16},{48,32},{64,48},{80,64},{96,80},{112,96},{1... | collective-permute-start | bytes 393224 | tf_op jit(solution)/shard_map/ppermute | solution.py:276
  51.0 1.0 %collective-permute-start.13 = (bf16[512,128]{1,0:T(8,128)(2,1)S(1)}, bf16[512,128]{1,0:T(8,128)(2,1)S(1)}, u32[]{:S(2)}, u32[]{:S(2)}) collective-permute-start(bf16[512,128]{1,0:T(8,128)(2,1)S(1)} %collective-permute-done.3.refs_2_), channel_id=1, source_target_pairs={{0,8},{8,0},{1,9},{9,1},{2,10},{10,2},{3,11},{11,3},{4,12},{12,4},... | collective-permute-start | bytes 393224 | tf_op jit(solution)/shard_map/ppermute | solution.py:277
  52.0 3.5 %part.4.refs_4_ = f32[2048,1024]{1,0:T(8,128)S(1)} custom-call(s32[16]{0:T(128)S(1)} %fusion.19.pair_ref, s32[8,16,1,64]{3,2,1,0:T(1,128)S(1)} %broadcast_add_fusion.code_ref, bf16[2048,512]{1,0:T(8,128)(2,1)S(1)} %get-tuple-element.25.turn_ref, bf16[512,128]{1,0:T(8,128)(2,1)S(1)} %collective-permute-done.8.refs_0_, ...), custom_call_target="tpu_custom_call", output_to_operand_aliasing={{}: (7, {})} | custom-call | tf_op jit(solution)/shard_map/part/pallas_call | solution.py:183
  55.6 0.6 collective-permute-start.10
  56.3 3.4 %part.5.refs_4_ = f32[2048,1024]{1,0:T(8,128)S(1)} custom-call(s32[16]{0:T(128)S(1)} %fusion.19.pair_ref, s32[8,16,1,64]{3,2,1,0:T(1,128)S(1)} %broadcast_add_fusion.code_ref, bf16[2048,512]{1,0:T(8,128)(2,1)S(1)} %get-tuple-element.29.turn_ref, bf16[512,128]{1,0:T(8,128)(2,1)S(1)} %collective-permute-done.13.refs_0_, ...), custom_call_target="tpu_custom_call", output_to_operand_aliasing={{}: (7, {})} | custom-call | tf_op jit(solution)/shard_map/part/pallas_call | solution.py:183
  59.8 1.6 %collective-permute-done.12.refs_2_ = bf16[512,128]{1,0:T(8,128)(2,1)S(1)} collective-permute-done((bf16[512,128]{1,0:T(8,128)(2,1)S(1)}, bf16[512,128]{1,0:T(8,128)(2,1)S(1)}, u32[]{:S(2)}, u32[]{:S(2)}) %collective-permute-start.12) | collective-permute-done | bytes 131104 | tf_op jit(solution)/shard_map/ppermute | solution.py:285
  61.4 1.4 %collective-permute-start.15 = (bf16[512,128]{1,0:T(8,128)(2,1)S(1)}, bf16[512,128]{1,0:T(8,128)(2,1)S(1)}, u32[]{:S(2)}, u32[]{:S(2)}) collective-permute-start(bf16[512,128]{1,0:T(8,128)(2,1)S(1)} %collective-permute-done.12.refs_2_), channel_id=1, source_target_pairs={{0,8},{8,0},{1,9},{9,1},{2,10},{10,2},{3,11},{11,3},{4,12},{12,4},... | collective-permute-start | bytes 393224 | tf_op jit(solution)/shard_map/ppermute | solution.py:289
  62.7 1.0 %collective-permute-done.15.refs_3_ = bf16[512,128]{1,0:T(8,128)(2,1)S(1)} collective-permute-done((bf16[512,128]{1,0:T(8,128)(2,1)S(1)}, bf16[512,128]{1,0:T(8,128)(2,1)S(1)}, u32[]{:S(2)}, u32[]{:S(2)}) %collective-permute-start.15) | collective-permute-done | bytes 131104 | tf_op jit(solution)/shard_map/ppermute | solution.py:289
  63.7 4.5 %last.1 = bf16[1024,2,1024]{2,1,0:T(2,128)(2,1)} custom-call(s32[16]{0:T(128)S(1)} %fusion.19.pair_ref, s32[8,16,1,64]{3,2,1,0:T(1,128)S(1)} %broadcast_add_fusion.code_ref, bf16[2048,512]{1,0:T(8,128)(2,1)S(1)} %get-tuple-element.19.turn_ref, bf16[512,128]{1,0:T(8,128)(2,1)S(1)} %collective-permute-done.10.refs_0_, ...), custom_call_target="tpu_custom_call" | custom-call | tf_op jit(solution)/shard_map/last/pallas_call | solution.py:196
  (45 shorter events, 1.3 us)
Async XLA Ops:
  0.0 1.3 %copy-start = (s32[64,32]{0,1:T(8,128)S(1)}, s32[64,32]{0,1:T(8,128)}, u32[]{:S(2)}) copy-start(s32[64,32]{0,1:T(8,128)} %param.11) | copy-start | bytes 24580
  0.0 15.7 %copy-start.1 = (bf16[8,128,128]{2,1,0:T(8,128)(2,1)S(1)}, bf16[8,128,128]{2,1,0:T(8,128)(2,1)}, u32[]{:S(2)}) copy-start(bf16[8,128,128]{2,1,0:T(8,128)(2,1)} %param.13) | copy-start | bytes 786436
  7.0 14.6 %all-to-all-start = ((bf16[8,256,128]{2,1,0:T(8,128)(2,1)}), bf16[8,256,128]{2,1,0:T(8,128)(2,1)S(1)}, u32[]{:S(2)}, u32[]{:S(2)}) async-start(bf16[8,256,128]{2,1,0:T(8,128)(2,1)} %bitcast.6), calls=%async_computation | async-start | bytes 1048576 | tf_op jit(solution)/shard_map/all_to_all | solution.py:243
  21.8 4.7 %collective-permute-start = (bf16[256,128]{1,0:T(8,128)(2,1)S(1)}, bf16[256,128]{1,0:T(8,128)(2,1)S(1)}, u32[]{:S(2)}, u32[]{:S(2)}) collective-permute-start(bf16[256,128]{1,0:T(8,128)(2,1)S(1)} %focus.1), channel_id=1, source_target_pairs={{0,128},{128,0},{1,129},{129,1},{2,130},{130,2},{3,131},{131,3},{4... | collective-permute-start | bytes 196616 | tf_op jit(solution)/shard_map/ppermute | solution.py:271
  26.5 11.6 %collective-permute-start.2 = (bf16[512,128]{1,0:T(8,128)(2,1)S(1)}, bf16[512,128]{1,0:T(8,128)(2,1)S(1)}, u32[]{:S(2)}, u32[]{:S(2)}) collective-permute-start(bf16[512,128]{1,0:T(8,128)(2,1)S(1)} %pad_maximum_fusion.2.refs_0_), channel_id=1, source_target_pairs={{0,112},{16,0},{32,16},{48,32},{64,48},{80,64},{96,80},{112,96},{1... | collective-permute-start | bytes 393224 | tf_op jit(solution)/shard_map/ppermute | solution.py:276
  32.1 5.9 %collective-permute-start.1 = (bf16[512,128]{1,0:T(8,128)(2,1)S(1)}, bf16[512,128]{1,0:T(8,128)(2,1)S(1)}, u32[]{:S(2)}, u32[]{:S(2)}) collective-permute-start(bf16[512,128]{1,0:T(8,128)(2,1)S(1)} %pad_maximum_fusion.2.refs_0_), channel_id=1, source_target_pairs={{0,16},{16,32},{32,48},{48,64},{64,80},{80,96},{96,112},{112,0},{1... | collective-permute-start | bytes 393224 | tf_op jit(solution)/shard_map/ppermute | solution.py:276
  34.8 10.2 %collective-permute-start.5 = (bf16[512,128]{1,0:T(8,128)(2,1)S(1)}, bf16[512,128]{1,0:T(8,128)(2,1)S(1)}, u32[]{:S(2)}, u32[]{:S(2)}) collective-permute-start(bf16[512,128]{1,0:T(8,128)(2,1)S(1)} %pad_maximum_fusion.2.refs_0_), channel_id=1, source_target_pairs={{0,8},{8,0},{1,9},{9,1},{2,10},{10,2},{3,11},{11,3},{4,12},{12,4},... | collective-permute-start | bytes 393224 | tf_op jit(solution)/shard_map/ppermute | solution.py:277
  38.0 10.2 %collective-permute-start.3 = (bf16[512,128]{1,0:T(8,128)(2,1)S(1)}, bf16[512,128]{1,0:T(8,128)(2,1)S(1)}, u32[]{:S(2)}, u32[]{:S(2)}) collective-permute-start(bf16[512,128]{1,0:T(8,128)(2,1)S(1)} %collective-permute-done.1.refs_2_), channel_id=1, source_target_pairs={{0,16},{16,32},{32,48},{48,64},{64,80},{80,96},{96,112},{112,0},{1... | collective-permute-start | bytes 393224 | tf_op jit(solution)/shard_map/ppermute | solution.py:276
  38.1 10.2 %collective-permute-start.4 = (bf16[512,128]{1,0:T(8,128)(2,1)S(1)}, bf16[512,128]{1,0:T(8,128)(2,1)S(1)}, u32[]{:S(2)}, u32[]{:S(2)}) collective-permute-start(bf16[512,128]{1,0:T(8,128)(2,1)S(1)} %collective-permute-done.2.refs_3_), channel_id=1, source_target_pairs={{0,112},{16,0},{32,16},{48,32},{64,48},{80,64},{96,80},{112,96},{1... | collective-permute-start | bytes 393224 | tf_op jit(solution)/shard_map/ppermute | solution.py:276
  41.1 10.9 %collective-permute-start.8 = (bf16[512,128]{1,0:T(8,128)(2,1)S(1)}, bf16[512,128]{1,0:T(8,128)(2,1)S(1)}, u32[]{:S(2)}, u32[]{:S(2)}) collective-permute-start(bf16[512,128]{1,0:T(8,128)(2,1)S(1)} %collective-permute-done.1.refs_2_), channel_id=1, source_target_pairs={{0,8},{8,0},{1,9},{9,1},{2,10},{10,2},{3,11},{11,3},{4,12},{12,4},... | collective-permute-start | bytes 393224 | tf_op jit(solution)/shard_map/ppermute | solution.py:277
  44.9 7.1 %collective-permute-start.9 = (bf16[512,128]{1,0:T(8,128)(2,1)S(1)}, bf16[512,128]{1,0:T(8,128)(2,1)S(1)}, u32[]{:S(2)}, u32[]{:S(2)}) collective-permute-start(bf16[512,128]{1,0:T(8,128)(2,1)S(1)} %collective-permute-done.2.refs_3_), channel_id=1, source_target_pairs={{0,8},{8,0},{1,9},{9,1},{2,10},{10,2},{3,11},{11,3},{4,12},{12,4},... | collective-permute-start | bytes 393224 | tf_op jit(solution)/shard_map/ppermute | solution.py:277
  48.3 7.2 %collective-permute-start.6 = (bf16[512,128]{1,0:T(8,128)(2,1)S(1)}, bf16[512,128]{1,0:T(8,128)(2,1)S(1)}, u32[]{:S(2)}, u32[]{:S(2)}) collective-permute-start(bf16[512,128]{1,0:T(8,128)(2,1)S(1)} %collective-permute-done.3.refs_2_), channel_id=1, source_target_pairs={{0,16},{16,32},{32,48},{48,64},{64,80},{80,96},{96,112},{112,0},{1... | collective-permute-start | bytes 393224 | tf_op jit(solution)/shard_map/ppermute | solution.py:276
  48.4 7.2 %collective-permute-start.7 = (bf16[512,128]{1,0:T(8,128)(2,1)S(1)}, bf16[512,128]{1,0:T(8,128)(2,1)S(1)}, u32[]{:S(2)}, u32[]{:S(2)}) collective-permute-start(bf16[512,128]{1,0:T(8,128)(2,1)S(1)} %collective-permute-done.4.refs_3_), channel_id=1, source_target_pairs={{0,112},{16,0},{32,16},{48,32},{64,48},{80,64},{96,80},{112,96},{1... | collective-permute-start | bytes 393224 | tf_op jit(solution)/shard_map/ppermute | solution.py:276
  51.0 5.3 %collective-permute-start.13 = (bf16[512,128]{1,0:T(8,128)(2,1)S(1)}, bf16[512,128]{1,0:T(8,128)(2,1)S(1)}, u32[]{:S(2)}, u32[]{:S(2)}) collective-permute-start(bf16[512,128]{1,0:T(8,128)(2,1)S(1)} %collective-permute-done.3.refs_2_), channel_id=1, source_target_pairs={{0,8},{8,0},{1,9},{9,1},{2,10},{10,2},{3,11},{11,3},{4,12},{12,4},... | collective-permute-start | bytes 393224 | tf_op jit(solution)/shard_map/ppermute | solution.py:277
  52.0 4.3 %collective-permute-start.14 = (bf16[512,128]{1,0:T(8,128)(2,1)S(1)}, bf16[512,128]{1,0:T(8,128)(2,1)S(1)}, u32[]{:S(2)}, u32[]{:S(2)}) collective-permute-start(bf16[512,128]{1,0:T(8,128)(2,1)S(1)} %collective-permute-done.4.refs_3_), channel_id=1, source_target_pairs={{0,8},{8,0},{1,9},{9,1},{2,10},{10,2},{3,11},{11,3},{4,12},{12,4},... | collective-permute-start | bytes 393224 | tf_op jit(solution)/shard_map/ppermute | solution.py:277
  55.5 5.8 %collective-permute-start.12 = (bf16[512,128]{1,0:T(8,128)(2,1)S(1)}, bf16[512,128]{1,0:T(8,128)(2,1)S(1)}, u32[]{:S(2)}, u32[]{:S(2)}) collective-permute-start(bf16[512,128]{1,0:T(8,128)(2,1)S(1)} %collective-permute-done.6.refs_2_), channel_id=1, source_target_pairs={{0,16},{16,32},{32,48},{48,64},{64,80},{80,96},{96,112},{112,0},{1... | collective-permute-start | bytes 393224 | tf_op jit(solution)/shard_map/ppermute | solution.py:285
  55.6 7.1 %collective-permute-start.10 = (bf16[512,128]{1,0:T(8,128)(2,1)S(1)}, bf16[512,128]{1,0:T(8,128)(2,1)S(1)}, u32[]{:S(2)}, u32[]{:S(2)}) collective-permute-start(bf16[512,128]{1,0:T(8,128)(2,1)S(1)} %collective-permute-done.6.refs_2_), channel_id=1, source_target_pairs={{0,8},{8,0},{1,9},{9,1},{2,10},{10,2},{3,11},{11,3},{4,12},{12,4},... | collective-permute-start | bytes 393224 | tf_op jit(solution)/shard_map/ppermute | solution.py:286
  56.2 6.5 %collective-permute-start.11 = (bf16[512,128]{1,0:T(8,128)(2,1)S(1)}, bf16[512,128]{1,0:T(8,128)(2,1)S(1)}, u32[]{:S(2)}, u32[]{:S(2)}) collective-permute-start(bf16[512,128]{1,0:T(8,128)(2,1)S(1)} %collective-permute-done.7.refs_3_), channel_id=1, source_target_pairs={{0,8},{8,0},{1,9},{9,1},{2,10},{10,2},{3,11},{11,3},{4,12},{12,4},... | collective-permute-start | bytes 393224 | tf_op jit(solution)/shard_map/ppermute | solution.py:286
  61.4 2.3 %collective-permute-start.15 = (bf16[512,128]{1,0:T(8,128)(2,1)S(1)}, bf16[512,128]{1,0:T(8,128)(2,1)S(1)}, u32[]{:S(2)}, u32[]{:S(2)}) collective-permute-start(bf16[512,128]{1,0:T(8,128)(2,1)S(1)} %collective-permute-done.12.refs_2_), channel_id=1, source_target_pairs={{0,8},{8,0},{1,9},{9,1},{2,10},{10,2},{3,11},{11,3},{4,12},{12,4},... | collective-permute-start | bytes 393224 | tf_op jit(solution)/shard_map/ppermute | solution.py:289

commit v4 on v3

--- a/solution.py
+++ b/solution.py
@@ -18,7 +18,6 @@
 SMEM = pl.BlockSpec(memory_space=pltpu.SMEM)
 VMEM = pl.BlockSpec(memory_space=pltpu.VMEM)
 
-
 def pack_kernel(word_ref, bins_ref, out_ref, cut_sc):
     tiles, per_block = word_ref.shape
     lane = lax.broadcasted_iota(jnp.int32, (2, LANES), 1)
@@ -31,14 +30,14 @@
                 row = pl.multiple_of(word >> 7, 2)
                 low = bins_ref[pl.ds(row, 2), :]
                 high = bins_ref[pl.ds(pl.multiple_of(row + 2, 2), 2), :]
-                cut = jnp.where(lane >= (word & (LANES - 1)), low, high)
                 at = ((step * at_once + u) * per_block + entry) * 2
-                cut_sc[pl.ds(pl.multiple_of(at, 2), 2), :] = pltpu.roll(cut, (-word) & (LANES - 1), 1)
+                cut_sc[pl.ds(pl.multiple_of(at, 2), 2), :] = jnp.where(
+                    lane >= (word & (LANES - 1)), low, high
+                )
         return 0
 
     lax.fori_loop(0, tiles // at_once, take, 0)
     out_ref[...] = cut_sc[...].astype(jnp.bfloat16)
-
 
 def pack(echoes, ids, starts, live):
     pulses, parts, bins = echoes.shape
@@ -62,32 +61,35 @@
         name="pack",
     )(word, rows)
 
-
-def focus_kernel(got_ref, turned_ref, out_ref):
-    tiles = turned_ref.shape[0]
+def focus_kernel(back_ref, got_ref, turned_ref, out_ref, panels):
+    tiles, per_block = back_ref.shape
     rows = out_ref.shape[0] // tiles
-    panels = got_ref[0].astype(jnp.float32)
+    total = got_ref[0].astype(jnp.float32)
     for source in range(1, got_ref.shape[0]):
-        panels += got_ref[source].astype(jnp.float32)
-    panels = panels.astype(jnp.bfloat16)
+        total += got_ref[source].astype(jnp.float32)
+    panels[...] = total
     for tile in range(tiles):
-        out_ref[tile * rows : (tile + 1) * rows, :] = lax.dot_general(
-            panels[tile * rows : (tile + 1) * rows, :],
+        windows = []
+        for entry in range(per_block):
+            at = tile * rows + entry * 2
+            windows.append(pltpu.roll(panels[at : at + 2, :], back_ref[tile, entry], 1))
+        out_ref[tile * rows : (tile + 1) * rows, :] = jnp.dot(
+            jnp.concatenate(windows, 0).astype(jnp.bfloat16),
             turned_ref[tile],
-            (((1,), (0,)), ((), ())),
             preferred_element_type=jnp.float32,
         ).astype(jnp.bfloat16)
 
 
-def focus(got, turned):
+def focus(back, got, turned):
     return pl.pallas_call(
         focus_kernel,
         out_shape=jax.ShapeDtypeStruct(got.shape[1:], jnp.bfloat16),
-        in_specs=[VMEM] * 2,
+        in_specs=[SMEM, VMEM, VMEM],
         out_specs=VMEM,
+        scratch_shapes=[pltpu.VMEM(got.shape[1:], jnp.float32)],
         compiler_params=pltpu.CompilerParams(vmem_limit_bytes=4 << 20),
         name="focus",
-    )(got, turned)
+    )(back, got, turned)
 
 
 def place(pair_ref, code_ref, blocks, first, spread):
@@ -109,7 +111,6 @@
             spread[number * slots : (number + 1) * slots, columns] = placed[:slots]
             spread[half + number * slots : half + (number + 1) * slots, columns] = placed[slots:]
 
-
 def turn_kernel(coarse_ref, fine_ref, *out_refs):
     pulses = coarse_ref.shape[3] // len(out_refs)
     rows = fine_ref.shape[1]
@@ -126,7 +127,6 @@
 
     lax.fori_loop(0, coarse_ref.shape[1], step, 0, unroll=4)
 
-
 def turns(coarse, fine, parts):
     rows = coarse.shape[1] * fine.shape[1]
     shape = jax.ShapeDtypeStruct((rows, 2 * coarse.shape[3] // parts), jnp.bfloat16)
@@ -135,10 +135,9 @@
         out_shape=[shape] * parts,
         in_specs=[VMEM] * 2,
         out_specs=[VMEM] * parts,
-        compiler_params=pltpu.CompilerParams(vmem_limit_bytes=24 << 20),
+        compiler_params=pltpu.CompilerParams(vmem_limit_bytes=2 << 20),
         name="turns",
     )(coarse, fine)
-
 
 def part_kernel(pair_ref, code_ref, turn_ref, *refs, first, n_blocks, more):
     blocks, rest = refs[:n_blocks], refs[n_blocks:]
@@ -149,7 +148,6 @@
         here = slice(start, start + rows)
         new = jnp.dot(turn_ref[here, :], spread[...], preferred_element_type=jnp.float32)
         total_ref[here, :] = rest[0][here, :] + new if more else new
-
 
 def last_kernel(pair_ref, code_ref, turn_ref, *refs, first, n_blocks, scale):
     blocks, (held_ref, out_ref, spread, ready, sems) = refs[:n_blocks], refs[n_blocks:]
@@ -170,7 +168,6 @@
     for copy in sent:
         copy.wait()
 
-
 def part(pairs, code, turn, blocks, held, first, scale=None):
     tiles = code.shape[0]
     rows, depth = turn.shape
@@ -178,7 +175,7 @@
     operands = (pairs, code, turn, *blocks) + (() if held is None else (held,))
     specs = [SMEM] + [VMEM] * (len(operands) - 1)
     scratch = [pltpu.VMEM((depth, n), jnp.bfloat16)]
-    params = pltpu.CompilerParams(vmem_limit_bytes=24 << 20)
+    params = pltpu.CompilerParams(vmem_limit_bytes=(6 if scale is None else 10) << 20)
     if scale is None:
         return pl.pallas_call(
             functools.partial(
@@ -204,11 +201,9 @@
         name="last",
     )(*operands)
 
-
 def pick(table, index):
     hot = index[:, None] == jnp.arange(table.shape[0], dtype=jnp.int32)[None, :]
     return jnp.sum(jnp.where(hot[:, :, None], table[None], 0), axis=1)
-
 
 def twiddles(rates, first_column, columns):
     step_angle = 2.0 * math.pi / COLS
@@ -222,7 +217,6 @@
         jnp.stack([jnp.cos(within), jnp.sin(within)]),
     )
 
-
 def body(echoes, pulse_ids, bin_start, live_count, wavenum, interp):
     blocks = lax.axis_size(ANG)
     ang_index = lax.axis_index(ANG)
@@ -241,7 +235,9 @@
     packed = pack(echoes, my_ids - ang_index * block_pulses, my_starts, my_live)
     rows = packed.shape[0] // n_rows
     got = lax.all_to_all(packed.reshape(n_rows, rows, LANES), ROW, 0, 0, tiled=True)
-    mine = focus(got, interp.swapaxes(1, 2))
+    my_tiles = lax.axis_index(ROW) * tiles_mine
+    back = (-lax.dynamic_slice(bin_start, (my_tiles, first_entry), (tiles_mine, per_block))) & (LANES - 1)
+    mine = focus(back, got, interp.swapaxes(1, 2))
 
     yh, z, core = (lax.axis_index(name) for name in ANG)
     half = ring // 2
@@ -254,7 +250,7 @@
     pairs = ((z + shift) % ring) * 2 + (core ^ side)
     order = (pairs[:, None] + 2 * ring * (yh ^ jnp.arange(2, dtype=jnp.int32))[None, :]).reshape(-1)
     tile_ids = lax.dynamic_slice_in_dim(
-        pulse_ids, lax.axis_index(ROW) * tiles_mine, tiles_mine, 0
+        pulse_ids, my_tiles, tiles_mine, 0
     ).reshape(tiles_mine, 2, 2 * ring, per_block)
     tile_ids = jnp.where(yh == 0, tile_ids, tile_ids[:, ::-1]) % block_pulses
     tile_ids = tile_ids + block_pulses * jnp.arange(2, dtype=jnp.int32)[None, :, None, None]
@@ -269,16 +265,19 @@
     ahead = [(i, (i + 1) % ring) for i in range(ring)]
     behind = [(i, (i - 1) % ring) for i in range(ring)]
     other = lax.ppermute(mine, "yh", swap)
+
     forward = backward = jnp.concatenate([mine, other], 0)
     near = [forward]
     far, total = [], None
     for step in range(1, half):
         arriving = lax.ppermute(forward, "z", ahead), lax.ppermute(backward, "z", behind)
-        far = [lax.ppermute(block, "core", swap) for block in near]
         if step > 1:
             total = part(pairs, code, tables[step - 2], blocks, total, 4 * (step - 2))
+            *leaving, total = lax.optimization_barrier((*near, total))
+            far = [lax.ppermute(block, "core", swap) for block in leaving]
             forward, backward, total = lax.optimization_barrier((*arriving, total))
         else:
+            far = [lax.ppermute(block, "core", swap) for block in near]
             forward, backward = lax.optimization_barrier(arriving)
         blocks = ([*near] if step == 1 else []) + far + [forward, backward]
         near = [forward, backward]
@@ -289,7 +288,6 @@
     blocks = far + [opposite, lax.ppermute(opposite, "core", swap)]
     return part(pairs, code, tables[half - 1], blocks, total, 4 * (half - 1), foot_len ** (-0.5))
 
-
 def solution(mesh):
     finer = Mesh(mesh.devices.reshape(2, -1, 2, 4, 2), FINE)
     return jax.shard_map(

time: 68.7 us -> 65 us (0.946)
  starting transfers between devices: 30.2 us -> 28.2 us
  waiting for transfers between devices: 8.45 us -> 6.89 us
    ppermute x7 -> x3, starting transfers between devices: 8.74 us -> 4.78 us  [body(): far = [lax.ppermute(block, 'core', swap) for block in near]]
    ppermute x3, starting transfers between devices: 11.3 us -> 9.38 us  [body(): lax.ppermute(backward, 'z', behind)]
    ppermute x0 -> x4, starting transfers between devices: none -> 1.86 us  [body(): far = [lax.ppermute(block, 'core', swap) for block in leaving]]
    ppermute x3, starting transfers between devices: 0.09 us -> 1.91 us  [body(): lax.ppermute(forward, 'z', ahead)]
    pallas_call x1, Pallas kernels: 4.84 us -> 3.44 us  [pack(): pl.pallas_call(pack_kernel, out_shape=jax.ShapeDtypeStruct((tiles * per_b...]
    ppermute x1, waiting for transfers between devices: 1.61 us -> 0.4 us  [body(): opposite = lax.ppermute(forward, 'z', ahead)]
    unnamed x5 -> x9, local copies, waits for them, and re-layouts: 0.19 us -> 1.13 us
    and x0 -> x1, other arithmetic: none -> 0.77 us  [body(): -lax.dynamic_slice(bin_start, (my_tiles, first_entry), (tiles_mine, per_b...]
  transfers between devices with their start and end apart: 17 -> 17, of which waited for: 4 -> 4; matrix products, arithmetic and copies ran while one was open for 8% -> 9% of each run, Pallas kernels for 18% -> 19%
where the time goes in v4:
time: 65 us; the launch traced here: 64.7 us
  starting transfers between devices  28.2 us (43%)
  Pallas kernels  21.3 us (33%)
  waiting for transfers between devices  6.89 us (11%)
  other arithmetic  3.99 us (6%)
  local copies, waits for them, and re-layouts  3.93 us (6%)
    pallas_call x3, Pallas kernels, part(): pl.pallas_call(functools.partial(part_kernel, first=first, n_blocks=len(b...  10.3 us
    ppermute x3, starting transfers between devices, body(): lax.ppermute(backward, 'z', behind)  9.38 us
    all_to_all x1, starting transfers between devices, body(): lax.all_to_all(packed.reshape(n_rows, rows, LANES), ROW, 0, 0, tiled=True)  5.86 us
    ppermute x3, starting transfers between devices, body(): far = [lax.ppermute(block, 'core', swap) for block in near]  4.78 us
    pallas_call x1, Pallas kernels, part(): pl.pallas_call(functools.partial(last_kernel, first=first, n_blocks=len(b...  4.57 us
    all_to_all x1, waiting for transfers between devices, body(): lax.all_to_all(packed.reshape(n_rows, rows, LANES), ROW, 0, 0, tiled=True)  3.5 us
    pallas_call x1, Pallas kernels, pack(): pl.pallas_call(pack_kernel, out_shape=jax.ShapeDtypeStruct((tiles * per_b...  3.44 us
    ppermute x1, starting transfers between devices, body(): other = lax.ppermute(mine, 'yh', swap)  2.7 us
  transfers between devices with their start and end apart: 17, of which 4 were waited for; matrix products, arithmetic and copies ran while one was open for 9% of the time, Pallas kernels for 19%

profile of v4, /device:TPU:1, one launch (start us, length us, event | category | flops | bytes accessed | tf_op | source)
XLA Modules:
  0.0 64.7 jit_solution(9680984820332158137)
XLA Ops:
  0.0 1.2 %pad.5 = bf16[32,18,2,128]{3,2,1,0:T(2,128)(2,1)S(1)} pad(bf16[32,16,2,128]{3,2,1,0:T(2,128)(2,1)} %bitcast.15, bf16[]{:T(256)} %constant.140.clone.1), padding=0_0x1_1x0_0x0_0 | pad | bytes 557058 | tf_op jit(solution)/shard_map/jit(_pad)/pad | solution.py:47
  1.3 0.9 %and_add_fusion.word_ref = s32[64,16]{1,0:T(8,128)S(1)} fusion(s32[64,512]{1,0:T(8,128)} %param.9, s32[]{:T(128)S(6)} %select_n.104, s32[64,512]{1,0:T(8,128)} %param.10, s32[]{:T(128)S(6)} %mul.193, s32[]{:T(128)S(6)} %mul.192, s32[64]{0:T(128)S(1)} %fusion.20), kind=kLoop, calls=%fused_computation.29 | loop fusion | flops 15360 | bytes 12556 | tf_op jit(solution)/shard_map/add | solution.py:53
  2.2 3.4 %pack.1 = bf16[2048,128]{1,0:T(8,128)(2,1)} custom-call(s32[64,16]{1,0:T(8,128)S(1)} %and_add_fusion.word_ref, f32[1152,128]{1,0:T(8,128)S(1)} %convert.5.bins_ref), custom_call_target="tpu_custom_call" | custom-call | tf_op jit(solution)/shard_map/pack/pallas_call | solution.py:54
  5.6 5.9 %all-to-all-start = ((bf16[8,256,128]{2,1,0:T(8,128)(2,1)}), bf16[8,256,128]{2,1,0:T(8,128)(2,1)S(1)}, u32[]{:S(2)}, u32[]{:S(2)}) async-start(bf16[8,256,128]{2,1,0:T(8,128)(2,1)} %bitcast.6), calls=%async_computation | async-start | bytes 1048576 | tf_op jit(solution)/shard_map/all_to_all | solution.py:237
  11.5 0.8 %negate_and_fusion.back_ref = s32[8,16]{1,0:T(8,128)S(1)} fusion(s32[64,512]{1,0:T(8,128)} %param.10, s32[]{:T(128)S(6)} %select_n.96, s32[]{:T(128)S(6)} %select_n.104), kind=kLoop, calls=%fused_computation.36 | loop fusion | flops 256 | bytes 1032 | tf_op jit(solution)/shard_map/and | solution.py:239
  12.3 0.7 %constant_dynamic-slice_fusion.1 = s32[8,512]{1,0:T(8,128)S(1)} fusion(s32[64,512]{1,0:T(8,128)} %param.9, s32[]{:T(128)S(6)} %select_n.96), kind=kLoop, calls=%fused_computation.47 | loop fusion | bytes 32772 | tf_op jit(solution)/shard_map/dynamic_slice | solution.py:252
  13.0 1.1 %copy.20 = bf16[8,128,128]{1,2,0:T(8,128)(2,1)S(1)} copy(bf16[8,128,128]{2,1,0:T(8,128)(2,1)} %param.13) | data formatting | bytes 524288 | tf_op args[5]
  14.5 0.2 select_reduce_fusion
  14.9 0.6 fusion.12
  15.6 1.1 %fusion.4 = (f32[1,64,1024]{2,1,0:T(8,128)S(1)}, f32[1,64,1024]{2,1,0:T(8,128)S(1)}) fusion(s32[64]{0:T(128)S(1)} %get-tuple-element.50, s32[64]{0:T(128)S(1)} %get-tuple-element.49, s32[1024]{0:T(1024)S(1)} %mul.173), kind=kLoop, calls=%fused_computation.19 | loop fusion | flops 983040 | bytes 528896 | tf_op jit(solution)/shard_map/cos | solution.py:217
  16.7 3.5 %all-to-all-done.got_ref = bf16[8,256,128]{2,1,0:T(8,128)(2,1)S(1)} async-done(((bf16[8,256,128]{2,1,0:T(8,128)(2,1)}), bf16[8,256,128]{2,1,0:T(8,128)(2,1)S(1)}, u32[]{:S(2)}, u32[]{:S(2)}) %all-to-all-start) | async-done | bytes 524320 | tf_op jit(solution)/shard_map/all_to_all | solution.py:237
  20.2 0.9 %focus.1 = bf16[256,128]{1,0:T(8,128)(2,1)S(1)} custom-call(s32[8,16]{1,0:T(8,128)S(1)} %negate_and_fusion.back_ref, bf16[8,256,128]{2,1,0:T(8,128)(2,1)S(1)} %all-to-all-done.got_ref, bf16[8,128,128]{2,1,0:T(8,128)(2,1)S(1)} %bitcast.12), custom_call_target="tpu_custom_call" | custom-call | tf_op jit(solution)/shard_map/focus/pallas_call | solution.py:84
  21.1 2.7 %collective-permute-start = (bf16[256,128]{1,0:T(8,128)(2,1)S(1)}, bf16[256,128]{1,0:T(8,128)(2,1)S(1)}, u32[]{:S(2)}, u32[]{:S(2)}) collective-permute-start(bf16[256,128]{1,0:T(8,128)(2,1)S(1)} %focus.1), channel_id=1, source_target_pairs={{0,128},{128,0},{1,129},{129,1},{2,130},{130,2},{3,131},{131,3},{4... | collective-permute-start | bytes 196616 | tf_op jit(solution)/shard_map/ppermute | solution.py:267
  23.8 2.0 %collective-permute-done = bf16[256,128]{1,0:T(8,128)(2,1)S(1)} collective-permute-done((bf16[256,128]{1,0:T(8,128)(2,1)S(1)}, bf16[256,128]{1,0:T(8,128)(2,1)S(1)}, u32[]{:S(2)}, u32[]{:S(2)}) %collective-permute-start) | collective-permute-done | bytes 65568 | tf_op jit(solution)/shard_map/ppermute | solution.py:267
  25.8 1.7 %collective-permute-start.1 = (bf16[512,128]{1,0:T(8,128)(2,1)S(1)}, bf16[512,128]{1,0:T(8,128)(2,1)S(1)}, u32[]{:S(2)}, u32[]{:S(2)}) collective-permute-start(bf16[512,128]{1,0:T(8,128)(2,1)S(1)} %pad_maximum_fusion.2.refs_0_), channel_id=1, source_target_pairs={{0,16},{16,32},{32,48},{48,64},{64,80},{80,96},{96,112},{112,0},{1... | collective-permute-start | bytes 393224 | tf_op jit(solution)/shard_map/ppermute | solution.py:273
  27.6 4.0 %collective-permute-start.2 = (bf16[512,128]{1,0:T(8,128)(2,1)S(1)}, bf16[512,128]{1,0:T(8,128)(2,1)S(1)}, u32[]{:S(2)}, u32[]{:S(2)}) collective-permute-start(bf16[512,128]{1,0:T(8,128)(2,1)S(1)} %pad_maximum_fusion.2.refs_0_), channel_id=1, source_target_pairs={{0,112},{16,0},{32,16},{48,32},{64,48},{80,64},{96,80},{112,96},{1... | collective-permute-start | bytes 393224 | tf_op jit(solution)/shard_map/ppermute | solution.py:273
  32.2 2.1 %turns.1 = (bf16[2048,512]{1,0:T(8,128)(2,1)S(1)}, bf16[2048,512]{1,0:T(8,128)(2,1)S(1)}, bf16[2048,512]{1,0:T(8,128)(2,1)S(1)}, bf16[2048,512]{1,0:T(8,128)(2,1)S(1)}) custom-call(f32[2,32,1,1024]{3,2,1,0:T(1,128)S(1)} %broadcast_in_dim.44.coarse_ref, f32[2,64,1024]{2,1,0:T(8,128)S(1)} %pad_maximum_fusion.fine_ref), custom_call_target="tpu_custom_call" | custom-call | tf_op jit(solution)/shard_map/turns/pallas_call | solution.py:133
  34.3 3.2 %collective-permute-start.5 = (bf16[512,128]{1,0:T(8,128)(2,1)S(1)}, bf16[512,128]{1,0:T(8,128)(2,1)S(1)}, u32[]{:S(2)}, u32[]{:S(2)}) collective-permute-start(bf16[512,128]{1,0:T(8,128)(2,1)S(1)} %pad_maximum_fusion.2.refs_0_), channel_id=1, source_target_pairs={{0,8},{8,0},{1,9},{9,1},{2,10},{10,2},{3,11},{11,3},{4,12},{12,4},... | collective-permute-start | bytes 393224 | tf_op jit(solution)/shard_map/ppermute | solution.py:280
  37.5 2.7 %collective-permute-start.4 = (bf16[512,128]{1,0:T(8,128)(2,1)S(1)}, bf16[512,128]{1,0:T(8,128)(2,1)S(1)}, u32[]{:S(2)}, u32[]{:S(2)}) collective-permute-start(bf16[512,128]{1,0:T(8,128)(2,1)S(1)} %collective-permute-done.2.refs_3_), channel_id=1, source_target_pairs={{0,112},{16,0},{32,16},{48,32},{64,48},{80,64},{96,80},{112,96},{1... | collective-permute-start | bytes 393224 | tf_op jit(solution)/shard_map/ppermute | solution.py:273
  40.3 3.3 %part.3.refs_4_ = f32[2048,1024]{1,0:T(8,128)S(1)} custom-call(s32[16]{0:T(128)S(1)} %fusion.19.pair_ref, s32[8,16,1,64]{3,2,1,0:T(1,128)S(1)} %broadcast_add_fusion.code_ref, bf16[2048,512]{1,0:T(8,128)(2,1)S(1)} %get-tuple-element.28.turn_ref, bf16[512,128]{1,0:T(8,128)(2,1)S(1)} %pad_maximum_fusion.2.refs_0_, ...), custom_call_target="tpu_custom_call" | custom-call | tf_op jit(solution)/shard_map/part/pallas_call | solution.py:180
  43.6 0.8 %collective-permute-start.8 = (bf16[512,128]{1,0:T(8,128)(2,1)S(1)}, bf16[512,128]{1,0:T(8,128)(2,1)S(1)}, u32[]{:S(2)}, u32[]{:S(2)}) collective-permute-start(bf16[512,128]{1,0:T(8,128)(2,1)S(1)} %collective-permute-done.1.refs_2_), channel_id=1, source_target_pairs={{0,8},{8,0},{1,9},{9,1},{2,10},{10,2},{3,11},{11,3},{4,12},{12,4},... | collective-permute-start | bytes 393224 | tf_op jit(solution)/shard_map/ppermute | solution.py:277
  44.5 0.2 collective-permute-start.6
  44.7 2.7 %collective-permute-start.7 = (bf16[512,128]{1,0:T(8,128)(2,1)S(1)}, bf16[512,128]{1,0:T(8,128)(2,1)S(1)}, u32[]{:S(2)}, u32[]{:S(2)}) collective-permute-start(bf16[512,128]{1,0:T(8,128)(2,1)S(1)} %collective-permute-done.4.refs_3_), channel_id=1, source_target_pairs={{0,112},{16,0},{32,16},{48,32},{64,48},{80,64},{96,80},{112,96},{1... | collective-permute-start | bytes 393224 | tf_op jit(solution)/shard_map/ppermute | solution.py:273
  47.3 3.5 %part.4.refs_4_ = f32[2048,1024]{1,0:T(8,128)S(1)} custom-call(s32[16]{0:T(128)S(1)} %fusion.19.pair_ref, s32[8,16,1,64]{3,2,1,0:T(1,128)S(1)} %broadcast_add_fusion.code_ref, bf16[2048,512]{1,0:T(8,128)(2,1)S(1)} %get-tuple-element.32.turn_ref, bf16[512,128]{1,0:T(8,128)(2,1)S(1)} %collective-permute-done.8.refs_0_, ...), custom_call_target="tpu_custom_call", output_to_operand_aliasing={{}: (7, {})} | custom-call | tf_op jit(solution)/shard_map/part/pallas_call | solution.py:180
  50.8 0.9 %collective-permute-start.13 = (bf16[512,128]{1,0:T(8,128)(2,1)S(1)}, bf16[512,128]{1,0:T(8,128)(2,1)S(1)}, u32[]{:S(2)}, u32[]{:S(2)}) collective-permute-start(bf16[512,128]{1,0:T(8,128)(2,1)S(1)} %collective-permute-done.3.refs_2_), channel_id=1, source_target_pairs={{0,8},{8,0},{1,9},{9,1},{2,10},{10,2},{3,11},{11,3},{4,12},{12,4},... | collective-permute-start | bytes 393224 | tf_op jit(solution)/shard_map/ppermute | solution.py:277
  51.8 0.4 collective-permute-start.12
  52.3 1.5 %collective-permute-start.10 = (bf16[512,128]{1,0:T(8,128)(2,1)S(1)}, bf16[512,128]{1,0:T(8,128)(2,1)S(1)}, u32[]{:S(2)}, u32[]{:S(2)}) collective-permute-start(bf16[512,128]{1,0:T(8,128)(2,1)S(1)} %collective-permute-done.6.refs_2_), channel_id=1, source_target_pairs={{0,8},{8,0},{1,9},{9,1},{2,10},{10,2},{3,11},{11,3},{4,12},{12,4},... | collective-permute-start | bytes 393224 | tf_op jit(solution)/shard_map/ppermute | solution.py:285
  53.8 3.5 %part.5.refs_4_ = f32[2048,1024]{1,0:T(8,128)S(1)} custom-call(s32[16]{0:T(128)S(1)} %fusion.19.pair_ref, s32[8,16,1,64]{3,2,1,0:T(1,128)S(1)} %broadcast_add_fusion.code_ref, bf16[2048,512]{1,0:T(8,128)(2,1)S(1)} %get-tuple-element.39.turn_ref, bf16[512,128]{1,0:T(8,128)(2,1)S(1)} %collective-permute-done.13.refs_0_, ...), custom_call_target="tpu_custom_call", output_to_operand_aliasing={{}: (7, {})} | custom-call | tf_op jit(solution)/shard_map/part/pallas_call | solution.py:180
  57.3 0.4 collective-permute-done.12.refs_2_
  57.7 1.2 %collective-permute-start.15 = (bf16[512,128]{1,0:T(8,128)(2,1)S(1)}, bf16[512,128]{1,0:T(8,128)(2,1)S(1)}, u32[]{:S(2)}, u32[]{:S(2)}) collective-permute-start(bf16[512,128]{1,0:T(8,128)(2,1)S(1)} %collective-permute-done.12.refs_2_), channel_id=1, source_target_pairs={{0,8},{8,0},{1,9},{9,1},{2,10},{10,2},{3,11},{11,3},{4,12},{12,4},... | collective-permute-start | bytes 393224 | tf_op jit(solution)/shard_map/ppermute | solution.py:288
  59.0 1.0 %collective-permute-done.15.refs_3_ = bf16[512,128]{1,0:T(8,128)(2,1)S(1)} collective-permute-done((bf16[512,128]{1,0:T(8,128)(2,1)S(1)}, bf16[512,128]{1,0:T(8,128)(2,1)S(1)}, u32[]{:S(2)}, u32[]{:S(2)}) %collective-permute-start.15) | collective-permute-done | bytes 131104 | tf_op jit(solution)/shard_map/ppermute | solution.py:288
  59.9 4.6 %last.1 = bf16[1024,2,1024]{2,1,0:T(2,128)(2,1)} custom-call(s32[16]{0:T(128)S(1)} %fusion.19.pair_ref, s32[8,16,1,64]{3,2,1,0:T(1,128)S(1)} %broadcast_add_fusion.code_ref, bf16[2048,512]{1,0:T(8,128)(2,1)S(1)} %get-tuple-element.25.turn_ref, bf16[512,128]{1,0:T(8,128)(2,1)S(1)} %collective-permute-done.10.refs_0_, ...), custom_call_target="tpu_custom_call" | custom-call | tf_op jit(solution)/shard_map/last/pallas_call | solution.py:193
  (50 shorter events, 1.6 us)
Async XLA Ops:
  0.0 1.3 %copy-start = (s32[64,32]{0,1:T(8,128)S(1)}, s32[64,32]{0,1:T(8,128)}, u32[]{:S(2)}) copy-start(s32[64,32]{0,1:T(8,128)} %param.11) | copy-start | bytes 24580
  0.0 14.1 %copy-start.2 = (s32[16]{0:T(128)S(1)}, s32[16]{0:T(128)}, u32[]{:S(2)}) copy-start(s32[16]{0:T(128)} %constant.141.clone) | copy-start | bytes 196
  0.0 14.1 %copy-start.3 = (s32[16]{0:T(128)S(1)}, s32[16]{0:T(128)}, u32[]{:S(2)}) copy-start(s32[16]{0:T(128)} %constant.142.clone) | copy-start | bytes 196
  0.0 14.4 %copy-start.1 = (s32[1024]{0:T(1024)S(1)}, s32[1024]{0:T(1024)}, u32[]{:S(2)}) copy-start(s32[1024]{0:T(1024)} %param.12) | copy-start | bytes 12292
  5.6 14.6 %all-to-all-start = ((bf16[8,256,128]{2,1,0:T(8,128)(2,1)}), bf16[8,256,128]{2,1,0:T(8,128)(2,1)S(1)}, u32[]{:S(2)}, u32[]{:S(2)}) async-start(bf16[8,256,128]{2,1,0:T(8,128)(2,1)} %bitcast.6), calls=%async_computation | async-start | bytes 1048576 | tf_op jit(solution)/shard_map/all_to_all | solution.py:237
  21.1 4.7 %collective-permute-start = (bf16[256,128]{1,0:T(8,128)(2,1)S(1)}, bf16[256,128]{1,0:T(8,128)(2,1)S(1)}, u32[]{:S(2)}, u32[]{:S(2)}) collective-permute-start(bf16[256,128]{1,0:T(8,128)(2,1)S(1)} %focus.1), channel_id=1, source_target_pairs={{0,128},{128,0},{1,129},{129,1},{2,130},{130,2},{3,131},{131,3},{4... | collective-permute-start | bytes 196616 | tf_op jit(solution)/shard_map/ppermute | solution.py:267
  25.8 11.7 %collective-permute-start.1 = (bf16[512,128]{1,0:T(8,128)(2,1)S(1)}, bf16[512,128]{1,0:T(8,128)(2,1)S(1)}, u32[]{:S(2)}, u32[]{:S(2)}) collective-permute-start(bf16[512,128]{1,0:T(8,128)(2,1)S(1)} %pad_maximum_fusion.2.refs_0_), channel_id=1, source_target_pairs={{0,16},{16,32},{32,48},{48,64},{64,80},{80,96},{96,112},{112,0},{1... | collective-permute-start | bytes 393224 | tf_op jit(solution)/shard_map/ppermute | solution.py:273
  27.6 10.0 %collective-permute-start.2 = (bf16[512,128]{1,0:T(8,128)(2,1)S(1)}, bf16[512,128]{1,0:T(8,128)(2,1)S(1)}, u32[]{:S(2)}, u32[]{:S(2)}) collective-permute-start(bf16[512,128]{1,0:T(8,128)(2,1)S(1)} %pad_maximum_fusion.2.refs_0_), channel_id=1, source_target_pairs={{0,112},{16,0},{32,16},{48,32},{64,48},{80,64},{96,80},{112,96},{1... | collective-permute-start | bytes 393224 | tf_op jit(solution)/shard_map/ppermute | solution.py:273
  34.3 6.0 %collective-permute-start.5 = (bf16[512,128]{1,0:T(8,128)(2,1)S(1)}, bf16[512,128]{1,0:T(8,128)(2,1)S(1)}, u32[]{:S(2)}, u32[]{:S(2)}) collective-permute-start(bf16[512,128]{1,0:T(8,128)(2,1)S(1)} %pad_maximum_fusion.2.refs_0_), channel_id=1, source_target_pairs={{0,8},{8,0},{1,9},{9,1},{2,10},{10,2},{3,11},{11,3},{4,12},{12,4},... | collective-permute-start | bytes 393224 | tf_op jit(solution)/shard_map/ppermute | solution.py:280
  37.5 6.9 %collective-permute-start.3 = (bf16[512,128]{1,0:T(8,128)(2,1)S(1)}, bf16[512,128]{1,0:T(8,128)(2,1)S(1)}, u32[]{:S(2)}, u32[]{:S(2)}) collective-permute-start(bf16[512,128]{1,0:T(8,128)(2,1)S(1)} %collective-permute-done.1.refs_2_), channel_id=1, source_target_pairs={{0,16},{16,32},{32,48},{48,64},{64,80},{80,96},{96,112},{112,0},{1... | collective-permute-start | bytes 393224 | tf_op jit(solution)/shard_map/ppermute | solution.py:273
  37.5 6.9 %collective-permute-start.4 = (bf16[512,128]{1,0:T(8,128)(2,1)S(1)}, bf16[512,128]{1,0:T(8,128)(2,1)S(1)}, u32[]{:S(2)}, u32[]{:S(2)}) collective-permute-start(bf16[512,128]{1,0:T(8,128)(2,1)S(1)} %collective-permute-done.2.refs_3_), channel_id=1, source_target_pairs={{0,112},{16,0},{32,16},{48,32},{64,48},{80,64},{96,80},{112,96},{1... | collective-permute-start | bytes 393224 | tf_op jit(solution)/shard_map/ppermute | solution.py:273
  43.6 3.7 %collective-permute-start.8 = (bf16[512,128]{1,0:T(8,128)(2,1)S(1)}, bf16[512,128]{1,0:T(8,128)(2,1)S(1)}, u32[]{:S(2)}, u32[]{:S(2)}) collective-permute-start(bf16[512,128]{1,0:T(8,128)(2,1)S(1)} %collective-permute-done.1.refs_2_), channel_id=1, source_target_pairs={{0,8},{8,0},{1,9},{9,1},{2,10},{10,2},{3,11},{11,3},{4,12},{12,4},... | collective-permute-start | bytes 393224 | tf_op jit(solution)/shard_map/ppermute | solution.py:277
  44.4 3.0 %collective-permute-start.9 = (bf16[512,128]{1,0:T(8,128)(2,1)S(1)}, bf16[512,128]{1,0:T(8,128)(2,1)S(1)}, u32[]{:S(2)}, u32[]{:S(2)}) collective-permute-start(bf16[512,128]{1,0:T(8,128)(2,1)S(1)} %collective-permute-done.2.refs_3_), channel_id=1, source_target_pairs={{0,8},{8,0},{1,9},{9,1},{2,10},{10,2},{3,11},{11,3},{4,12},{12,4},... | collective-permute-start | bytes 393224 | tf_op jit(solution)/shard_map/ppermute | solution.py:277
  44.5 7.4 %collective-permute-start.6 = (bf16[512,128]{1,0:T(8,128)(2,1)S(1)}, bf16[512,128]{1,0:T(8,128)(2,1)S(1)}, u32[]{:S(2)}, u32[]{:S(2)}) collective-permute-start(bf16[512,128]{1,0:T(8,128)(2,1)S(1)} %collective-permute-done.3.refs_2_), channel_id=1, source_target_pairs={{0,16},{16,32},{32,48},{48,64},{64,80},{80,96},{96,112},{112,0},{1... | collective-permute-start | bytes 393224 | tf_op jit(solution)/shard_map/ppermute | solution.py:273
  44.7 7.2 %collective-permute-start.7 = (bf16[512,128]{1,0:T(8,128)(2,1)S(1)}, bf16[512,128]{1,0:T(8,128)(2,1)S(1)}, u32[]{:S(2)}, u32[]{:S(2)}) collective-permute-start(bf16[512,128]{1,0:T(8,128)(2,1)S(1)} %collective-permute-done.4.refs_3_), channel_id=1, source_target_pairs={{0,112},{16,0},{32,16},{48,32},{64,48},{80,64},{96,80},{112,96},{1... | collective-permute-start | bytes 393224 | tf_op jit(solution)/shard_map/ppermute | solution.py:273
  50.8 3.0 %collective-permute-start.13 = (bf16[512,128]{1,0:T(8,128)(2,1)S(1)}, bf16[512,128]{1,0:T(8,128)(2,1)S(1)}, u32[]{:S(2)}, u32[]{:S(2)}) collective-permute-start(bf16[512,128]{1,0:T(8,128)(2,1)S(1)} %collective-permute-done.3.refs_2_), channel_id=1, source_target_pairs={{0,8},{8,0},{1,9},{9,1},{2,10},{10,2},{3,11},{11,3},{4,12},{12,4},... | collective-permute-start | bytes 393224 | tf_op jit(solution)/shard_map/ppermute | solution.py:277
  51.7 2.1 %collective-permute-start.14 = (bf16[512,128]{1,0:T(8,128)(2,1)S(1)}, bf16[512,128]{1,0:T(8,128)(2,1)S(1)}, u32[]{:S(2)}, u32[]{:S(2)}) collective-permute-start(bf16[512,128]{1,0:T(8,128)(2,1)S(1)} %collective-permute-done.4.refs_3_), channel_id=1, source_target_pairs={{0,8},{8,0},{1,9},{9,1},{2,10},{10,2},{3,11},{11,3},{4,12},{12,4},... | collective-permute-start | bytes 393224 | tf_op jit(solution)/shard_map/ppermute | solution.py:277
  51.8 5.9 %collective-permute-start.12 = (bf16[512,128]{1,0:T(8,128)(2,1)S(1)}, bf16[512,128]{1,0:T(8,128)(2,1)S(1)}, u32[]{:S(2)}, u32[]{:S(2)}) collective-permute-start(bf16[512,128]{1,0:T(8,128)(2,1)S(1)} %collective-permute-done.6.refs_2_), channel_id=1, source_target_pairs={{0,16},{16,32},{32,48},{48,64},{64,80},{80,96},{96,112},{112,0},{1... | collective-permute-start | bytes 393224 | tf_op jit(solution)/shard_map/ppermute | solution.py:284
  52.3 6.7 %collective-permute-start.10 = (bf16[512,128]{1,0:T(8,128)(2,1)S(1)}, bf16[512,128]{1,0:T(8,128)(2,1)S(1)}, u32[]{:S(2)}, u32[]{:S(2)}) collective-permute-start(bf16[512,128]{1,0:T(8,128)(2,1)S(1)} %collective-permute-done.6.refs_2_), channel_id=1, source_target_pairs={{0,8},{8,0},{1,9},{9,1},{2,10},{10,2},{3,11},{11,3},{4,12},{12,4},... | collective-permute-start | bytes 393224 | tf_op jit(solution)/shard_map/ppermute | solution.py:285
  53.8 5.2 %collective-permute-start.11 = (bf16[512,128]{1,0:T(8,128)(2,1)S(1)}, bf16[512,128]{1,0:T(8,128)(2,1)S(1)}, u32[]{:S(2)}, u32[]{:S(2)}) collective-permute-start(bf16[512,128]{1,0:T(8,128)(2,1)S(1)} %collective-permute-done.7.refs_3_), channel_id=1, source_target_pairs={{0,8},{8,0},{1,9},{9,1},{2,10},{10,2},{3,11},{11,3},{4,12},{12,4},... | collective-permute-start | bytes 393224 | tf_op jit(solution)/shard_map/ppermute | solution.py:285
  57.7 2.2 %collective-permute-start.15 = (bf16[512,128]{1,0:T(8,128)(2,1)S(1)}, bf16[512,128]{1,0:T(8,128)(2,1)S(1)}, u32[]{:S(2)}, u32[]{:S(2)}) collective-permute-start(bf16[512,128]{1,0:T(8,128)(2,1)S(1)} %collective-permute-done.12.refs_2_), channel_id=1, source_target_pairs={{0,8},{8,0},{1,9},{9,1},{2,10},{10,2},{3,11},{11,3},{4,12},{12,4},... | collective-permute-start | bytes 393224 | tf_op jit(solution)/shard_map/ppermute | solution.py:288

commit v5 on v4

--- a/solution.py
+++ b/solution.py
@@ -18,48 +18,46 @@
 SMEM = pl.BlockSpec(memory_space=pltpu.SMEM)
 VMEM = pl.BlockSpec(memory_space=pltpu.VMEM)
 
-def pack_kernel(word_ref, bins_ref, out_ref, cut_sc):
+def pack_kernel(word_ref, bins_ref, out_ref):
     tiles, per_block = word_ref.shape
-    lane = lax.broadcasted_iota(jnp.int32, (2, LANES), 1)
+    _, parts, lanes = bins_ref.shape
+    lane = lax.broadcasted_iota(jnp.int32, (parts, lanes), 1)
     at_once = 4
 
     def take(step, _):
         for u in range(at_once):
             for entry in range(per_block):
                 word = word_ref[step * at_once + u, entry]
-                row = pl.multiple_of(word >> 7, 2)
-                low = bins_ref[pl.ds(row, 2), :]
-                high = bins_ref[pl.ds(pl.multiple_of(row + 2, 2), 2), :]
-                at = ((step * at_once + u) * per_block + entry) * 2
-                cut_sc[pl.ds(pl.multiple_of(at, 2), 2), :] = jnp.where(
-                    lane >= (word & (LANES - 1)), low, high
-                )
+                row = word >> 7
+                low = bins_ref[row].astype(jnp.float32)
+                high = bins_ref[row + 1].astype(jnp.float32)
+                cut = jnp.where(lane >= (word & (lanes - 1)), low, high)
+                out_ref[(step * at_once + u) * per_block + entry] = cut.astype(out_ref.dtype)
         return 0
 
     lax.fori_loop(0, tiles // at_once, take, 0)
-    out_ref[...] = cut_sc[...].astype(jnp.bfloat16)
+
 
 def pack(echoes, ids, starts, live):
     pulses, parts, bins = echoes.shape
     panels = bins // LANES
     tiles, per_block = ids.shape
-    rows = echoes.astype(jnp.float32).reshape(pulses, parts, panels, LANES).transpose(0, 2, 1, 3)
+    rows = echoes.reshape(pulses, parts, panels, LANES).transpose(0, 2, 1, 3)
     rows = jnp.pad(rows, ((0, 0), (1, 1), (0, 0), (0, 0)))
-    rows = rows.reshape(pulses * (panels + 2) * parts, LANES)
     offs = starts - lax.axis_index(ROW) * bins
     used = jnp.arange(per_block, dtype=jnp.int32)[None, :] < live
     inside = used & (offs > -LANES) & (offs < bins)
     first = jnp.where(inside, ids * (panels + 2) + (offs >> 7) + 1, panels + 1)
-    word = first * (parts * LANES) + (offs & (LANES - 1))
+    word = first * LANES + (offs & (LANES - 1))
     return pl.pallas_call(
         pack_kernel,
-        out_shape=jax.ShapeDtypeStruct((tiles * per_block * parts, LANES), jnp.bfloat16),
+        out_shape=jax.ShapeDtypeStruct((tiles * per_block, parts, LANES), echoes.dtype),
         in_specs=[SMEM, VMEM],
         out_specs=VMEM,
-        scratch_shapes=[pltpu.VMEM((tiles * per_block * parts, LANES), jnp.float32)],
-        compiler_params=pltpu.CompilerParams(vmem_limit_bytes=8 << 20),
+        compiler_params=pltpu.CompilerParams(vmem_limit_bytes=4 << 20),
         name="pack",
-    )(word, rows)
+    )(word, rows.reshape(pulses * (panels + 2), parts, LANES))
+
 
 def focus_kernel(back_ref, got_ref, turned_ref, out_ref, panels):
     tiles, per_block = back_ref.shape
@@ -111,7 +109,7 @@
             spread[number * slots : (number + 1) * slots, columns] = placed[:slots]
             spread[half + number * slots : half + (number + 1) * slots, columns] = placed[slots:]
 
-def turn_kernel(coarse_ref, fine_ref, *out_refs):
+def turn_kernel(coarse_ref, fine_ref, mark_ref, *out_refs):
     pulses = coarse_ref.shape[3] // len(out_refs)
     rows = fine_ref.shape[1]
 
@@ -126,15 +124,16 @@
         return 0
 
     lax.fori_loop(0, coarse_ref.shape[1], step, 0, unroll=4)
+    mark_ref[...] = jnp.zeros(mark_ref.shape, mark_ref.dtype)
 
 def turns(coarse, fine, parts):
     rows = coarse.shape[1] * fine.shape[1]
     shape = jax.ShapeDtypeStruct((rows, 2 * coarse.shape[3] // parts), jnp.bfloat16)
     return pl.pallas_call(
         turn_kernel,
-        out_shape=[shape] * parts,
+        out_shape=[jax.ShapeDtypeStruct((8, LANES), jnp.float32)] + [shape] * parts,
         in_specs=[VMEM] * 2,
-        out_specs=[VMEM] * parts,
+        out_specs=[VMEM] * (parts + 1),
         compiler_params=pltpu.CompilerParams(vmem_limit_bytes=2 << 20),
         name="turns",
     )(coarse, fine)
@@ -168,11 +167,11 @@
     for copy in sent:
         copy.wait()
 
-def part(pairs, code, turn, blocks, held, first, scale=None):
+def part(pairs, code, turn, blocks, held, first, scale=None, mark=None):
     tiles = code.shape[0]
     rows, depth = turn.shape
     n = tiles * LANES
-    operands = (pairs, code, turn, *blocks) + (() if held is None else (held,))
+    operands = (pairs, code, turn, *blocks, mark if held is None else held)
     specs = [SMEM] + [VMEM] * (len(operands) - 1)
     scratch = [pltpu.VMEM((depth, n), jnp.bfloat16)]
     params = pltpu.CompilerParams(vmem_limit_bytes=(6 if scale is None else 10) << 20)
@@ -233,8 +232,7 @@
     my_starts = lax.dynamic_slice_in_dim(bin_start, first_entry, per_block, 1)
     my_live = lax.dynamic_slice_in_dim(live_count, ang_index, 1, 1)
     packed = pack(echoes, my_ids - ang_index * block_pulses, my_starts, my_live)
-    rows = packed.shape[0] // n_rows
-    got = lax.all_to_all(packed.reshape(n_rows, rows, LANES), ROW, 0, 0, tiled=True)
+    got = lax.all_to_all(packed.reshape(n_rows, -1, LANES), ROW, 0, 0, tiled=True)
     my_tiles = lax.axis_index(ROW) * tiles_mine
     back = (-lax.dynamic_slice(bin_start, (my_tiles, first_entry), (tiles_mine, per_block))) & (LANES - 1)
     mine = focus(back, got, interp.swapaxes(1, 2))
@@ -259,12 +257,13 @@
     rates = pick(wavenum.reshape(blocks, block_pulses), order).reshape(-1)
     coarse, fine = twiddles(rates, ang_index * col_dev, col_dev)
 
-    tables = turns(coarse, fine, half)
+    mark, *tables = turns(coarse, fine, half)
 
     swap = [(0, 1), (1, 0)]
     ahead = [(i, (i + 1) % ring) for i in range(ring)]
     behind = [(i, (i - 1) % ring) for i in range(ring)]
     other = lax.ppermute(mine, "yh", swap)
+    other, mark = lax.optimization_barrier((other, mark))
 
     forward = backward = jnp.concatenate([mine, other], 0)
     near = [forward]
@@ -272,7 +271,9 @@
     for step in range(1, half):
         arriving = lax.ppermute(forward, "z", ahead), lax.ppermute(backward, "z", behind)
         if step > 1:
-            total = part(pairs, code, tables[step - 2], blocks, total, 4 * (step - 2))
+            total = part(
+                pairs, code, tables[step - 2], blocks, total, 4 * (step - 2), mark=mark
+            )
             *leaving, total = lax.optimization_barrier((*near, total))
             far = [lax.ppermute(block, "core", swap) for block in leaving]
             forward, backward, total = lax.optimization_barrier((*arriving, total))
@@ -282,11 +283,16 @@
         blocks = ([*near] if step == 1 else []) + far + [forward, backward]
         near = [forward, backward]
     opposite = lax.ppermute(forward, "z", ahead)
+    crossing = [
+        (2 * i + side, 2 * ((i - 1) % ring) + 1 - side) for i in range(ring) for side in (0, 1)
+    ]
+    across = lax.ppermute(backward, ("z", "core"), crossing)
     far = [lax.ppermute(block, "core", swap) for block in near]
     total = part(pairs, code, tables[half - 2], blocks, total, 4 * (half - 2))
-    opposite, total = lax.optimization_barrier((opposite, total))
-    blocks = far + [opposite, lax.ppermute(opposite, "core", swap)]
+    opposite, across, total = lax.optimization_barrier((opposite, across, total))
+    blocks = far + [opposite, across]
     return part(pairs, code, tables[half - 1], blocks, total, 4 * (half - 1), foot_len ** (-0.5))
+
 
 def solution(mesh):
     finer = Mesh(mesh.devices.reshape(2, -1, 2, 4, 2), FINE)

time: 65 us -> 64.8 us (level)
  waiting for transfers between devices: 6.89 us -> 1.57 us
  starting transfers between devices: 28.2 us -> 31.2 us
  local copies, waits for them, and re-layouts: 3.93 us -> 5.31 us
    ppermute x4, starting transfers between devices: 1.86 us -> 4.69 us  [body(): far = [lax.ppermute(block, 'core', swap) for block in leaving]]
    ppermute x1, waiting for transfers between devices: 1.98 us -> 0.01 us  [body(): other = lax.ppermute(mine, 'yh', swap)]
    all_to_all x1, waiting for transfers between devices: 3.5 us -> 1.53 us  [body(): lax.all_to_all(packed.reshape(n_rows, -1, LANES), ROW, 0, 0, tiled=True)]
    ppermute x1, starting transfers between devices: 1.24 us -> 2.75 us  [body(): across = lax.ppermute(backward, ('z', 'core'), crossing)]
    ppermute x3, starting transfers between devices: 4.78 us -> 3.54 us  [body(): far = [lax.ppermute(block, 'core', swap) for block in near]]
    ppermute x1, waiting for transfers between devices: 0.98 us -> 0.01 us  [body(): across = lax.ppermute(backward, ('z', 'core'), crossing)]
    unnamed x9 -> x3, local copies, waits for them, and re-layouts: 1.13 us -> 1.84 us
    broadcast_in_dim x1, local copies, waits for them, and re-layouts: 0.07 us -> 0.76 us  [pick(): return jnp.sum(jnp.where(hot[:, :, None], table[None], 0), axis=1)]
  transfers between devices with their start and end apart: 17 -> 17, of which waited for: 4 -> 1; matrix products, arithmetic and copies ran while one was open for 9% -> 11% of each run, Pallas kernels for 19% -> 19%
where the time goes in v5:
time: 64.8 us; the launch traced here: 64.3 us
  starting transfers between devices  31.2 us (48%)
  Pallas kernels  21.2 us (33%)
  local copies, waits for them, and re-layouts  5.31 us (8%)
  other arithmetic  4.62 us (7%)
  waiting for transfers between devices  1.57 us (2%)
    pallas_call x3, Pallas kernels, part(): pl.pallas_call(functools.partial(part_kernel, first=first, n_blocks=len(b...  10.3 us
    ppermute x3, starting transfers between devices, body(): lax.ppermute(backward, 'z', behind)  9.35 us
    all_to_all x1, starting transfers between devices, body(): lax.all_to_all(packed.reshape(n_rows, -1, LANES), ROW, 0, 0, tiled=True)  5.86 us
    ppermute x4, starting transfers between devices, body(): far = [lax.ppermute(block, 'core', swap) for block in leaving]  4.69 us
    pallas_call x1, Pallas kernels, part(): pl.pallas_call(functools.partial(last_kernel, first=first, n_blocks=len(b...  4.58 us
    ppermute x3, starting transfers between devices, body(): far = [lax.ppermute(block, 'core', swap) for block in near]  3.54 us
    pallas_call x1, Pallas kernels, pack(): pl.pallas_call(pack_kernel, out_shape=jax.ShapeDtypeStruct((tiles * per_b...  3.39 us
    ppermute x1, starting transfers between devices, body(): across = lax.ppermute(backward, ('z', 'core'), crossing)  2.75 us
  transfers between devices with their start and end apart: 17, of which 1 were waited for; matrix products, arithmetic and copies ran while one was open for 11% of the time, Pallas kernels for 19%

profile of v5, /device:TPU:1, one launch (start us, length us, event | category | flops | bytes accessed | tf_op | source)
XLA Modules:
  0.0 64.3 jit_solution(4293359159174022009)
XLA Ops:
  0.0 0.7 %copy-done = s32[64,32]{0,1:T(8,128)S(1)} copy-done((s32[64,32]{0,1:T(8,128)S(1)}, s32[64,32]{0,1:T(8,128)}, u32[]{:S(2)}) %copy-start) | copy-done | bytes 8216
  0.7 1.2 %pad.4 = bf16[32,18,2,128]{3,2,1,0:T(2,128)(2,1)S(1)} pad(bf16[32,16,2,128]{3,2,1,0:T(2,128)(2,1)} %bitcast.14, bf16[]{:T(256)} %constant.139.clone.1), padding=0_0x1_1x0_0x0_0 | pad | bytes 557058 | tf_op jit(solution)/shard_map/jit(_pad)/pad | solution.py:46
  1.9 0.9 %and_add_fusion.word_ref = s32[64,16]{1,0:T(8,128)S(1)} fusion(s32[64,512]{1,0:T(8,128)} %param.9, s32[]{:T(128)S(6)} %select_n.104, s32[64,512]{1,0:T(8,128)} %param.10, s32[]{:T(128)S(6)} %mul.193, s32[]{:T(128)S(6)} %mul.192, s32[64]{0:T(128)S(1)} %fusion.20), kind=kLoop, calls=%fused_computation.29 | loop fusion | flops 15360 | bytes 12556 | tf_op jit(solution)/shard_map/add | solution.py:51
  2.8 3.4 %pack.1 = bf16[1024,2,128]{2,1,0:T(2,128)(2,1)} custom-call(s32[64,16]{1,0:T(8,128)S(1)} %and_add_fusion.word_ref, bf16[576,2,128]{2,1,0:T(2,128)(2,1)S(1)} %bitcast.11), custom_call_target="tpu_custom_call" | custom-call | tf_op jit(solution)/shard_map/pack/pallas_call | solution.py:52
  6.2 5.9 %all-to-all-start = ((bf16[8,256,128]{2,1,0:T(8,128)(2,1)}), bf16[8,256,128]{2,1,0:T(8,128)(2,1)S(1)}, u32[]{:S(2)}, u32[]{:S(2)}) async-start(bf16[8,256,128]{2,1,0:T(8,128)(2,1)} %bitcast.6), calls=%async_computation | async-start | bytes 1048576 | tf_op jit(solution)/shard_map/all_to_all | solution.py:235
  12.1 1.1 %copy.20 = bf16[8,128,128]{1,2,0:T(8,128)(2,1)S(1)} copy(bf16[8,128,128]{2,1,0:T(8,128)(2,1)} %param.13) | data formatting | bytes 524288 | tf_op args[5]
  13.2 0.7 %fusion.19.pair_ref = s32[16]{0:T(128)S(1)} fusion(s32[16]{0:T(128)} %constant.140.clone, s32[16]{0:T(128)} %constant.141.clone, s32[]{:T(128)S(6)} %axis_index.36, s32[]{:T(128)S(6)} %axis_index.33), kind=kLoop, calls=%fused_computation.52 | loop fusion | flops 240 | bytes 200 | tf_op jit(solution)/shard_map/add | solution.py:248
  14.1 0.8 %broadcast_in_dim.41 = s32[32,32]{1,0:T(8,128)S(1)} reshape(s32[1024]{0:T(1024)} %param.12) | data formatting | bytes 8192 | tf_op jit(solution)/shard_map/jit(_where)/broadcast_in_dim | solution.py:205
  14.9 0.2 select_reduce_fusion
  15.2 0.6 fusion.12
  15.8 0.2 broadcast_in_dim.44.coarse_ref
  16.0 0.7 %constant_dynamic-slice_fusion.1 = s32[8,512]{1,0:T(8,128)S(1)} fusion(s32[64,512]{1,0:T(8,128)} %param.9, s32[]{:T(128)S(6)} %select_n.96), kind=kLoop, calls=%fused_computation.47 | loop fusion | bytes 32772 | tf_op jit(solution)/shard_map/dynamic_slice | solution.py:250
  17.3 0.8 %negate_and_fusion.back_ref = s32[8,16]{1,0:T(8,128)S(1)} fusion(s32[64,512]{1,0:T(8,128)} %param.10, s32[]{:T(128)S(6)} %select_n.96, s32[]{:T(128)S(6)} %select_n.104), kind=kLoop, calls=%fused_computation.36 | loop fusion | flops 256 | bytes 1032 | tf_op jit(solution)/shard_map/and | solution.py:237
  18.1 1.1 %fusion.4 = (f32[1,64,1024]{2,1,0:T(8,128)S(1)}, f32[1,64,1024]{2,1,0:T(8,128)S(1)}) fusion(s32[64]{0:T(128)S(1)} %get-tuple-element.58, s32[64]{0:T(128)S(1)} %get-tuple-element.57, s32[1024]{0:T(1024)S(1)} %mul.173), kind=kLoop, calls=%fused_computation.19 | loop fusion | flops 983040 | bytes 528896 | tf_op jit(solution)/shard_map/cos | solution.py:216
  19.2 1.5 %all-to-all-done.got_ref = bf16[8,256,128]{2,1,0:T(8,128)(2,1)S(1)} async-done(((bf16[8,256,128]{2,1,0:T(8,128)(2,1)}), bf16[8,256,128]{2,1,0:T(8,128)(2,1)S(1)}, u32[]{:S(2)}, u32[]{:S(2)}) %all-to-all-start) | async-done | bytes 524320 | tf_op jit(solution)/shard_map/all_to_all | solution.py:235
  20.7 0.9 %focus.1 = bf16[256,128]{1,0:T(8,128)(2,1)S(1)} custom-call(s32[8,16]{1,0:T(8,128)S(1)} %negate_and_fusion.back_ref, bf16[8,256,128]{2,1,0:T(8,128)(2,1)S(1)} %all-to-all-done.got_ref, bf16[8,128,128]{2,1,0:T(8,128)(2,1)S(1)} %bitcast.12), custom_call_target="tpu_custom_call" | custom-call | tf_op jit(solution)/shard_map/focus/pallas_call | solution.py:82
  21.7 2.7 %collective-permute-start = (bf16[256,128]{1,0:T(8,128)(2,1)S(1)}, bf16[256,128]{1,0:T(8,128)(2,1)S(1)}, u32[]{:S(2)}, u32[]{:S(2)}) collective-permute-start(bf16[256,128]{1,0:T(8,128)(2,1)S(1)} %focus.1), channel_id=1, source_target_pairs={{0,128},{128,0},{1,129},{129,1},{2,130},{130,2},{3,131},{131,3},{4... | collective-permute-start | bytes 196616 | tf_op jit(solution)/shard_map/ppermute | solution.py:265
  24.4 2.1 %turns.1 = (f32[8,128]{1,0:T(8,128)S(1)}, bf16[2048,512]{1,0:T(8,128)(2,1)S(1)}, bf16[2048,512]{1,0:T(8,128)(2,1)S(1)}, bf16[2048,512]{1,0:T(8,128)(2,1)S(1)}, bf16[2048,512]{1,0:T(8,128)(2,1)S(1)}) custom-call(f32[2,32,1,1024]{3,2,1,0:T(1,128)S(1)} %broadcast_in_dim.44.coarse_ref, f32[2,64,1024]{2,1,0:T(8,128)S(1)} %pad_maximum_fusion.fine_ref), custom_call_target="tpu_custom_call" | custom-call | tf_op jit(solution)/shard_map/turns/pallas_call | solution.py:132
  26.5 1.7 %collective-permute-start.1 = (bf16[512,128]{1,0:T(8,128)(2,1)S(1)}, bf16[512,128]{1,0:T(8,128)(2,1)S(1)}, u32[]{:S(2)}, u32[]{:S(2)}) collective-permute-start(bf16[512,128]{1,0:T(8,128)(2,1)S(1)} %pad_maximum_fusion.2.refs_0_), channel_id=1, source_target_pairs={{0,16},{16,32},{32,48},{48,64},{64,80},{80,96},{96,112},{112,0},{1... | collective-permute-start | bytes 393224 | tf_op jit(solution)/shard_map/ppermute | solution.py:272
  28.2 4.0 %collective-permute-start.2 = (bf16[512,128]{1,0:T(8,128)(2,1)S(1)}, bf16[512,128]{1,0:T(8,128)(2,1)S(1)}, u32[]{:S(2)}, u32[]{:S(2)}) collective-permute-start(bf16[512,128]{1,0:T(8,128)(2,1)S(1)} %pad_maximum_fusion.2.refs_0_), channel_id=1, source_target_pairs={{0,112},{16,0},{32,16},{48,32},{64,48},{80,64},{96,80},{112,96},{1... | collective-permute-start | bytes 393224 | tf_op jit(solution)/shard_map/ppermute | solution.py:272
  32.2 3.0 %collective-permute-start.5 = (bf16[512,128]{1,0:T(8,128)(2,1)S(1)}, bf16[512,128]{1,0:T(8,128)(2,1)S(1)}, u32[]{:S(2)}, u32[]{:S(2)}) collective-permute-start(bf16[512,128]{1,0:T(8,128)(2,1)S(1)} %pad_maximum_fusion.2.refs_0_), channel_id=1, source_target_pairs={{0,8},{8,0},{1,9},{9,1},{2,10},{10,2},{3,11},{11,3},{4,12},{12,4},... | collective-permute-start | bytes 393224 | tf_op jit(solution)/shard_map/ppermute | solution.py:281
  35.4 2.7 %collective-permute-start.4 = (bf16[512,128]{1,0:T(8,128)(2,1)S(1)}, bf16[512,128]{1,0:T(8,128)(2,1)S(1)}, u32[]{:S(2)}, u32[]{:S(2)}) collective-permute-start(bf16[512,128]{1,0:T(8,128)(2,1)S(1)} %collective-permute-done.2.refs_3_), channel_id=1, source_target_pairs={{0,112},{16,0},{32,16},{48,32},{64,48},{80,64},{96,80},{112,96},{1... | collective-permute-start | bytes 393224 | tf_op jit(solution)/shard_map/ppermute | solution.py:272
  38.1 3.3 %part.3.refs_4_ = f32[2048,1024]{1,0:T(8,128)S(1)} custom-call(s32[16]{0:T(128)S(1)} %fusion.19.pair_ref, s32[8,16,1,64]{3,2,1,0:T(1,128)S(1)} %broadcast_add_fusion.code_ref, bf16[2048,512]{1,0:T(8,128)(2,1)S(1)} %get-tuple-element.34.turn_ref, bf16[512,128]{1,0:T(8,128)(2,1)S(1)} %pad_maximum_fusion.2.refs_0_, ...), custom_call_target="tpu_custom_call" | custom-call | tf_op jit(solution)/shard_map/part/pallas_call | solution.py:179
  41.4 3.4 %collective-permute-start.8 = (bf16[512,128]{1,0:T(8,128)(2,1)S(1)}, bf16[512,128]{1,0:T(8,128)(2,1)S(1)}, u32[]{:S(2)}, u32[]{:S(2)}) collective-permute-start(bf16[512,128]{1,0:T(8,128)(2,1)S(1)} %collective-permute-done.1.refs_2_), channel_id=1, source_target_pairs={{0,8},{8,0},{1,9},{9,1},{2,10},{10,2},{3,11},{11,3},{4,12},{12,4},... | collective-permute-start | bytes 393224 | tf_op jit(solution)/shard_map/ppermute | solution.py:278
  45.0 2.7 %collective-permute-start.7 = (bf16[512,128]{1,0:T(8,128)(2,1)S(1)}, bf16[512,128]{1,0:T(8,128)(2,1)S(1)}, u32[]{:S(2)}, u32[]{:S(2)}) collective-permute-start(bf16[512,128]{1,0:T(8,128)(2,1)S(1)} %collective-permute-done.4.refs_3_), channel_id=1, source_target_pairs={{0,112},{16,0},{32,16},{48,32},{64,48},{80,64},{96,80},{112,96},{1... | collective-permute-start | bytes 393224 | tf_op jit(solution)/shard_map/ppermute | solution.py:272
  47.6 3.5 %part.4.refs_4_ = f32[2048,1024]{1,0:T(8,128)S(1)} custom-call(s32[16]{0:T(128)S(1)} %fusion.19.pair_ref, s32[8,16,1,64]{3,2,1,0:T(1,128)S(1)} %broadcast_add_fusion.code_ref, bf16[2048,512]{1,0:T(8,128)(2,1)S(1)} %get-tuple-element.39.turn_ref, bf16[512,128]{1,0:T(8,128)(2,1)S(1)} %collective-permute-done.8.refs_0_, ...), custom_call_target="tpu_custom_call", output_to_operand_aliasing={{}: (7, {})} | custom-call | tf_op jit(solution)/shard_map/part/pallas_call | solution.py:179
  51.1 1.1 %collective-permute-start.14 = (bf16[512,128]{1,0:T(8,128)(2,1)S(1)}, bf16[512,128]{1,0:T(8,128)(2,1)S(1)}, u32[]{:S(2)}, u32[]{:S(2)}) collective-permute-start(bf16[512,128]{1,0:T(8,128)(2,1)S(1)} %collective-permute-done.3.refs_2_), channel_id=1, source_target_pairs={{0,8},{8,0},{1,9},{9,1},{2,10},{10,2},{3,11},{11,3},{4,12},{12,4},... | collective-permute-start | bytes 393224 | tf_op jit(solution)/shard_map/ppermute | solution.py:278
  52.3 0.5 collective-permute-start.12
  52.8 2.7 %collective-permute-start.13 = (bf16[512,128]{1,0:T(8,128)(2,1)S(1)}, bf16[512,128]{1,0:T(8,128)(2,1)S(1)}, u32[]{:S(2)}, u32[]{:S(2)}) collective-permute-start(bf16[512,128]{1,0:T(8,128)(2,1)S(1)} %collective-permute-done.7.refs_3_), channel_id=1, source_target_pairs={{0,120},{8,112},{16,8},{24,0},{32,24},{40,16},{48,40},{56,32},{64,... | collective-permute-start | bytes 393224 | tf_op jit(solution)/shard_map/ppermute | solution.py:289
  55.5 0.5 collective-permute-start.11
  56.1 3.5 %part.5.refs_4_ = f32[2048,1024]{1,0:T(8,128)S(1)} custom-call(s32[16]{0:T(128)S(1)} %fusion.19.pair_ref, s32[8,16,1,64]{3,2,1,0:T(1,128)S(1)} %broadcast_add_fusion.code_ref, bf16[2048,512]{1,0:T(8,128)(2,1)S(1)} %get-tuple-element.46.turn_ref, bf16[512,128]{1,0:T(8,128)(2,1)S(1)} %collective-permute-done.14.refs_0_, ...), custom_call_target="tpu_custom_call", output_to_operand_aliasing={{}: (7, {})} | custom-call | tf_op jit(solution)/shard_map/part/pallas_call | solution.py:179
  59.6 4.6 %last.1 = bf16[1024,2,1024]{2,1,0:T(2,128)(2,1)} custom-call(s32[16]{0:T(128)S(1)} %fusion.19.pair_ref, s32[8,16,1,64]{3,2,1,0:T(1,128)S(1)} %broadcast_add_fusion.code_ref, bf16[2048,512]{1,0:T(8,128)(2,1)S(1)} %get-tuple-element.29.turn_ref, bf16[512,128]{1,0:T(8,128)(2,1)S(1)} %collective-permute-done.10.refs_0_, ...), custom_call_target="tpu_custom_call" | custom-call | tf_op jit(solution)/shard_map/last/pallas_call | solution.py:192
  (43 shorter events, 1.3 us)
Async XLA Ops:
  0.0 0.7 %copy-start = (s32[64,32]{0,1:T(8,128)S(1)}, s32[64,32]{0,1:T(8,128)}, u32[]{:S(2)}) copy-start(s32[64,32]{0,1:T(8,128)} %param.11) | copy-start | bytes 24580
  6.2 14.6 %all-to-all-start = ((bf16[8,256,128]{2,1,0:T(8,128)(2,1)}), bf16[8,256,128]{2,1,0:T(8,128)(2,1)S(1)}, u32[]{:S(2)}, u32[]{:S(2)}) async-start(bf16[8,256,128]{2,1,0:T(8,128)(2,1)} %bitcast.6), calls=%async_computation | async-start | bytes 1048576 | tf_op jit(solution)/shard_map/all_to_all | solution.py:235
  21.7 4.8 %collective-permute-start = (bf16[256,128]{1,0:T(8,128)(2,1)S(1)}, bf16[256,128]{1,0:T(8,128)(2,1)S(1)}, u32[]{:S(2)}, u32[]{:S(2)}) collective-permute-start(bf16[256,128]{1,0:T(8,128)(2,1)S(1)} %focus.1), channel_id=1, source_target_pairs={{0,128},{128,0},{1,129},{129,1},{2,130},{130,2},{3,131},{131,3},{4... | collective-permute-start | bytes 196616 | tf_op jit(solution)/shard_map/ppermute | solution.py:265
  26.5 8.8 %collective-permute-start.1 = (bf16[512,128]{1,0:T(8,128)(2,1)S(1)}, bf16[512,128]{1,0:T(8,128)(2,1)S(1)}, u32[]{:S(2)}, u32[]{:S(2)}) collective-permute-start(bf16[512,128]{1,0:T(8,128)(2,1)S(1)} %pad_maximum_fusion.2.refs_0_), channel_id=1, source_target_pairs={{0,16},{16,32},{32,48},{48,64},{64,80},{80,96},{96,112},{112,0},{1... | collective-permute-start | bytes 393224 | tf_op jit(solution)/shard_map/ppermute | solution.py:272
  28.2 7.1 %collective-permute-start.2 = (bf16[512,128]{1,0:T(8,128)(2,1)S(1)}, bf16[512,128]{1,0:T(8,128)(2,1)S(1)}, u32[]{:S(2)}, u32[]{:S(2)}) collective-permute-start(bf16[512,128]{1,0:T(8,128)(2,1)S(1)} %pad_maximum_fusion.2.refs_0_), channel_id=1, source_target_pairs={{0,112},{16,0},{32,16},{48,32},{64,48},{80,64},{96,80},{112,96},{1... | collective-permute-start | bytes 393224 | tf_op jit(solution)/shard_map/ppermute | solution.py:272
  32.2 5.9 %collective-permute-start.5 = (bf16[512,128]{1,0:T(8,128)(2,1)S(1)}, bf16[512,128]{1,0:T(8,128)(2,1)S(1)}, u32[]{:S(2)}, u32[]{:S(2)}) collective-permute-start(bf16[512,128]{1,0:T(8,128)(2,1)S(1)} %pad_maximum_fusion.2.refs_0_), channel_id=1, source_target_pairs={{0,8},{8,0},{1,9},{9,1},{2,10},{10,2},{3,11},{11,3},{4,12},{12,4},... | collective-permute-start | bytes 393224 | tf_op jit(solution)/shard_map/ppermute | solution.py:281
  35.3 9.6 %collective-permute-start.3 = (bf16[512,128]{1,0:T(8,128)(2,1)S(1)}, bf16[512,128]{1,0:T(8,128)(2,1)S(1)}, u32[]{:S(2)}, u32[]{:S(2)}) collective-permute-start(bf16[512,128]{1,0:T(8,128)(2,1)S(1)} %collective-permute-done.1.refs_2_), channel_id=1, source_target_pairs={{0,16},{16,32},{32,48},{48,64},{64,80},{80,96},{96,112},{112,0},{1... | collective-permute-start | bytes 393224 | tf_op jit(solution)/shard_map/ppermute | solution.py:272
  35.4 9.5 %collective-permute-start.4 = (bf16[512,128]{1,0:T(8,128)(2,1)S(1)}, bf16[512,128]{1,0:T(8,128)(2,1)S(1)}, u32[]{:S(2)}, u32[]{:S(2)}) collective-permute-start(bf16[512,128]{1,0:T(8,128)(2,1)S(1)} %collective-permute-done.2.refs_3_), channel_id=1, source_target_pairs={{0,112},{16,0},{32,16},{48,32},{64,48},{80,64},{96,80},{112,96},{1... | collective-permute-start | bytes 393224 | tf_op jit(solution)/shard_map/ppermute | solution.py:272
  41.4 6.2 %collective-permute-start.8 = (bf16[512,128]{1,0:T(8,128)(2,1)S(1)}, bf16[512,128]{1,0:T(8,128)(2,1)S(1)}, u32[]{:S(2)}, u32[]{:S(2)}) collective-permute-start(bf16[512,128]{1,0:T(8,128)(2,1)S(1)} %collective-permute-done.1.refs_2_), channel_id=1, source_target_pairs={{0,8},{8,0},{1,9},{9,1},{2,10},{10,2},{3,11},{11,3},{4,12},{12,4},... | collective-permute-start | bytes 393224 | tf_op jit(solution)/shard_map/ppermute | solution.py:278
  44.8 2.8 %collective-permute-start.9 = (bf16[512,128]{1,0:T(8,128)(2,1)S(1)}, bf16[512,128]{1,0:T(8,128)(2,1)S(1)}, u32[]{:S(2)}, u32[]{:S(2)}) collective-permute-start(bf16[512,128]{1,0:T(8,128)(2,1)S(1)} %collective-permute-done.2.refs_3_), channel_id=1, source_target_pairs={{0,8},{8,0},{1,9},{9,1},{2,10},{10,2},{3,11},{11,3},{4,12},{12,4},... | collective-permute-start | bytes 393224 | tf_op jit(solution)/shard_map/ppermute | solution.py:278
  44.9 7.3 %collective-permute-start.6 = (bf16[512,128]{1,0:T(8,128)(2,1)S(1)}, bf16[512,128]{1,0:T(8,128)(2,1)S(1)}, u32[]{:S(2)}, u32[]{:S(2)}) collective-permute-start(bf16[512,128]{1,0:T(8,128)(2,1)S(1)} %collective-permute-done.3.refs_2_), channel_id=1, source_target_pairs={{0,16},{16,32},{32,48},{48,64},{64,80},{80,96},{96,112},{112,0},{1... | collective-permute-start | bytes 393224 | tf_op jit(solution)/shard_map/ppermute | solution.py:272
  45.0 7.3 %collective-permute-start.7 = (bf16[512,128]{1,0:T(8,128)(2,1)S(1)}, bf16[512,128]{1,0:T(8,128)(2,1)S(1)}, u32[]{:S(2)}, u32[]{:S(2)}) collective-permute-start(bf16[512,128]{1,0:T(8,128)(2,1)S(1)} %collective-permute-done.4.refs_3_), channel_id=1, source_target_pairs={{0,112},{16,0},{32,16},{48,32},{64,48},{80,64},{96,80},{112,96},{1... | collective-permute-start | bytes 393224 | tf_op jit(solution)/shard_map/ppermute | solution.py:272
  51.1 4.4 %collective-permute-start.14 = (bf16[512,128]{1,0:T(8,128)(2,1)S(1)}, bf16[512,128]{1,0:T(8,128)(2,1)S(1)}, u32[]{:S(2)}, u32[]{:S(2)}) collective-permute-start(bf16[512,128]{1,0:T(8,128)(2,1)S(1)} %collective-permute-done.3.refs_2_), channel_id=1, source_target_pairs={{0,8},{8,0},{1,9},{9,1},{2,10},{10,2},{3,11},{11,3},{4,12},{12,4},... | collective-permute-start | bytes 393224 | tf_op jit(solution)/shard_map/ppermute | solution.py:278
  52.2 3.9 %collective-permute-start.15 = (bf16[512,128]{1,0:T(8,128)(2,1)S(1)}, bf16[512,128]{1,0:T(8,128)(2,1)S(1)}, u32[]{:S(2)}, u32[]{:S(2)}) collective-permute-start(bf16[512,128]{1,0:T(8,128)(2,1)S(1)} %collective-permute-done.4.refs_3_), channel_id=1, source_target_pairs={{0,8},{8,0},{1,9},{9,1},{2,10},{10,2},{3,11},{11,3},{4,12},{12,4},... | collective-permute-start | bytes 393224 | tf_op jit(solution)/shard_map/ppermute | solution.py:278
  52.3 7.3 %collective-permute-start.12 = (bf16[512,128]{1,0:T(8,128)(2,1)S(1)}, bf16[512,128]{1,0:T(8,128)(2,1)S(1)}, u32[]{:S(2)}, u32[]{:S(2)}) collective-permute-start(bf16[512,128]{1,0:T(8,128)(2,1)S(1)} %collective-permute-done.6.refs_2_), channel_id=1, source_target_pairs={{0,16},{16,32},{32,48},{48,64},{64,80},{80,96},{96,112},{112,0},{1... | collective-permute-start | bytes 393224 | tf_op jit(solution)/shard_map/ppermute | solution.py:285
  52.8 6.8 %collective-permute-start.13 = (bf16[512,128]{1,0:T(8,128)(2,1)S(1)}, bf16[512,128]{1,0:T(8,128)(2,1)S(1)}, u32[]{:S(2)}, u32[]{:S(2)}) collective-permute-start(bf16[512,128]{1,0:T(8,128)(2,1)S(1)} %collective-permute-done.7.refs_3_), channel_id=1, source_target_pairs={{0,120},{8,112},{16,8},{24,0},{32,24},{40,16},{48,40},{56,32},{64,... | collective-permute-start | bytes 393224 | tf_op jit(solution)/shard_map/ppermute | solution.py:289
  55.5 4.0 %collective-permute-start.10 = (bf16[512,128]{1,0:T(8,128)(2,1)S(1)}, bf16[512,128]{1,0:T(8,128)(2,1)S(1)}, u32[]{:S(2)}, u32[]{:S(2)}) collective-permute-start(bf16[512,128]{1,0:T(8,128)(2,1)S(1)} %collective-permute-done.6.refs_2_), channel_id=1, source_target_pairs={{0,8},{8,0},{1,9},{9,1},{2,10},{10,2},{3,11},{11,3},{4,12},{12,4},... | collective-permute-start | bytes 393224 | tf_op jit(solution)/shard_map/ppermute | solution.py:290
  55.5 4.0 %collective-permute-start.11 = (bf16[512,128]{1,0:T(8,128)(2,1)S(1)}, bf16[512,128]{1,0:T(8,128)(2,1)S(1)}, u32[]{:S(2)}, u32[]{:S(2)}) collective-permute-start(bf16[512,128]{1,0:T(8,128)(2,1)S(1)} %collective-permute-done.7.refs_3_), channel_id=1, source_target_pairs={{0,8},{8,0},{1,9},{9,1},{2,10},{10,2},{3,11},{11,3},{4,12},{12,4},... | collective-permute-start | bytes 393224 | tf_op jit(solution)/shard_map/ppermute | solution.py:290

commit v6 on v5

--- a/solution.py
+++ b/solution.py
@@ -22,7 +22,7 @@
     tiles, per_block = word_ref.shape
     _, parts, lanes = bins_ref.shape
     lane = lax.broadcasted_iota(jnp.int32, (parts, lanes), 1)
-    at_once = 4
+    at_once = 8
 
     def take(step, _):
         for u in range(at_once):
@@ -62,10 +62,10 @@
 def focus_kernel(back_ref, got_ref, turned_ref, out_ref, panels):
     tiles, per_block = back_ref.shape
     rows = out_ref.shape[0] // tiles
-    total = got_ref[0].astype(jnp.float32)
+    total = got_ref[0]
     for source in range(1, got_ref.shape[0]):
-        total += got_ref[source].astype(jnp.float32)
-    panels[...] = total
+        total += got_ref[source]
+    panels[...] = total.astype(jnp.float32)
     for tile in range(tiles):
         windows = []
         for entry in range(per_block):
@@ -142,7 +142,7 @@
     blocks, rest = refs[:n_blocks], refs[n_blocks:]
     total_ref, spread = rest[-2:]
     place(pair_ref, code_ref, blocks, first, spread)
-    rows = 512
+    rows = 1024
     for start in range(0, turn_ref.shape[0], rows):
         here = slice(start, start + rows)
         new = jnp.dot(turn_ref[here, :], spread[...], preferred_element_type=jnp.float32)

time: 64.8 us -> 64.5 us (level)
  no operation moved by 1% of the time
where the time goes in v6:
time: 64.5 us; the launch traced here: 64 us
  starting transfers between devices  31.2 us (48%)
  Pallas kernels  20.9 us (32%)
  local copies, waits for them, and re-layouts  5.31 us (8%)
  other arithmetic  4.62 us (7%)
  waiting for transfers between devices  1.57 us (2%)
    pallas_call x3, Pallas kernels, part(): pl.pallas_call(functools.partial(part_kernel, first=first, n_blocks=len(b...  9.99 us
    ppermute x3, starting transfers between devices, body(): lax.ppermute(backward, 'z', behind)  9.35 us
    all_to_all x1, starting transfers between devices, body(): lax.all_to_all(packed.reshape(n_rows, -1, LANES), ROW, 0, 0, tiled=True)  5.86 us
    ppermute x4, starting transfers between devices, body(): far = [lax.ppermute(block, 'core', swap) for block in leaving]  4.71 us
    pallas_call x1, Pallas kernels, part(): pl.pallas_call(functools.partial(last_kernel, first=first, n_blocks=len(b...  4.58 us
    ppermute x3, starting transfers between devices, body(): far = [lax.ppermute(block, 'core', swap) for block in near]  3.54 us
    pallas_call x1, Pallas kernels, pack(): pl.pallas_call(pack_kernel, out_shape=jax.ShapeDtypeStruct((tiles * per_b...  3.36 us
    ppermute x1, starting transfers between devices, body(): across = lax.ppermute(backward, ('z', 'core'), crossing)  2.72 us
  transfers between devices with their start and end apart: 17, of which 1 were waited for; matrix products, arithmetic and copies ran while one was open for 11% of the time, Pallas kernels for 19%

profile of v6, /device:TPU:1, one launch (start us, length us, event | category | flops | bytes accessed | tf_op | source)
XLA Modules:
  0.0 64.0 jit_solution(15713299153167454466)
XLA Ops:
  0.0 0.7 %copy-done = s32[64,32]{0,1:T(8,128)S(1)} copy-done((s32[64,32]{0,1:T(8,128)S(1)}, s32[64,32]{0,1:T(8,128)}, u32[]{:S(2)}) %copy-start) | copy-done | bytes 8216
  0.7 1.2 %pad.4 = bf16[32,18,2,128]{3,2,1,0:T(2,128)(2,1)S(1)} pad(bf16[32,16,2,128]{3,2,1,0:T(2,128)(2,1)} %bitcast.14, bf16[]{:T(256)} %constant.139.clone.1), padding=0_0x1_1x0_0x0_0 | pad | bytes 557058 | tf_op jit(solution)/shard_map/jit(_pad)/pad | solution.py:46
  1.9 0.9 %and_add_fusion.word_ref = s32[64,16]{1,0:T(8,128)S(1)} fusion(s32[64,512]{1,0:T(8,128)} %param.9, s32[]{:T(128)S(6)} %select_n.104, s32[64,512]{1,0:T(8,128)} %param.10, s32[]{:T(128)S(6)} %mul.193, s32[]{:T(128)S(6)} %mul.192, s32[64]{0:T(128)S(1)} %fusion.20), kind=kLoop, calls=%fused_computation.29 | loop fusion | flops 15360 | bytes 12556 | tf_op jit(solution)/shard_map/add | solution.py:51
  2.8 3.4 %pack.1 = bf16[1024,2,128]{2,1,0:T(2,128)(2,1)} custom-call(s32[64,16]{1,0:T(8,128)S(1)} %and_add_fusion.word_ref, bf16[576,2,128]{2,1,0:T(2,128)(2,1)S(1)} %bitcast.11), custom_call_target="tpu_custom_call" | custom-call | tf_op jit(solution)/shard_map/pack/pallas_call | solution.py:52
  6.1 5.9 %all-to-all-start = ((bf16[8,256,128]{2,1,0:T(8,128)(2,1)}), bf16[8,256,128]{2,1,0:T(8,128)(2,1)S(1)}, u32[]{:S(2)}, u32[]{:S(2)}) async-start(bf16[8,256,128]{2,1,0:T(8,128)(2,1)} %bitcast.6), calls=%async_computation | async-start | bytes 1048576 | tf_op jit(solution)/shard_map/all_to_all | solution.py:235
  12.0 1.1 %copy.20 = bf16[8,128,128]{1,2,0:T(8,128)(2,1)S(1)} copy(bf16[8,128,128]{2,1,0:T(8,128)(2,1)} %param.13) | data formatting | bytes 524288 | tf_op args[5]
  13.2 0.7 %fusion.19.pair_ref = s32[16]{0:T(128)S(1)} fusion(s32[16]{0:T(128)} %constant.140.clone, s32[16]{0:T(128)} %constant.141.clone, s32[]{:T(128)S(6)} %axis_index.36, s32[]{:T(128)S(6)} %axis_index.33), kind=kLoop, calls=%fused_computation.52 | loop fusion | flops 240 | bytes 200 | tf_op jit(solution)/shard_map/add | solution.py:248
  14.1 0.8 %broadcast_in_dim.41 = s32[32,32]{1,0:T(8,128)S(1)} reshape(s32[1024]{0:T(1024)} %param.12) | data formatting | bytes 8192 | tf_op jit(solution)/shard_map/jit(_where)/broadcast_in_dim | solution.py:205
  14.8 0.2 select_reduce_fusion
  15.2 0.6 fusion.12
  15.8 0.2 broadcast_in_dim.44.coarse_ref
  16.0 0.7 %constant_dynamic-slice_fusion.1 = s32[8,512]{1,0:T(8,128)S(1)} fusion(s32[64,512]{1,0:T(8,128)} %param.9, s32[]{:T(128)S(6)} %select_n.96), kind=kLoop, calls=%fused_computation.47 | loop fusion | bytes 32772 | tf_op jit(solution)/shard_map/dynamic_slice | solution.py:250
  17.3 0.8 %negate_and_fusion.back_ref = s32[8,16]{1,0:T(8,128)S(1)} fusion(s32[64,512]{1,0:T(8,128)} %param.10, s32[]{:T(128)S(6)} %select_n.96, s32[]{:T(128)S(6)} %select_n.104), kind=kLoop, calls=%fused_computation.36 | loop fusion | flops 256 | bytes 1032 | tf_op jit(solution)/shard_map/and | solution.py:237
  18.1 1.1 %fusion.4 = (f32[1,64,1024]{2,1,0:T(8,128)S(1)}, f32[1,64,1024]{2,1,0:T(8,128)S(1)}) fusion(s32[64]{0:T(128)S(1)} %get-tuple-element.58, s32[64]{0:T(128)S(1)} %get-tuple-element.57, s32[1024]{0:T(1024)S(1)} %mul.173), kind=kLoop, calls=%fused_computation.19 | loop fusion | flops 983040 | bytes 528896 | tf_op jit(solution)/shard_map/cos | solution.py:216
  19.2 1.5 %all-to-all-done.got_ref = bf16[8,256,128]{2,1,0:T(8,128)(2,1)S(1)} async-done(((bf16[8,256,128]{2,1,0:T(8,128)(2,1)}), bf16[8,256,128]{2,1,0:T(8,128)(2,1)S(1)}, u32[]{:S(2)}, u32[]{:S(2)}) %all-to-all-start) | async-done | bytes 524320 | tf_op jit(solution)/shard_map/all_to_all | solution.py:235
  20.7 0.9 %focus.1 = bf16[256,128]{1,0:T(8,128)(2,1)S(1)} custom-call(s32[8,16]{1,0:T(8,128)S(1)} %negate_and_fusion.back_ref, bf16[8,256,128]{2,1,0:T(8,128)(2,1)S(1)} %all-to-all-done.got_ref, bf16[8,128,128]{2,1,0:T(8,128)(2,1)S(1)} %bitcast.12), custom_call_target="tpu_custom_call" | custom-call | tf_op jit(solution)/shard_map/focus/pallas_call | solution.py:82
  21.6 2.7 %collective-permute-start = (bf16[256,128]{1,0:T(8,128)(2,1)S(1)}, bf16[256,128]{1,0:T(8,128)(2,1)S(1)}, u32[]{:S(2)}, u32[]{:S(2)}) collective-permute-start(bf16[256,128]{1,0:T(8,128)(2,1)S(1)} %focus.1), channel_id=1, source_target_pairs={{0,128},{128,0},{1,129},{129,1},{2,130},{130,2},{3,131},{131,3},{4... | collective-permute-start | bytes 196616 | tf_op jit(solution)/shard_map/ppermute | solution.py:265
  24.4 2.1 %turns.1 = (f32[8,128]{1,0:T(8,128)S(1)}, bf16[2048,512]{1,0:T(8,128)(2,1)S(1)}, bf16[2048,512]{1,0:T(8,128)(2,1)S(1)}, bf16[2048,512]{1,0:T(8,128)(2,1)S(1)}, bf16[2048,512]{1,0:T(8,128)(2,1)S(1)}) custom-call(f32[2,32,1,1024]{3,2,1,0:T(1,128)S(1)} %broadcast_in_dim.44.coarse_ref, f32[2,64,1024]{2,1,0:T(8,128)S(1)} %pad_maximum_fusion.fine_ref), custom_call_target="tpu_custom_call" | custom-call | tf_op jit(solution)/shard_map/turns/pallas_call | solution.py:132
  26.5 1.7 %collective-permute-start.1 = (bf16[512,128]{1,0:T(8,128)(2,1)S(1)}, bf16[512,128]{1,0:T(8,128)(2,1)S(1)}, u32[]{:S(2)}, u32[]{:S(2)}) collective-permute-start(bf16[512,128]{1,0:T(8,128)(2,1)S(1)} %pad_maximum_fusion.2.refs_0_), channel_id=1, source_target_pairs={{0,16},{16,32},{32,48},{48,64},{64,80},{80,96},{96,112},{112,0},{1... | collective-permute-start | bytes 393224 | tf_op jit(solution)/shard_map/ppermute | solution.py:272
  28.2 4.0 %collective-permute-start.2 = (bf16[512,128]{1,0:T(8,128)(2,1)S(1)}, bf16[512,128]{1,0:T(8,128)(2,1)S(1)}, u32[]{:S(2)}, u32[]{:S(2)}) collective-permute-start(bf16[512,128]{1,0:T(8,128)(2,1)S(1)} %pad_maximum_fusion.2.refs_0_), channel_id=1, source_target_pairs={{0,112},{16,0},{32,16},{48,32},{64,48},{80,64},{96,80},{112,96},{1... | collective-permute-start | bytes 393224 | tf_op jit(solution)/shard_map/ppermute | solution.py:272
  32.2 3.0 %collective-permute-start.5 = (bf16[512,128]{1,0:T(8,128)(2,1)S(1)}, bf16[512,128]{1,0:T(8,128)(2,1)S(1)}, u32[]{:S(2)}, u32[]{:S(2)}) collective-permute-start(bf16[512,128]{1,0:T(8,128)(2,1)S(1)} %pad_maximum_fusion.2.refs_0_), channel_id=1, source_target_pairs={{0,8},{8,0},{1,9},{9,1},{2,10},{10,2},{3,11},{11,3},{4,12},{12,4},... | collective-permute-start | bytes 393224 | tf_op jit(solution)/shard_map/ppermute | solution.py:281
  35.4 2.7 %collective-permute-start.4 = (bf16[512,128]{1,0:T(8,128)(2,1)S(1)}, bf16[512,128]{1,0:T(8,128)(2,1)S(1)}, u32[]{:S(2)}, u32[]{:S(2)}) collective-permute-start(bf16[512,128]{1,0:T(8,128)(2,1)S(1)} %collective-permute-done.2.refs_3_), channel_id=1, source_target_pairs={{0,112},{16,0},{32,16},{48,32},{64,48},{80,64},{96,80},{112,96},{1... | collective-permute-start | bytes 393224 | tf_op jit(solution)/shard_map/ppermute | solution.py:272
  38.1 3.2 %part.3.refs_4_ = f32[2048,1024]{1,0:T(8,128)S(1)} custom-call(s32[16]{0:T(128)S(1)} %fusion.19.pair_ref, s32[8,16,1,64]{3,2,1,0:T(1,128)S(1)} %broadcast_add_fusion.code_ref, bf16[2048,512]{1,0:T(8,128)(2,1)S(1)} %get-tuple-element.34.turn_ref, bf16[512,128]{1,0:T(8,128)(2,1)S(1)} %pad_maximum_fusion.2.refs_0_, ...), custom_call_target="tpu_custom_call" | custom-call | tf_op jit(solution)/shard_map/part/pallas_call | solution.py:179
  41.3 3.5 %collective-permute-start.8 = (bf16[512,128]{1,0:T(8,128)(2,1)S(1)}, bf16[512,128]{1,0:T(8,128)(2,1)S(1)}, u32[]{:S(2)}, u32[]{:S(2)}) collective-permute-start(bf16[512,128]{1,0:T(8,128)(2,1)S(1)} %collective-permute-done.1.refs_2_), channel_id=1, source_target_pairs={{0,8},{8,0},{1,9},{9,1},{2,10},{10,2},{3,11},{11,3},{4,12},{12,4},... | collective-permute-start | bytes 393224 | tf_op jit(solution)/shard_map/ppermute | solution.py:278
  44.9 2.7 %collective-permute-start.7 = (bf16[512,128]{1,0:T(8,128)(2,1)S(1)}, bf16[512,128]{1,0:T(8,128)(2,1)S(1)}, u32[]{:S(2)}, u32[]{:S(2)}) collective-permute-start(bf16[512,128]{1,0:T(8,128)(2,1)S(1)} %collective-permute-done.4.refs_3_), channel_id=1, source_target_pairs={{0,112},{16,0},{32,16},{48,32},{64,48},{80,64},{96,80},{112,96},{1... | collective-permute-start | bytes 393224 | tf_op jit(solution)/shard_map/ppermute | solution.py:272
  47.6 3.4 %part.4.refs_4_ = f32[2048,1024]{1,0:T(8,128)S(1)} custom-call(s32[16]{0:T(128)S(1)} %fusion.19.pair_ref, s32[8,16,1,64]{3,2,1,0:T(1,128)S(1)} %broadcast_add_fusion.code_ref, bf16[2048,512]{1,0:T(8,128)(2,1)S(1)} %get-tuple-element.39.turn_ref, bf16[512,128]{1,0:T(8,128)(2,1)S(1)} %collective-permute-done.8.refs_0_, ...), custom_call_target="tpu_custom_call", output_to_operand_aliasing={{}: (7, {})} | custom-call | tf_op jit(solution)/shard_map/part/pallas_call | solution.py:179
  50.9 1.1 %collective-permute-start.14 = (bf16[512,128]{1,0:T(8,128)(2,1)S(1)}, bf16[512,128]{1,0:T(8,128)(2,1)S(1)}, u32[]{:S(2)}, u32[]{:S(2)}) collective-permute-start(bf16[512,128]{1,0:T(8,128)(2,1)S(1)} %collective-permute-done.3.refs_2_), channel_id=1, source_target_pairs={{0,8},{8,0},{1,9},{9,1},{2,10},{10,2},{3,11},{11,3},{4,12},{12,4},... | collective-permute-start | bytes 393224 | tf_op jit(solution)/shard_map/ppermute | solution.py:278
  52.1 0.5 collective-permute-start.12
  52.6 2.7 %collective-permute-start.13 = (bf16[512,128]{1,0:T(8,128)(2,1)S(1)}, bf16[512,128]{1,0:T(8,128)(2,1)S(1)}, u32[]{:S(2)}, u32[]{:S(2)}) collective-permute-start(bf16[512,128]{1,0:T(8,128)(2,1)S(1)} %collective-permute-done.7.refs_3_), channel_id=1, source_target_pairs={{0,120},{8,112},{16,8},{24,0},{32,24},{40,16},{48,40},{56,32},{64,... | collective-permute-start | bytes 393224 | tf_op jit(solution)/shard_map/ppermute | solution.py:289
  55.4 0.5 collective-permute-start.11
  55.9 3.4 %part.5.refs_4_ = f32[2048,1024]{1,0:T(8,128)S(1)} custom-call(s32[16]{0:T(128)S(1)} %fusion.19.pair_ref, s32[8,16,1,64]{3,2,1,0:T(1,128)S(1)} %broadcast_add_fusion.code_ref, bf16[2048,512]{1,0:T(8,128)(2,1)S(1)} %get-tuple-element.46.turn_ref, bf16[512,128]{1,0:T(8,128)(2,1)S(1)} %collective-permute-done.14.refs_0_, ...), custom_call_target="tpu_custom_call", output_to_operand_aliasing={{}: (7, {})} | custom-call | tf_op jit(solution)/shard_map/part/pallas_call | solution.py:179
  59.3 4.6 %last.1 = bf16[1024,2,1024]{2,1,0:T(2,128)(2,1)} custom-call(s32[16]{0:T(128)S(1)} %fusion.19.pair_ref, s32[8,16,1,64]{3,2,1,0:T(1,128)S(1)} %broadcast_add_fusion.code_ref, bf16[2048,512]{1,0:T(8,128)(2,1)S(1)} %get-tuple-element.29.turn_ref, bf16[512,128]{1,0:T(8,128)(2,1)S(1)} %collective-permute-done.10.refs_0_, ...), custom_call_target="tpu_custom_call" | custom-call | tf_op jit(solution)/shard_map/last/pallas_call | solution.py:192
  (43 shorter events, 1.3 us)
Async XLA Ops:
  0.0 0.7 %copy-start = (s32[64,32]{0,1:T(8,128)S(1)}, s32[64,32]{0,1:T(8,128)}, u32[]{:S(2)}) copy-start(s32[64,32]{0,1:T(8,128)} %param.11) | copy-start | bytes 24580
  6.1 14.6 %all-to-all-start = ((bf16[8,256,128]{2,1,0:T(8,128)(2,1)}), bf16[8,256,128]{2,1,0:T(8,128)(2,1)S(1)}, u32[]{:S(2)}, u32[]{:S(2)}) async-start(bf16[8,256,128]{2,1,0:T(8,128)(2,1)} %bitcast.6), calls=%async_computation | async-start | bytes 1048576 | tf_op jit(solution)/shard_map/all_to_all | solution.py:235
  21.6 4.8 %collective-permute-start = (bf16[256,128]{1,0:T(8,128)(2,1)S(1)}, bf16[256,128]{1,0:T(8,128)(2,1)S(1)}, u32[]{:S(2)}, u32[]{:S(2)}) collective-permute-start(bf16[256,128]{1,0:T(8,128)(2,1)S(1)} %focus.1), channel_id=1, source_target_pairs={{0,128},{128,0},{1,129},{129,1},{2,130},{130,2},{3,131},{131,3},{4... | collective-permute-start | bytes 196616 | tf_op jit(solution)/shard_map/ppermute | solution.py:265
  26.5 8.8 %collective-permute-start.1 = (bf16[512,128]{1,0:T(8,128)(2,1)S(1)}, bf16[512,128]{1,0:T(8,128)(2,1)S(1)}, u32[]{:S(2)}, u32[]{:S(2)}) collective-permute-start(bf16[512,128]{1,0:T(8,128)(2,1)S(1)} %pad_maximum_fusion.2.refs_0_), channel_id=1, source_target_pairs={{0,16},{16,32},{32,48},{48,64},{64,80},{80,96},{96,112},{112,0},{1... | collective-permute-start | bytes 393224 | tf_op jit(solution)/shard_map/ppermute | solution.py:272
  28.2 7.1 %collective-permute-start.2 = (bf16[512,128]{1,0:T(8,128)(2,1)S(1)}, bf16[512,128]{1,0:T(8,128)(2,1)S(1)}, u32[]{:S(2)}, u32[]{:S(2)}) collective-permute-start(bf16[512,128]{1,0:T(8,128)(2,1)S(1)} %pad_maximum_fusion.2.refs_0_), channel_id=1, source_target_pairs={{0,112},{16,0},{32,16},{48,32},{64,48},{80,64},{96,80},{112,96},{1... | collective-permute-start | bytes 393224 | tf_op jit(solution)/shard_map/ppermute | solution.py:272
  32.2 5.9 %collective-permute-start.5 = (bf16[512,128]{1,0:T(8,128)(2,1)S(1)}, bf16[512,128]{1,0:T(8,128)(2,1)S(1)}, u32[]{:S(2)}, u32[]{:S(2)}) collective-permute-start(bf16[512,128]{1,0:T(8,128)(2,1)S(1)} %pad_maximum_fusion.2.refs_0_), channel_id=1, source_target_pairs={{0,8},{8,0},{1,9},{9,1},{2,10},{10,2},{3,11},{11,3},{4,12},{12,4},... | collective-permute-start | bytes 393224 | tf_op jit(solution)/shard_map/ppermute | solution.py:281
  35.3 9.6 %collective-permute-start.3 = (bf16[512,128]{1,0:T(8,128)(2,1)S(1)}, bf16[512,128]{1,0:T(8,128)(2,1)S(1)}, u32[]{:S(2)}, u32[]{:S(2)}) collective-permute-start(bf16[512,128]{1,0:T(8,128)(2,1)S(1)} %collective-permute-done.1.refs_2_), channel_id=1, source_target_pairs={{0,16},{16,32},{32,48},{48,64},{64,80},{80,96},{96,112},{112,0},{1... | collective-permute-start | bytes 393224 | tf_op jit(solution)/shard_map/ppermute | solution.py:272
  35.4 9.5 %collective-permute-start.4 = (bf16[512,128]{1,0:T(8,128)(2,1)S(1)}, bf16[512,128]{1,0:T(8,128)(2,1)S(1)}, u32[]{:S(2)}, u32[]{:S(2)}) collective-permute-start(bf16[512,128]{1,0:T(8,128)(2,1)S(1)} %collective-permute-done.2.refs_3_), channel_id=1, source_target_pairs={{0,112},{16,0},{32,16},{48,32},{64,48},{80,64},{96,80},{112,96},{1... | collective-permute-start | bytes 393224 | tf_op jit(solution)/shard_map/ppermute | solution.py:272
  41.3 6.2 %collective-permute-start.8 = (bf16[512,128]{1,0:T(8,128)(2,1)S(1)}, bf16[512,128]{1,0:T(8,128)(2,1)S(1)}, u32[]{:S(2)}, u32[]{:S(2)}) collective-permute-start(bf16[512,128]{1,0:T(8,128)(2,1)S(1)} %collective-permute-done.1.refs_2_), channel_id=1, source_target_pairs={{0,8},{8,0},{1,9},{9,1},{2,10},{10,2},{3,11},{11,3},{4,12},{12,4},... | collective-permute-start | bytes 393224 | tf_op jit(solution)/shard_map/ppermute | solution.py:278
  44.8 2.8 %collective-permute-start.9 = (bf16[512,128]{1,0:T(8,128)(2,1)S(1)}, bf16[512,128]{1,0:T(8,128)(2,1)S(1)}, u32[]{:S(2)}, u32[]{:S(2)}) collective-permute-start(bf16[512,128]{1,0:T(8,128)(2,1)S(1)} %collective-permute-done.2.refs_3_), channel_id=1, source_target_pairs={{0,8},{8,0},{1,9},{9,1},{2,10},{10,2},{3,11},{11,3},{4,12},{12,4},... | collective-permute-start | bytes 393224 | tf_op jit(solution)/shard_map/ppermute | solution.py:278
  44.9 7.2 %collective-permute-start.6 = (bf16[512,128]{1,0:T(8,128)(2,1)S(1)}, bf16[512,128]{1,0:T(8,128)(2,1)S(1)}, u32[]{:S(2)}, u32[]{:S(2)}) collective-permute-start(bf16[512,128]{1,0:T(8,128)(2,1)S(1)} %collective-permute-done.3.refs_2_), channel_id=1, source_target_pairs={{0,16},{16,32},{32,48},{48,64},{64,80},{80,96},{96,112},{112,0},{1... | collective-permute-start | bytes 393224 | tf_op jit(solution)/shard_map/ppermute | solution.py:272
  44.9 7.2 %collective-permute-start.7 = (bf16[512,128]{1,0:T(8,128)(2,1)S(1)}, bf16[512,128]{1,0:T(8,128)(2,1)S(1)}, u32[]{:S(2)}, u32[]{:S(2)}) collective-permute-start(bf16[512,128]{1,0:T(8,128)(2,1)S(1)} %collective-permute-done.4.refs_3_), channel_id=1, source_target_pairs={{0,112},{16,0},{32,16},{48,32},{64,48},{80,64},{96,80},{112,96},{1... | collective-permute-start | bytes 393224 | tf_op jit(solution)/shard_map/ppermute | solution.py:272
  50.9 4.4 %collective-permute-start.14 = (bf16[512,128]{1,0:T(8,128)(2,1)S(1)}, bf16[512,128]{1,0:T(8,128)(2,1)S(1)}, u32[]{:S(2)}, u32[]{:S(2)}) collective-permute-start(bf16[512,128]{1,0:T(8,128)(2,1)S(1)} %collective-permute-done.3.refs_2_), channel_id=1, source_target_pairs={{0,8},{8,0},{1,9},{9,1},{2,10},{10,2},{3,11},{11,3},{4,12},{12,4},... | collective-permute-start | bytes 393224 | tf_op jit(solution)/shard_map/ppermute | solution.py:278
  52.0 3.9 %collective-permute-start.15 = (bf16[512,128]{1,0:T(8,128)(2,1)S(1)}, bf16[512,128]{1,0:T(8,128)(2,1)S(1)}, u32[]{:S(2)}, u32[]{:S(2)}) collective-permute-start(bf16[512,128]{1,0:T(8,128)(2,1)S(1)} %collective-permute-done.4.refs_3_), channel_id=1, source_target_pairs={{0,8},{8,0},{1,9},{9,1},{2,10},{10,2},{3,11},{11,3},{4,12},{12,4},... | collective-permute-start | bytes 393224 | tf_op jit(solution)/shard_map/ppermute | solution.py:278
  52.1 7.2 %collective-permute-start.12 = (bf16[512,128]{1,0:T(8,128)(2,1)S(1)}, bf16[512,128]{1,0:T(8,128)(2,1)S(1)}, u32[]{:S(2)}, u32[]{:S(2)}) collective-permute-start(bf16[512,128]{1,0:T(8,128)(2,1)S(1)} %collective-permute-done.6.refs_2_), channel_id=1, source_target_pairs={{0,16},{16,32},{32,48},{48,64},{64,80},{80,96},{96,112},{112,0},{1... | collective-permute-start | bytes 393224 | tf_op jit(solution)/shard_map/ppermute | solution.py:285
  52.6 6.6 %collective-permute-start.13 = (bf16[512,128]{1,0:T(8,128)(2,1)S(1)}, bf16[512,128]{1,0:T(8,128)(2,1)S(1)}, u32[]{:S(2)}, u32[]{:S(2)}) collective-permute-start(bf16[512,128]{1,0:T(8,128)(2,1)S(1)} %collective-permute-done.7.refs_3_), channel_id=1, source_target_pairs={{0,120},{8,112},{16,8},{24,0},{32,24},{40,16},{48,40},{56,32},{64,... | collective-permute-start | bytes 393224 | tf_op jit(solution)/shard_map/ppermute | solution.py:289
  55.4 3.9 %collective-permute-start.10 = (bf16[512,128]{1,0:T(8,128)(2,1)S(1)}, bf16[512,128]{1,0:T(8,128)(2,1)S(1)}, u32[]{:S(2)}, u32[]{:S(2)}) collective-permute-start(bf16[512,128]{1,0:T(8,128)(2,1)S(1)} %collective-permute-done.6.refs_2_), channel_id=1, source_target_pairs={{0,8},{8,0},{1,9},{9,1},{2,10},{10,2},{3,11},{11,3},{4,12},{12,4},... | collective-permute-start | bytes 393224 | tf_op jit(solution)/shard_map/ppermute | solution.py:290
  55.4 3.9 %collective-permute-start.11 = (bf16[512,128]{1,0:T(8,128)(2,1)S(1)}, bf16[512,128]{1,0:T(8,128)(2,1)S(1)}, u32[]{:S(2)}, u32[]{:S(2)}) collective-permute-start(bf16[512,128]{1,0:T(8,128)(2,1)S(1)} %collective-permute-done.7.refs_3_), channel_id=1, source_target_pairs={{0,8},{8,0},{1,9},{9,1},{2,10},{10,2},{3,11},{11,3},{4,12},{12,4},... | collective-permute-start | bytes 393224 | tf_op jit(solution)/shard_map/ppermute | solution.py:290
